TPU v7x, 32 devices: a whole 2x2x4 slice. The times are simulated.
32 devices in a mesh: fsdp: 4 (over y, x), seq: 4 (over z), tp: 2 (over core).
Axes of the slice: x: 2, y: 2, z: 4, core: 2. Of those that a mesh axis runs over, the one named last changes fastest.
Arguments:
- tokens: bfloat16 [1024, 8192], P('seq'), may hold values from -6 to 6
- norm_gain: float32 [8192], replicated, may hold values from 0.1 to 1.9
- in_weight: bfloat16 [3, 8192, 8192], P(None, 'seq', ('fsdp', 'tp')), may hold values from -0.0625 to 0.0625
- short_filter: float32 [7, 3, 8192], P(None, None, ('fsdp', 'tp')), may hold values from -2.4 to 2.4
- long_filter: float32 [128, 512], P(None, ('fsdp', 'tp')), may hold values from -0.5 to 0.5
- out_weight: bfloat16 [8192, 8192], P(('fsdp', 'tp'), 'seq'), may hold values from -0.0625 to 0.0625
- segment_ids: int32 [1024], replicated, may hold values from 0 to 7, never falling along the last dimension, each value on 1 to 256 neighbouring positions
Outputs:
- block_out: bfloat16 [1024, 8192], P('seq', ('fsdp', 'tp'))
Inputs may be any that keep to these rules, and one draw needn't show every extreme that they name: `segment_ids`: segment numbers never fall along the sequence and each is used; a segment covers at most 256 positions and one covers exactly 256.
All inputs are finite; a program needn't handle non-finite values.
Results may differ from a plain program's by a relative error of at most 0.0087.
Values may be sent and summed in bfloat16 or wider, within the bound.
No kernel may reach another device: no remote copies, remote signals or barrier semaphores. Data moves between devices by JAX's collectives and lax.ppermute only.
A program may use at most 192 MiB of HBM per device.

v0:
```python
import jax
import jax.numpy as jnp
from jax import lax
from jax.sharding import PartitionSpec as P

GROUP = 16
KS = 7
KL = 128


def from_behind(value, axis, by):
    peers = lax.axis_size(axis)
    pairs = [(i, i + by) for i in range(peers) if 0 <= i + by < peers]
    return lax.ppermute(value, axis, pairs)


def short_conv(extended, ext_ids, short_filter, skip):
    out_rows = extended.shape[0] - skip
    summed_taps = jnp.zeros((out_rows,) + extended.shape[1:], jnp.float32)
    for offset in range(KS):
        source = extended[skip - offset : skip - offset + out_rows].astype(jnp.float32)
        same_seg = (
            ext_ids[skip - offset : skip - offset + out_rows] == ext_ids[skip : skip + out_rows]
        ).astype(jnp.float32)
        summed_taps = summed_taps + short_filter[offset][None] * source * same_seg[:, None, None]
    return summed_taps


def shards(tokens, norm_gain, in_weight, short_filter, long_filter, out_weight, segment_ids):
    rows_dev = tokens.shape[0]
    chan_dev = in_weight.shape[2]
    seq_index = lax.axis_index("seq")
    widened = tokens.astype(jnp.float32)
    squares = jnp.mean(widened * widened, axis=1, keepdims=True)
    normed = (widened * lax.rsqrt(squares + 1e-06) * norm_gain).astype(jnp.bfloat16)
    projected = jnp.einsum(
        "td,kdc->tkc",
        normed,
        lax.all_gather(in_weight, "seq", axis=1, tiled=True),
        preferred_element_type=jnp.float32,
    )
    projected = projected.astype(jnp.bfloat16)
    front = KL + KS - 2
    ids_padded = jnp.concatenate([jnp.full((front,), -1, jnp.int32), segment_ids])
    window = lax.dynamic_slice_in_dim(ids_padded, seq_index * rows_dev, rows_dev + front, 0)
    halo_rows = from_behind(projected[rows_dev - (KS - 1) :], "seq", 1)
    extended = jnp.concatenate([halo_rows, projected], axis=0)
    conv_short = short_conv(extended, window[KL - 1 :], short_filter, KS - 1)
    product = (conv_short[:, 1, :] * conv_short[:, 2, :]).astype(jnp.bfloat16)
    prod_rim = from_behind(product[rows_dev - (KL - 1) :], "seq", 1)
    padded = jnp.concatenate([prod_rim, product], axis=0)
    outer_gate = conv_short[:, 0, :]
    pad_ids = window[KS - 1 :]
    blocks = rows_dev // KL
    groups_dev = long_filter.shape[1]
    front_part = padded[:rows_dev].reshape(blocks, KL, chan_dev)
    back_part = jnp.concatenate(
        [padded[KL:], jnp.zeros((1, chan_dev), jnp.bfloat16)], axis=0
    ).reshape(blocks, KL, chan_dev)[:, : KL - 1]
    prod_window = jnp.concatenate([front_part, back_part], axis=1).astype(jnp.float32)
    prod_window = prod_window.reshape(blocks, 2 * KL - 1, groups_dev, GROUP)
    id_front = pad_ids[:rows_dev].reshape(blocks, KL)
    id_back = jnp.concatenate([pad_ids[KL:], jnp.full((1,), -1, jnp.int32)]).reshape(blocks, KL)[
        :, : KL - 1
    ]
    id_window = jnp.concatenate([id_front, id_back], axis=1)
    same_seg = (id_window[:, None, :] == id_window[:, KL - 1 :, None]).astype(jnp.float32)
    reversed_taps = jnp.concatenate(
        [long_filter[::-1], jnp.zeros((KL, groups_dev), jnp.float32)], axis=0
    )
    toeplitz = jnp.tile(reversed_taps, (KL, 1))[: KL * (2 * KL - 1)].reshape(
        KL, 2 * KL - 1, groups_dev
    )
    masked = toeplitz[None] * same_seg[..., None]
    conv_long = jnp.einsum(
        "btsg,bsgc->btgc", masked, prod_window, precision=lax.Precision.HIGHEST
    ).reshape(rows_dev, chan_dev)
    gated = (outer_gate * conv_long).astype(jnp.bfloat16)
    partial_value = jnp.dot(
        gated,
        lax.all_gather(out_weight, "seq", axis=1, tiled=True),
        preferred_element_type=jnp.float32,
    )
    summed = lax.psum_scatter(partial_value, ("fsdp", "tp"), scatter_dimension=1, tiled=True)
    slice_cols = summed.shape[1]
    residual = lax.dynamic_slice_in_dim(
        widened, lax.axis_index(("fsdp", "tp")) * slice_cols, slice_cols, 1
    )
    return (residual + summed).astype(jnp.bfloat16)


def solution(mesh):
    return jax.shard_map(
        shards,
        mesh=mesh,
        in_specs=(
            P("seq", None),
            P(),
            P(None, "seq", ("fsdp", "tp")),
            P(None, None, ("fsdp", "tp")),
            P(None, ("fsdp", "tp")),
            P(("fsdp", "tp"), "seq"),
            P(),
        ),
        out_specs=P("seq", ("fsdp", "tp")),
        check_vma=False,
    )
```

profile of v0, /device:TPU:18, one launch (start us, length us, event | category | flops | bytes accessed | tf_op | source)
XLA Modules:
  0.0 1231.8 jit_solution(8507929362208929343)
XLA Ops:
  6.5 0.7 all-gather.3.cloned.1.call-update
  7.3 0.0 all-gather.5.cloned.1.call-start
  7.3 0.7 all-gather.5.cloned.1.call-update
  8.0 0.0 reduce-scatter.2.cloned.1.call-start
  8.1 0.1 pad_dynamic-slice_fusion
  8.2 0.1 slice.155
  8.3 0.1 add_bitcast_fusion
  8.3 0.1 slice_bitcast_fusion.3
  8.4 0.1 fusion.29
  8.5 3.1 multiply_reduce_fusion
  11.6 0.1 fusion.31
  11.7 0.1 compare_convert_fusion
  11.8 0.0 copy-start.3
  11.9 832.4 %all-gather.3.cloned.1.call-done = bf16[3,8192,1024]{2,1,0:T(8,128)(2,1)} async-done(((bf16[3,2048,1024]{2,1,0:T(8,128)(2,1)}), bf16[3,8192,1024]{2,1,0:T(8,128)(2,1)}) %all-gather.3.cloned.1.call-update) | async-done | bytes 50331664 | tf_op jit(solution)/shard_map/all_gather | solution.py:39
  844.2 25.0 %fusion.10 = bf16[256,3,1024]{2,0,1:T(8,128)(2,1)S(1)} fusion(bf16[3,8192,1024]{2,1,0:T(8,128)(2,1)} %all-gather.3.cloned.1.call-done, f32[8192]{0:T(1024)S(1)} %copy-done.5, f32[256]{0:T(256)S(1)} %add_rsqrt_fusion, bf16[256,8192]{1,0:T(8,128)(2,1)} %param.7), kind=kOutput, calls=%fused_computation.17 | convolution fusion | flops 12894076928 | bytes 56132608 | tf_op jit(solution)/shard_map/td,kdc->tkc/dot_general | solution.py:36
  869.2 1.2 copy-done
  870.4 2.2 collective-permute-start
  872.6 0.1 compare_convert_fusion.6
  872.7 0.1 rev.3
  872.8 0.7 tile.4
  873.5 4.7 copy.23
  878.2 3.8 slice.175
  882.0 15.9 %mul.214 = f32[128,255,64]{1,0,2:T(8,128)} reshape(f32[32640,64]{0,1:T(8,128)} %slice.175) | data formatting | bytes 16711680 | tf_op jit(solution)/shard_map/mul | solution.py:74
  897.9 0.0 collective-permute-done
  897.9 0.6 copy-done.2
  898.5 10.2 multiply_add_fusion
  908.8 0.1 fusion.21
  908.9 0.8 slice_bitcast_fusion.2
  909.7 2.1 collective-permute-start.1
  911.9 0.1 slice_bitcast_fusion.1
  912.0 0.8 concatenate.33
  912.8 2.1 copy.12
  914.9 0.1 fusion.34
  915.1 20.1 %collective-permute-done.1 = bf16[127,1024]{1,0:T(8,128)(2,1)} collective-permute-done((bf16[127,1024]{1,0:T(8,128)(2,1)}, bf16[127,1024]{1,0:T(8,128)(2,1)}, u32[]{:S(2)}, u32[]{:S(2)}) %collective-permute-start.1) | collective-permute-done | bytes 260128 | tf_op jit(solution)/shard_map/ppermute | solution.py:14
  935.2 1.8 pad_maximum_fusion.1
  937.0 2.1 copy.11
  939.1 2.0 concatenate.32
  941.0 1.1 copy.13
  942.1 12.1 fusion.18
  954.2 0.8 copy.14
  955.0 1.0 copy.33
  956.1 2.6 copy.15
  958.7 172.1 %all-gather.5.cloned.1.call-done = bf16[1024,8192]{1,0:T(8,128)(2,1)} async-done(((bf16[1024,2048]{1,0:T(8,128)(2,1)}), bf16[1024,8192]{1,0:T(8,128)(2,1)}) %all-gather.5.cloned.1.call-update) | async-done | bytes 16777232 | tf_op jit(solution)/shard_map/all_gather | solution.py:81
  1130.8 14.1 %fusion.27 = f32[256,8192]{1,0:T(8,128)} fusion(bf16[1024,8192]{1,0:T(8,128)(2,1)} %all-gather.5.cloned.1.call-done, f32[256,1024]{1,0:T(8,128)} %copy.15, f32[256,3,1024]{2,0,1:T(8,128)S(1)} %multiply_add_fusion), kind=kOutput, calls=%fused_computation.38 | convolution fusion | flops 4295491584 | bytes 27262976 | tf_op jit(solution)/shard_map/dot_general | solution.py:79
  1144.9 0.0 reduce-scatter.2.cloned.1.call-update
  1144.9 6.4 convert_element_type.71
  1151.4 71.4 %reduce-scatter.2.cloned.1.call-done = f32[256,1024]{1,0:T(8,128)} async-done(((f32[256,8192]{1,0:T(8,128)}), f32[256,1024]{1,0:T(8,128)}) %reduce-scatter.2.cloned.1.call-update) | async-done | bytes 1048592 | tf_op jit(solution)/shard_map/reduce_scatter | solution.py:84
  1222.8 2.5 add_convert_fusion
  (18 shorter events, 0.1 us)
Async XLA Ops:
  6.5 837.7 %all-gather.3.cloned.1.call-start = ((), (), s32[]{:S(2)}) async-start(), calls=%async_computation.1 | async-start | bytes 62914560 | tf_op jit(solution)/shard_map/all_gather | solution.py:39
  7.3 0.8 copy-start.4
  7.3 1123.5 %all-gather.5.cloned.1.call-start = ((), (), s32[]{:S(2)}) async-start(), calls=%async_computation.2 | async-start | bytes 20971520 | tf_op jit(solution)/shard_map/all_gather | solution.py:81
  8.0 3.6 copy-start.1
  8.0 836.2 %copy-start.5 = (f32[8192]{0:T(1024)S(1)}, f32[8192]{0:T(1024)}, u32[]{:S(2)}) copy-start(f32[8192]{0:T(1024)} %param.8) | copy-start | bytes 98308
  8.0 1214.7 %reduce-scatter.2.cloned.1.call-start = ((), (), s32[]{:S(2)}) async-start(), calls=%async_computation.3 | async-start | bytes 9437184 | tf_op jit(solution)/shard_map/reduce_scatter | solution.py:84
  11.8 860.9 %copy-start.3 = (f32[128,64]{0,1:T(8,128)S(1)}, f32[128,64]{0,1:T(8,128)}, u32[]{:S(2)}) copy-start(f32[128,64]{0,1:T(8,128)} %param.11) | copy-start | bytes 98308
  869.2 1.2 copy-start
  870.4 27.5 %collective-permute-start = (bf16[6,3,1024]{2,0,1:T(8,128)(2,1)S(1)}, bf16[6,3,1024]{2,0,1:T(8,128)(2,1)S(1)}, u32[]{:S(2)}, u32[]{:S(2)}) collective-permute-start(bf16[6,3,1024]{2,0,1:T(8,128)(2,1)S(1)} %slice.158), channel_id=1, source_target_pairs={{0,2},{2,4},{4,6},{1,3},{3,5},{5,7},{8,10},{10,12},{12,14},{9,11},... | collective-permute-start | bytes 110600 | tf_op jit(solution)/shard_map/ppermute | solution.py:14
  897.9 0.6 copy-start.2
  909.7 25.4 %collective-permute-start.1 = (bf16[127,1024]{1,0:T(8,128)(2,1)}, bf16[127,1024]{1,0:T(8,128)(2,1)}, u32[]{:S(2)}, u32[]{:S(2)}) collective-permute-start(bf16[127,1024]{1,0:T(8,128)(2,1)} %slice_bitcast_fusion.2), channel_id=1, source_target_pairs={{0,2},{2,4},{4,6},{1,3},{3,5},{5,7},{8,10},{10,12},{12,14},{9,11},... | collective-permute-start | bytes 780296 | tf_op jit(solution)/shard_map/ppermute | solution.py:14
Sparse Core Ops, SparseCore 0:
  8.9 835.2 all-gather.2
  845.8 284.9 all-gather.4
  1145.1 77.6 reduce-scatter.1
where the time goes:
time: 1230 us
  waiting for transfers between devices  1100 us (89%)
  matrix products  51.2 us (4%)
  local copies, waits for them, and re-layouts  40.8 us (3%)
  other arithmetic  24.7 us (2%)
  between operations  13.3 us (1%)
    all_gather x1, waiting for transfers between devices, shards(): lax.all_gather(in_weight, 'seq', axis=1, tiled=True)  832 us
    all_gather x1, waiting for transfers between devices, shards(): lax.all_gather(out_weight, 'seq', axis=1, tiled=True)  172 us
    reduce_scatter x1, waiting for transfers between devices, shards(): lax.psum_scatter(partial_value, ('fsdp', 'tp'), scatter_dimension=1, tile...  71.4 us
    dot_general x1, matrix products, shards(): jnp.einsum('td,kdc->tkc', normed, lax.all_gather(in_weight, 'seq', axis=1...  25 us
  transfers between devices with their start and end apart: 5, of which 4 were waited for; matrix products, arithmetic and copies ran while one was open for 8% of the time, Pallas kernels for 0%

commit v1 on v0

v1 whole, which is shorter than its diff:
```python
import functools
import jax
import jax.numpy as jnp
from jax import lax
from jax.experimental import pallas as pl
from jax.experimental.pallas import tpu as pltpu
from jax.sharding import PartitionSpec as P

GROUP = 16
KS = 7
KL = 128
BF = jnp.bfloat16
F32 = jnp.float32
VMEM_MAX = 48 * 1024 * 1024


def in_proj_body(x_ref, w_ref, o_ref):
    pieces, rows = o_ref.shape[1], o_ref.shape[3]
    for i in range(pieces):
        acc = jnp.dot(x_ref[pl.ds(i * rows, rows), :], w_ref[0], preferred_element_type=F32)
        o_ref[0, i, 0] = acc.astype(BF)


def in_proj(x, w, parts):
    pieces, rows, depth = x.shape
    chan = w.shape[2]
    width = chan // parts
    if width % 128:
        y = jnp.einsum("ird,kdpc->pikrc", x, w.reshape(3, depth, parts, width), preferred_element_type=F32)
        return y.astype(BF)
    return pl.pallas_call(
        in_proj_body,
        grid=(parts, 3),
        in_specs=[
            pl.BlockSpec((pieces * rows, depth), lambda p, k: (0, 0)),
            pl.BlockSpec((1, depth, width), lambda p, k: (k, 0, p)),
        ],
        out_specs=pl.BlockSpec((1, pieces, 1, rows, width), lambda p, k: (p, 0, k, 0, 0)),
        out_shape=jax.ShapeDtypeStruct((parts, pieces, 3, rows, width), BF),
        compiler_params=pltpu.CompilerParams(vmem_limit_bytes=VMEM_MAX),
        cost_estimate=pl.CostEstimate(
            flops=2 * pieces * rows * depth * 3 * chan,
            bytes_accessed=2 * (3 * depth * chan + pieces * rows * (depth + 3 * chan)),
            transcendentals=0,
        ),
    )(x.reshape(pieces * rows, depth), w)


def conv_body(groups, shards, index_ref, y_ref, pos_ref, short_ref, taps_ref, o_ref, proj, prod, toep):
    pieces, rows = y_ref.shape[0], y_ref.shape[2]
    lanes = y_ref.shape[3]
    part = rows // shards
    seq_len = o_ref.shape[0]
    shard_len = seq_len // shards
    base = index_ref[0]
    for k in range(3):
        proj[k, pl.ds(0, 8), :] = jnp.zeros((8, lanes), F32)
        for q in range(pieces):
            piece = lax.bitwise_xor(jnp.int32(q), base)
            for t in range(shards):
                proj[k, pl.ds(8 + t * shard_len + q * part, part), :] = y_ref[
                    piece, k, pl.ds(t * part, part), :
                ].astype(F32)
    prod[pl.ds(0, KL), :] = jnp.zeros((KL, lanes), BF)
    for g in range(groups):
        row = jnp.broadcast_to(taps_ref[0, pl.ds(g, 1), :], (KL, 2 * KL))
        toep[pl.ds(g * KL, KL), :] = pltpu.roll(row, 0, 1, stride=1, stride_axis=0)
    lag = (
        KL
        + lax.broadcasted_iota(jnp.int32, (KL, 2 * KL), 0)
        - lax.broadcasted_iota(jnp.int32, (KL, 2 * KL), 1)
    )
    group_of = lax.broadcasted_iota(jnp.int32, (KL, lanes), 1) // GROUP

    def block(b, carry):
        start = pl.multiple_of(b * KL, KL)
        pos = pos_ref[pl.ds(start, KL), :]
        pos_lanes = jnp.broadcast_to(pos, (KL, lanes))
        sums = [None, None, None]
        window = [proj[k, pl.ds(start, KL + 8), :] for k in range(3)]
        for j in range(KS):
            keep = pos_lanes >= j
            for k in range(3):
                source = window[k][8 - j : 8 - j + KL]
                term = short_ref[j, k : k + 1, :] * source
                if j == 0:
                    sums[k] = term
                else:
                    sums[k] = sums[k] + jnp.where(keep, term, 0.0)
        prod[pl.ds(start + KL, KL), :] = (sums[1] * sums[2]).astype(BF)
        source = prod[pl.ds(start, 2 * KL), :]
        linked = (lag <= jnp.broadcast_to(pos, (KL, 2 * KL))) & (lag >= 0)
        total = jnp.zeros((KL, lanes), F32)
        for g in range(groups):
            masked = jnp.where(linked, toep[pl.ds(g * KL, KL), :], 0.0).astype(BF)
            made = jnp.dot(masked, source, preferred_element_type=F32)
            total = jnp.where(group_of == g, made, total)
        o_ref[pl.ds(start, KL), :] = (sums[0] * total).astype(BF)
        return carry

    lax.fori_loop(0, seq_len // KL, block, 0)


def convolve(y, position, short, taps, shards, base):
    pieces, _, rows, chan = y.shape
    seq_len = pieces * rows
    tile = 128 if chan % 128 == 0 else chan
    groups = tile // GROUP
    return pl.pallas_call(
        functools.partial(conv_body, groups, shards),
        grid_spec=pltpu.PrefetchScalarGridSpec(
            num_scalar_prefetch=1,
            grid=(chan // tile,),
            in_specs=[
                pl.BlockSpec((pieces, 3, rows, tile), lambda c, s: (0, 0, 0, c)),
                pl.BlockSpec((seq_len, 1), lambda c, s: (0, 0)),
                pl.BlockSpec((KS, 3, tile), lambda c, s: (0, 0, c)),
                pl.BlockSpec((1, groups, 2 * KL), lambda c, s: (c, 0, 0)),
            ],
            out_specs=pl.BlockSpec((seq_len, tile), lambda c, s: (0, c)),
            scratch_shapes=[
                pltpu.VMEM((3, seq_len + 8, tile), F32),
                pltpu.VMEM((seq_len + KL, tile), BF),
                pltpu.VMEM((groups * KL, 2 * KL), F32),
            ],
        ),
        out_shape=jax.ShapeDtypeStruct((seq_len, chan), BF),
        compiler_params=pltpu.CompilerParams(vmem_limit_bytes=VMEM_MAX),
        cost_estimate=pl.CostEstimate(
            flops=2 * seq_len * chan * 2 * KL * groups,
            bytes_accessed=seq_len * chan * 8,
            transcendentals=0,
        ),
    )(base, y, position, short, taps.reshape(chan // tile, groups, 2 * KL))


def out_proj_body(g_ref, w_ref, o_ref):
    parts, width = g_ref.shape[0], g_ref.shape[2]
    blocks, rows = o_ref.shape[0], o_ref.shape[2]
    for t in range(blocks):
        acc = None
        for p in range(parts):
            made = jnp.dot(
                g_ref[p, pl.ds(t * rows, rows), :],
                w_ref[pl.ds(p * width, width), :],
                preferred_element_type=F32,
            )
            acc = made if acc is None else acc + made
        o_ref[t, 0] = acc.astype(BF)


def out_proj(g, w, blocks, halves):
    parts, seq_len, width = g.shape
    depth = w.shape[1]
    cols = depth // halves
    tile = min(256, cols)
    per = cols // tile
    rows = seq_len // blocks
    return pl.pallas_call(
        out_proj_body,
        grid=(depth // tile,),
        in_specs=[
            pl.BlockSpec((parts, seq_len, width), lambda n: (0, 0, 0)),
            pl.BlockSpec((parts * width, tile), lambda n: (0, n)),
        ],
        out_specs=pl.BlockSpec((blocks, 1, rows, tile), lambda n: (0, n // per, 0, n % per)),
        out_shape=jax.ShapeDtypeStruct((blocks, halves, rows, cols), BF),
        compiler_params=pltpu.CompilerParams(vmem_limit_bytes=VMEM_MAX),
        cost_estimate=pl.CostEstimate(
            flops=2 * seq_len * parts * width * depth,
            bytes_accessed=2 * (parts * width * (seq_len + depth) + seq_len * depth),
            transcendentals=0,
        ),
    )(g, w)


def shards(tokens, norm_gain, in_weight, short_filter, long_filter, out_weight, segment_ids):
    n_seq, n_fsdp, n_tp = (lax.axis_size(a) for a in ("seq", "fsdp", "tp"))
    plane = n_fsdp * n_tp
    rows_dev, width_all = tokens.shape
    depth = in_weight.shape[1]
    chan_dev = in_weight.shape[2]
    z, f, c = (lax.axis_index(a) for a in ("seq", "fsdp", "tp"))
    q = f * n_tp + c
    rows = rows_dev // plane
    seq_len = segment_ids.shape[0]

    def swap_core(v):
        return lax.ppermute(v, "tp", [(i, i ^ 1) for i in range(n_tp)])

    def swap_chip(v, e):
        return lax.ppermute(v, "fsdp", [(i, i ^ e) for i in range(n_fsdp)])

    mine = lax.dynamic_slice_in_dim(tokens, q * rows, rows, 0).astype(F32)
    squares = jnp.mean(mine * mine, axis=1, keepdims=True)
    normed = (mine * lax.rsqrt(squares + 1e-06) * norm_gain).astype(BF)
    split = normed.reshape(rows, n_seq, depth).transpose(1, 0, 2)
    own = lax.all_to_all(split, "seq", 0, 0).reshape(n_seq * rows, depth)
    near = swap_core(own)
    far = [swap_chip(own, e) for e in range(1, n_fsdp)]
    first = in_proj(jnp.stack([own, near]), in_weight, n_seq)
    got_first = lax.psum_scatter(first, "seq", scatter_dimension=0)
    far_pairs = []
    for e in range(n_fsdp - 1):
        far_pairs += [far[e], swap_core(far[e])]
    second = in_proj(jnp.stack(far_pairs), in_weight, n_seq)
    got_second = lax.psum_scatter(second, "seq", scatter_dimension=0)
    projected = jnp.concatenate([got_first, got_second], axis=0)

    chan = chan_dev // n_seq
    groups = chan // GROUP
    at = jnp.arange(seq_len, dtype=jnp.int32)
    earlier = (segment_ids[None, :] == segment_ids[:, None]) & (at[None, :] < at[:, None])
    position = jnp.sum(earlier.astype(jnp.int32), axis=1, keepdims=True)
    short = lax.dynamic_slice_in_dim(short_filter, z * chan, chan, 2)
    taps = lax.dynamic_slice_in_dim(long_filter, z * groups, groups, 1)
    taps = jnp.concatenate(
        [jnp.zeros((1, groups), F32), taps[::-1], jnp.zeros((KL - 1, groups), F32)], axis=0
    ).T
    gated = convolve(projected, position, short, taps, n_seq, q.astype(jnp.int32).reshape(1))

    gathered = lax.all_gather(gated, "seq", axis=0)
    halves = plane // n_seq
    partial = out_proj(gathered, out_weight, n_seq, halves)
    cols = partial.shape[3]
    partial = partial.reshape(n_fsdp, n_tp, rows_dev, cols)
    away = lax.dynamic_index_in_dim(partial, 1 - c, 1, keepdims=False)
    keep = lax.dynamic_index_in_dim(partial, c, 1, keepdims=False)
    both = (keep.astype(F32) + swap_core(away).astype(F32)).astype(BF)
    total = lax.dynamic_index_in_dim(both, f, 0, keepdims=False).astype(F32)
    for e in range(1, n_fsdp):
        sent = lax.dynamic_index_in_dim(both, f ^ e, 0, keepdims=False)
        total = total + swap_chip(sent, e).astype(F32)
    total = total.astype(BF)

    def flat(s, p):
        return (p // n_tp * n_seq + s) * n_tp + p % n_tp

    pairs = [
        (flat(s, p), flat(p // halves, s * halves + p % halves))
        for s in range(n_seq)
        for p in range(plane)
    ]
    placed = lax.ppermute(total, ("fsdp", "seq", "tp"), pairs)
    residual = lax.dynamic_slice_in_dim(tokens, q * cols, cols, 1)
    return (residual.astype(F32) + placed.astype(F32)).astype(BF)


def solution(mesh):
    return jax.shard_map(
        shards,
        mesh=mesh,
        in_specs=(
            P("seq", None),
            P(),
            P(None, "seq", ("fsdp", "tp")),
            P(None, None, ("fsdp", "tp")),
            P(None, ("fsdp", "tp")),
            P(("fsdp", "tp"), "seq"),
            P(),
        ),
        out_specs=P("seq", ("fsdp", "tp")),
        check_vma=False,
    )
```

time: 1230 us -> 333 us (0.27)
  the two profiles are of different devices: /device:TPU:18 before, /device:TPU:2 now
where the time goes in v1:
time: 333 us; the launch traced here: 332 us
  waiting for transfers between devices  225 us (68%)
  Pallas kernels  47.3 us (14%)
  blocking collectives  19.2 us (6%)
  between operations  13.3 us (4%)
  other arithmetic  11.7 us (4%)
  starting transfers between devices  9.71 us (3%)
  local copies, waits for them, and re-layouts  6.32 us (2%)
    reduce_scatter x1, waiting for transfers between devices, shards(): got_second = lax.psum_scatter(second, 'seq', scatter_dimension=0)  86.6 us
    all_gather x1, waiting for transfers between devices, shards(): gathered = lax.all_gather(gated, 'seq', axis=0)  46.6 us
    ppermute x1, waiting for transfers between devices, shards(): placed = lax.ppermute(total, ('fsdp', 'seq', 'tp'), pairs)  37.1 us
    ppermute x6, waiting for transfers between devices, swap_chip(): return lax.ppermute(v, 'fsdp', [(i, i ^ e) for i in range(n_fsdp)])  34.3 us
    pallas_call x2, Pallas kernels, in_proj(): pl.pallas_call(in_proj_body, grid=(parts, 3), in_specs=[pl.BlockSpec((pie...  28.3 us
    all_to_all x1, blocking collectives, shards(): own = lax.all_to_all(split, 'seq', 0, 0).reshape(n_seq * rows, depth)  19.2 us
    reduce_scatter x1, waiting for transfers between devices, shards(): got_first = lax.psum_scatter(first, 'seq', scatter_dimension=0)  13.7 us
    pallas_call x1, Pallas kernels, convolve(): pl.pallas_call(functools.partial(conv_body, groups, shards), grid_spec=pl...  9.63 us
  transfers between devices with their start and end apart: 15, of which 10 were waited for; matrix products, arithmetic and copies ran while one was open for 1% of the time, Pallas kernels for 9%

profile of v1, /device:TPU:2, one launch (start us, length us, event | category | flops | bytes accessed | tf_op | source)
XLA Modules:
  0.0 332.1 jit_solution(12760334472341556675)
XLA Ops:
  6.5 1.3 fusion.2
  7.8 1.3 fusion.4
  9.1 0.4 reshape.34
  9.5 0.3 copy.20
  9.8 19.2 %all_to_all.5 = bf16[4,32,2048]{2,1,0:T(8,128)(2,1)S(1)} all-to-all(bf16[4,32,2048]{2,1,0:T(8,128)(2,1)S(1)} %copy.20), channel_id=1, replica_groups=mesh['fsdp'=4,'seq'=4,'tp'=2] {'seq'}, dimensions={0} | all-to-all | bytes 1048576 | tf_op jit(solution)/shard_map/all_to_all | solution.py:198
  28.9 0.5 collective-permute-start.1
  29.5 1.5 collective-permute-start.3
  31.0 1.4 collective-permute-start.5
  32.4 11.4 %collective-permute-done.1 = bf16[128,2048]{1,0:T(8,128)(2,1)S(1)} collective-permute-done((bf16[128,2048]{1,0:T(8,128)(2,1)S(1)}, bf16[128,2048]{1,0:T(8,128)(2,1)S(1)}, u32[]{:S(2)}, u32[]{:S(2)}) %collective-permute-start.1) | collective-permute-done | bytes 524320 | tf_op jit(solution)/shard_map/ppermute | solution.py:192
  43.8 0.1 pad_maximum_fusion.1
  43.9 12.0 %shard_map.73 = bf16[4,2,3,128,256]{4,3,2,1,0:T(8,128)(2,1)} custom-call(bf16[256,2048]{1,0:T(8,128)(2,1)S(1)} %bitcast.42, bf16[3,2048,1024]{2,1,0:T(8,128)(2,1)} %w_ref.4), custom_call_target="tpu_custom_call" | custom-call | flops 3221225472 | bytes 15204352 | tf_op jit(solution)/shard_map/pallas_call | solution.py:31
  55.9 0.0 reduce-scatter.3.cloned.1.call-update
  56.0 0.0 reduce-scatter.5.cloned.1.call-start
  56.0 0.6 collective-permute-start.4
  56.6 0.1 collective-permute-start.6
  56.8 1.3 collective-permute-done.4
  58.2 0.7 collective-permute-done.6
  58.9 16.2 %shard_map.74 = bf16[4,6,3,128,256]{4,3,2,1,0:T(8,128)(2,1)} custom-call(bf16[768,2048]{1,0:T(8,128)(2,1)S(1)} %bitcast.43, bf16[3,2048,1024]{2,1,0:T(8,128)(2,1)} %w_ref.4), custom_call_target="tpu_custom_call" | custom-call | flops 9663676416 | bytes 20447232 | tf_op jit(solution)/shard_map/pallas_call | solution.py:31
  75.2 0.0 reduce-scatter.5.cloned.1.call-update
  75.2 0.0 all-gather.3.cloned.1.call-start
  75.3 0.7 constant_dynamic-slice_fusion
  76.0 0.1 rev.3
  76.1 0.1 pad.2.clone
  76.2 0.5 convert_reduce_fusion
  76.7 0.2 copy.22.pos_ref
  76.9 0.1 maximum_bitcast_fusion.taps_ref
  77.0 13.7 %reduce-scatter.3.cloned.1.call-done = bf16[1,2,3,128,256]{4,3,2,1,0:T(8,128)(2,1)} async-done(((bf16[4,2,3,128,256]{4,3,2,1,0:T(8,128)(2,1)}), bf16[1,2,3,128,256]{4,3,2,1,0:T(8,128)(2,1)}) %reduce-scatter.3.cloned.1.call-update) | async-done | bytes 393232 | tf_op jit(solution)/shard_map/reduce_scatter | solution.py:202
  90.7 86.6 %reduce-scatter.5.cloned.1.call-done = bf16[1,6,3,128,256]{4,3,2,1,0:T(8,128)(2,1)} async-done(((bf16[4,6,3,128,256]{4,3,2,1,0:T(8,128)(2,1)}), bf16[1,6,3,128,256]{4,3,2,1,0:T(8,128)(2,1)}) %reduce-scatter.5.cloned.1.call-update) | async-done | bytes 1179664 | tf_op jit(solution)/shard_map/reduce_scatter | solution.py:207
  177.2 1.5 pad_maximum_fusion.y_ref
  178.7 9.6 %shard_map.75 = bf16[1024,256]{1,0:T(8,128)(2,1)} custom-call(s32[1]{0:T(128)} %bitcast.index_ref, bf16[8,3,128,256]{3,2,1,0:T(8,128)(2,1)S(1)} %pad_maximum_fusion.y_ref, s32[1024,1]{1,0:T(8,128)S(1)} %copy.22.pos_ref, f32[7,3,256]{2,1,0:T(4,128)S(1)} %copy.23.short_ref, f32[2,8,256]{2,1,0:T(8,128)S(1)} %maximum_bitcast_fusion.taps_ref), custom_call_target="tpu_custom_call" | custom-call | flops 1073741824 | bytes 2097152 | tf_op jit(solution)/shard_map/pallas_call | solution.py:109
  188.4 0.0 all-gather.3.cloned.1.call-update
  188.4 46.6 %all-gather.3.cloned.1.call-done = bf16[4096,256]{1,0:T(8,128)(2,1)} async-done(((bf16[1024,256]{1,0:T(8,128)(2,1)}), bf16[4096,256]{1,0:T(8,128)(2,1)}) %all-gather.3.cloned.1.call-update) | async-done | bytes 2097168 | tf_op jit(solution)/shard_map/all_gather | solution.py:222
  235.0 1.6 copy-done.1
  236.6 9.3 %shard_map.76 = bf16[4,2,256,1024]{3,2,1,0:T(8,128)(2,1)} custom-call(bf16[4,1024,256]{2,1,0:T(8,128)(2,1)S(1)} %bitcast.44, bf16[1024,2048]{1,0:T(8,128)(2,1)} %w_ref.5), custom_call_target="tpu_custom_call" | custom-call | flops 4294967296 | bytes 10485760 | tf_op jit(solution)/shard_map/pallas_call | solution.py:159
  245.9 1.8 dynamic-slice_bitcast_fusion
  247.7 0.1 collective-permute-start.7
  247.8 4.3 %collective-permute-done.7 = bf16[4,256,1024]{2,1,0:T(8,128)(2,1)} collective-permute-done((bf16[4,256,1024]{2,1,0:T(8,128)(2,1)S(1)}, bf16[4,256,1024]{2,1,0:T(8,128)(2,1)}, u32[]{:S(2)}, u32[]{:S(2)}) %collective-permute-start.7) | collective-permute-done | bytes 2097184 | tf_op jit(solution)/shard_map/ppermute | solution.py:189
  252.1 3.2 fusion
  255.3 1.0 dynamic-slice_bitcast_fusion.3
  256.3 1.5 collective-permute-start.10
  257.7 1.4 collective-permute-start.8
  259.2 0.6 collective-permute-start.9
  259.8 12.5 %collective-permute-done.10 = bf16[256,1024]{1,0:T(8,128)(2,1)} collective-permute-done((bf16[256,1024]{1,0:T(8,128)(2,1)}, bf16[256,1024]{1,0:T(8,128)(2,1)}, u32[]{:S(2)}, u32[]{:S(2)}) %collective-permute-start.10) | collective-permute-done | bytes 524320 | tf_op jit(solution)/shard_map/ppermute | solution.py:192
  272.3 10.4 %collective-permute-done.8 = bf16[256,1024]{1,0:T(8,128)(2,1)} collective-permute-done((bf16[256,1024]{1,0:T(8,128)(2,1)S(1)}, bf16[256,1024]{1,0:T(8,128)(2,1)}, u32[]{:S(2)}, u32[]{:S(2)}) %collective-permute-start.8) | collective-permute-done | bytes 524320 | tf_op jit(solution)/shard_map/ppermute | solution.py:192
  282.7 1.7 fusion.7
  284.4 1.9 collective-permute-start.11
  286.4 37.1 %collective-permute-done.11 = bf16[256,1024]{1,0:T(8,128)(2,1)S(1)} collective-permute-done((bf16[256,1024]{1,0:T(8,128)(2,1)S(1)}, bf16[256,1024]{1,0:T(8,128)(2,1)S(1)}, u32[]{:S(2)}, u32[]{:S(2)}) %collective-permute-start.11) | collective-permute-done | bytes 524320 | tf_op jit(solution)/shard_map/ppermute | solution.py:244
  323.5 2.0 add_convert_fusion
  (24 shorter events, 0.3 us)
Async XLA Ops:
  6.5 68.7 %copy-start = (f32[7,3,1024]{2,0,1:T(8,128)S(1)}, f32[7,3,1024]{2,0,1:T(8,128)}, u32[]{:S(2)}) copy-start(f32[7,3,1024]{2,0,1:T(8,128)} %param.10) | copy-start | bytes 258052
  6.5 84.1 %reduce-scatter.3.cloned.1.call-start = ((), (), s32[]{:S(2)}) async-start(), calls=%async_computation.3 | async-start | bytes 1966080 | tf_op jit(solution)/shard_map/reduce_scatter | solution.py:202
  28.9 14.9 %collective-permute-start.1 = (bf16[128,2048]{1,0:T(8,128)(2,1)S(1)}, bf16[128,2048]{1,0:T(8,128)(2,1)S(1)}, u32[]{:S(2)}, u32[]{:S(2)}) collective-permute-start(bf16[128,2048]{1,0:T(8,128)(2,1)S(1)} %bitcast.46), channel_id=1, source_target_pairs={{0,8},{8,0},{16,24},{24,16},{1,9},{9,1},{17,25},{25,17},{2,10},{10... | collective-permute-start | bytes 1572872 | tf_op jit(solution)/shard_map/ppermute | solution.py:192
  29.5 14.3 %collective-permute-start = (bf16[128,2048]{1,0:T(8,128)(2,1)S(1)}, bf16[128,2048]{1,0:T(8,128)(2,1)S(1)}, u32[]{:S(2)}, u32[]{:S(2)}) collective-permute-start(bf16[128,2048]{1,0:T(8,128)(2,1)S(1)} %bitcast.47), channel_id=1, source_target_pairs={{0,1},{1,0},{2,3},{3,2},{4,5},{5,4},{6,7},{7,6},{8,9},{9,8},{10,11... | collective-permute-start | bytes 1572872 | tf_op jit(solution)/shard_map/ppermute | solution.py:189
  29.5 26.5 %collective-permute-start.3 = (bf16[128,2048]{1,0:T(8,128)(2,1)S(1)}, bf16[128,2048]{1,0:T(8,128)(2,1)S(1)}, u32[]{:S(2)}, u32[]{:S(2)}) collective-permute-start(bf16[128,2048]{1,0:T(8,128)(2,1)S(1)} %bitcast.48), channel_id=1, source_target_pairs={{0,16},{8,24},{16,0},{24,8},{1,17},{9,25},{17,1},{25,9},{2,18},{10... | collective-permute-start | bytes 1572872 | tf_op jit(solution)/shard_map/ppermute | solution.py:192
  31.0 25.6 %collective-permute-start.5 = (bf16[128,2048]{1,0:T(8,128)(2,1)S(1)}, bf16[128,2048]{1,0:T(8,128)(2,1)S(1)}, u32[]{:S(2)}, u32[]{:S(2)}) collective-permute-start(bf16[128,2048]{1,0:T(8,128)(2,1)S(1)} %bitcast.49), channel_id=1, source_target_pairs={{0,24},{8,16},{16,8},{24,0},{1,25},{9,17},{17,9},{25,1},{2,26},{10... | collective-permute-start | bytes 1572872 | tf_op jit(solution)/shard_map/ppermute | solution.py:192
  43.8 12.9 %collective-permute-start.2 = (bf16[128,2048]{1,0:T(8,128)(2,1)S(1)}, bf16[128,2048]{1,0:T(8,128)(2,1)S(1)}, u32[]{:S(2)}, u32[]{:S(2)}) collective-permute-start(bf16[128,2048]{1,0:T(8,128)(2,1)S(1)} %collective-permute-done.1), channel_id=1, source_target_pairs={{0,1},{1,0},{2,3},{3,2},{4,5},{5,4},{6,7},{7,6},{8,9},{9,8},{10,11... | collective-permute-start | bytes 1572872 | tf_op jit(solution)/shard_map/ppermute | solution.py:189
  56.0 121.3 %reduce-scatter.5.cloned.1.call-start = ((), (), s32[]{:S(2)}) async-start(), calls=%async_computation.4 | async-start | bytes 5898240 | tf_op jit(solution)/shard_map/reduce_scatter | solution.py:207
  56.0 2.1 collective-permute-start.4
  56.6 2.3 collective-permute-start.6
  75.2 1.0 copy-start.2
  75.2 159.8 %all-gather.3.cloned.1.call-start = ((), (), s32[]{:S(2)}) async-start(), calls=%async_computation.5 | async-start | bytes 2621440 | tf_op jit(solution)/shard_map/all_gather | solution.py:222
  235.0 1.6 copy-start.1
  247.7 4.4 %collective-permute-start.7 = (bf16[4,256,1024]{2,1,0:T(8,128)(2,1)S(1)}, bf16[4,256,1024]{2,1,0:T(8,128)(2,1)}, u32[]{:S(2)}, u32[]{:S(2)}) collective-permute-start(bf16[4,256,1024]{2,1,0:T(8,128)(2,1)S(1)} %dynamic-slice_bitcast_fusion), channel_id=1, source_target_pairs={{0,1},{1,0},{2,3},{3,2},{4,5},{5,4},{6,7},{7,6},{8,9},{9,8},{10,11... | collective-permute-start | bytes 6291464 | tf_op jit(solution)/shard_map/ppermute | solution.py:189
  256.3 16.0 %collective-permute-start.10 = (bf16[256,1024]{1,0:T(8,128)(2,1)}, bf16[256,1024]{1,0:T(8,128)(2,1)}, u32[]{:S(2)}, u32[]{:S(2)}) collective-permute-start(bf16[256,1024]{1,0:T(8,128)(2,1)} %get-tuple-element.6), channel_id=1, source_target_pairs={{0,24},{8,16},{16,8},{24,0},{1,25},{9,17},{17,9},{25,1},{2,26},{10... | collective-permute-start | bytes 1572872 | tf_op jit(solution)/shard_map/ppermute | solution.py:192
  257.7 25.0 %collective-permute-start.8 = (bf16[256,1024]{1,0:T(8,128)(2,1)S(1)}, bf16[256,1024]{1,0:T(8,128)(2,1)}, u32[]{:S(2)}, u32[]{:S(2)}) collective-permute-start(bf16[256,1024]{1,0:T(8,128)(2,1)S(1)} %get-tuple-element.5), channel_id=1, source_target_pairs={{0,8},{8,0},{16,24},{24,16},{1,9},{9,1},{17,25},{25,17},{2,10},{10... | collective-permute-start | bytes 1572872 | tf_op jit(solution)/shard_map/ppermute | solution.py:192
  259.2 23.5 %collective-permute-start.9 = (bf16[256,1024]{1,0:T(8,128)(2,1)S(1)}, bf16[256,1024]{1,0:T(8,128)(2,1)}, u32[]{:S(2)}, u32[]{:S(2)}) collective-permute-start(bf16[256,1024]{1,0:T(8,128)(2,1)S(1)} %get-tuple-element.7), channel_id=1, source_target_pairs={{0,16},{8,24},{16,0},{24,8},{1,17},{9,25},{17,1},{25,9},{2,18},{10... | collective-permute-start | bytes 1572872 | tf_op jit(solution)/shard_map/ppermute | solution.py:192
  284.4 39.1 %collective-permute-start.11 = (bf16[256,1024]{1,0:T(8,128)(2,1)S(1)}, bf16[256,1024]{1,0:T(8,128)(2,1)S(1)}, u32[]{:S(2)}, u32[]{:S(2)}) collective-permute-start(bf16[256,1024]{1,0:T(8,128)(2,1)S(1)} %fusion.7), channel_id=1, source_target_pairs={{0,0},{1,1},{8,2},{9,3},{16,4},{17,5},{24,6},{25,7},{2,8},{3,9},{1... | collective-permute-start | bytes 1572872 | tf_op jit(solution)/shard_map/ppermute | solution.py:244
Sparse Core Ops, SparseCore 0:
  56.1 34.5 reduce-scatter.2
  93.0 84.2 reduce-scatter.4
  188.5 46.4 all-gather.2

commit v2 on v1

v2 whole, which is shorter than its diff:
```python
import functools
import jax
import jax.numpy as jnp
from jax import lax
from jax.experimental import pallas as pl
from jax.experimental.pallas import tpu as pltpu
from jax.sharding import PartitionSpec as P

GROUP = 16
SPLIT = 128
KS = 7
KL = 128
BF = jnp.bfloat16
F32 = jnp.float32
MIB = 1024 * 1024


def in_proj_body(x_ref, w_ref, o_ref):
    parts, pieces, rows, width = o_ref.shape[0], o_ref.shape[1], o_ref.shape[3], o_ref.shape[4]
    made = jnp.dot(x_ref[...], w_ref[0], preferred_element_type=F32).astype(BF)
    for p in range(parts):
        for i in range(pieces):
            o_ref[p, i, 0] = made[i * rows : (i + 1) * rows, p * width : (p + 1) * width]


def in_proj(x, w, parts, weight=1):
    pieces, rows, depth = x.shape
    chan = w.shape[2]
    width = chan // parts
    if width % 128:
        y = jnp.einsum("ird,kdpc->pikrc", x, w.reshape(3, depth, parts, width), preferred_element_type=F32)
        return y.astype(BF)
    tile = chan if pieces * rows <= 256 else max(width, chan // 2)
    each = tile // width
    return pl.pallas_call(
        in_proj_body,
        grid=(3, chan // tile),
        in_specs=[
            pl.BlockSpec((pieces * rows, depth), lambda k, p: (0, 0)),
            pl.BlockSpec((1, depth, tile), lambda k, p: (k, 0, p)),
        ],
        out_specs=pl.BlockSpec((each, pieces, 1, rows, width), lambda k, p: (p, 0, k, 0, 0)),
        out_shape=jax.ShapeDtypeStruct((parts, pieces, 3, rows, width), BF),
        compiler_params=pltpu.CompilerParams(vmem_limit_bytes=48 * MIB),
        cost_estimate=pl.CostEstimate(
            flops=2 * pieces * rows * depth * 3 * chan * weight,
            bytes_accessed=2 * (3 * depth * chan + pieces * rows * (depth + 3 * chan)),
            transcendentals=0,
        ),
    )(x.reshape(pieces * rows, depth), w)


def conv_body(groups, base_ref, a_ref, b_ref, pos_ref, short_ref, taps_ref, *refs):
    outs, (proj, prod, toep) = refs[:-3], refs[-3:]
    shards = outs[0].shape[0]
    rows, lanes = a_ref.shape[2], a_ref.shape[3]
    part = rows // shards
    shard_len = sum(o.shape[1] for o in outs)
    near = a_ref.shape[0]
    for k in range(3):
        proj[k, pl.ds(0, 8), :] = jnp.zeros((8, lanes), F32)
    for i in range(near + b_ref.shape[0]):
        y_ref, at, base = (a_ref, i, base_ref[0]) if i < near else (b_ref, i - near, base_ref[1])
        offset = lax.bitwise_xor(jnp.int32(i), base) * part + 8
        for t in range(shards):
            place = pl.ds(pl.multiple_of(offset + t * shard_len, 8), part)
            for k in range(3):
                proj[k, place, :] = y_ref[at, k, pl.ds(t * part, part), :].astype(F32)
    prod[pl.ds(0, KL), :] = jnp.zeros((KL, lanes), BF)
    for g in range(groups):
        row = jnp.broadcast_to(taps_ref[0, pl.ds(g, 1), :], (KL, 2 * KL))
        toep[pl.ds(g * KL, KL), :] = pltpu.roll(row, 0, 1, stride=1, stride_axis=0)
    lag = (
        KL
        + lax.broadcasted_iota(jnp.int32, (KL, 2 * KL), 0)
        - lax.broadcasted_iota(jnp.int32, (KL, 2 * KL), 1)
    )
    group_of = lax.broadcasted_iota(jnp.int32, (KL, lanes), 1) // GROUP

    def block(start):
        pos = pos_ref[pl.ds(start, KL), :]
        pos_lanes = jnp.broadcast_to(pos, (KL, lanes))
        sums = [None, None, None]
        window = [proj[k, pl.ds(start, KL + 8), :] for k in range(3)]
        for j in range(KS):
            keep = pos_lanes >= j
            for k in range(3):
                source = window[k][8 - j : 8 - j + KL]
                term = short_ref[j, k : k + 1, :] * source
                if j == 0:
                    sums[k] = term
                else:
                    sums[k] = sums[k] + jnp.where(keep, term, 0.0)
        prod[pl.ds(start + KL, KL), :] = (sums[1] * sums[2]).astype(BF)
        source = prod[pl.ds(start, 2 * KL), :]
        linked = (lag <= jnp.broadcast_to(pos, (KL, 2 * KL))) & (lag >= 0)
        total = jnp.zeros((KL, lanes), F32)
        for g in range(groups):
            masked = jnp.where(linked, toep[pl.ds(g * KL, KL), :], 0.0).astype(BF)
            made = jnp.dot(masked, source, preferred_element_type=F32)
            total = jnp.where(group_of == g, made, total)
        return (sums[0] * total).astype(BF)

    def shard(t, carry):
        for b in range(shard_len // KL):
            gated = block(pl.multiple_of(t * shard_len + b * KL, KL))
            begin = 0
            for o in outs:
                end = begin + o.shape[1]
                lo, hi = max(begin, b * KL), min(end, b * KL + KL)
                if lo < hi:
                    o[t, lo - begin : hi - begin, :] = gated[lo - b * KL : hi - b * KL]
                begin = end
        return carry

    lax.fori_loop(0, shards, shard, 0)


def convolve(first, second, position, short, taps, shards, base, splits):
    pieces, _, rows, chan = second.shape
    near = first.shape[0]
    pieces += near
    seq_len = pieces * rows
    tile = 128 if chan % 128 == 0 else chan
    groups = tile // GROUP
    return pl.pallas_call(
        functools.partial(conv_body, groups),
        grid_spec=pltpu.PrefetchScalarGridSpec(
            num_scalar_prefetch=1,
            grid=(chan // tile,),
            in_specs=[
                pl.BlockSpec((near, 3, rows, tile), lambda c, s: (0, 0, 0, c)),
                pl.BlockSpec((pieces - near, 3, rows, tile), lambda c, s: (0, 0, 0, c)),
                pl.BlockSpec((seq_len, 1), lambda c, s: (0, 0)),
                pl.BlockSpec((KS, 3, tile), lambda c, s: (0, 0, c)),
                pl.BlockSpec((1, groups, 2 * KL), lambda c, s: (c, 0, 0)),
            ],
            out_specs=[pl.BlockSpec((shards, n, tile), lambda c, s: (0, 0, c)) for n in splits],
            scratch_shapes=[
                pltpu.VMEM((3, seq_len + 8, tile), F32),
                pltpu.VMEM((seq_len + KL, tile), BF),
                pltpu.VMEM((groups * KL, 2 * KL), F32),
            ],
        ),
        out_shape=[jax.ShapeDtypeStruct((shards, n, chan), BF) for n in splits],
        compiler_params=pltpu.CompilerParams(vmem_limit_bytes=48 * MIB),
        cost_estimate=pl.CostEstimate(
            flops=2 * seq_len * chan * 2 * KL * groups,
            bytes_accessed=seq_len * chan * 8,
            transcendentals=0,
        ),
    )(base, first, second, position, short, taps.reshape(chan // tile, groups, 2 * KL))


def out_proj_body(place_ref, g_ref, w_ref, o_ref):
    parts, seq_len = g_ref.shape[0], g_ref.shape[1]
    pieces, rows = o_ref.shape[0], o_ref.shape[1]

    def product(at):
        left = jnp.concatenate([g_ref[p, at, :] for p in range(parts)], axis=1)
        return jnp.dot(left, w_ref[...], preferred_element_type=F32).astype(BF)

    if pieces * rows == seq_len:
        made = product(pl.ds(0, seq_len))
        for t in range(pieces):
            o_ref[place_ref[1 + pieces + t]] = made[t * rows : (t + 1) * rows]
    else:
        for e in range(pieces):
            at = pl.multiple_of(place_ref[1 + e] * rows, rows)
            o_ref[e] = product(pl.ds(at, rows))


def out_proj(g, w, place, pieces, rows, cols):
    parts, seq_len, width = g.shape
    tile = min(512, cols)
    per = cols // tile
    return pl.pallas_call(
        out_proj_body,
        grid_spec=pltpu.PrefetchScalarGridSpec(
            num_scalar_prefetch=1,
            grid=(per,),
            in_specs=[
                pl.BlockSpec((parts, seq_len, width), lambda n, s: (0, 0, 0)),
                pl.BlockSpec((parts * width, tile), lambda n, s: (0, s[0] * per + n)),
            ],
            out_specs=pl.BlockSpec((pieces, rows, tile), lambda n, s: (0, 0, n)),
        ),
        out_shape=jax.ShapeDtypeStruct((pieces, rows, cols), BF),
        compiler_params=pltpu.CompilerParams(vmem_limit_bytes=48 * MIB),
        cost_estimate=pl.CostEstimate(
            flops=2 * pieces * rows * parts * width * cols * 16,
            bytes_accessed=2 * (parts * width * (seq_len + cols) + pieces * rows * cols),
            transcendentals=0,
        ),
    )(place, g, w)


def shards(tokens, norm_gain, in_weight, short_filter, long_filter, out_weight, segment_ids):
    n_seq, n_fsdp, n_tp = (lax.axis_size(a) for a in ("seq", "fsdp", "tp"))
    plane = n_fsdp * n_tp
    rows_dev, width_all = tokens.shape
    depth = in_weight.shape[1]
    chan_dev = in_weight.shape[2]
    z, f, c = (lax.axis_index(a) for a in ("seq", "fsdp", "tp"))
    q = f * n_tp + c
    rows = rows_dev // plane
    seq_len = segment_ids.shape[0]

    def swap_core(v):
        return lax.ppermute(v, "tp", [(i, i ^ 1) for i in range(n_tp)])

    def swap_chip(v, e):
        return lax.ppermute(v, "fsdp", [(i, i ^ e) for i in range(n_fsdp)])

    mine = lax.dynamic_slice_in_dim(tokens, q * rows, rows, 0).astype(F32)
    squares = jnp.mean(mine * mine, axis=1, keepdims=True)
    normed = (mine * lax.rsqrt(squares + 1e-06) * norm_gain).astype(BF)
    split = normed.reshape(rows, n_seq, depth).transpose(1, 0, 2)
    own = lax.all_to_all(split, "seq", 0, 0).reshape(n_seq * rows, depth)
    near = swap_core(own)
    far = [swap_chip(own, e) for e in range(1, n_fsdp)]
    first = in_proj(jnp.stack([own, near]), in_weight, n_seq)
    got_first = lax.psum_scatter(first, "seq", scatter_dimension=0)
    far, first = lax.optimization_barrier((far, first))
    both = jnp.broadcast_to(jnp.stack(far)[None], (n_tp, n_fsdp - 1, n_seq * rows, depth))
    both = lax.all_to_all(both, "tp", 0, 0)
    both = both.transpose(1, 0, 2, 3).reshape(n_tp * (n_fsdp - 1), n_seq * rows, depth)
    second = in_proj(both, in_weight, n_seq, 10)
    got_second = lax.psum_scatter(second, "seq", scatter_dimension=0)

    chan = chan_dev // n_seq
    groups = chan // GROUP
    at = jnp.arange(seq_len, dtype=jnp.int32)
    earlier = (segment_ids[None, :] == segment_ids[:, None]) & (at[None, :] < at[:, None])
    position = jnp.sum(earlier.astype(jnp.int32), axis=1, keepdims=True)
    short = lax.dynamic_slice_in_dim(short_filter, z * chan, chan, 2)
    taps = lax.dynamic_slice_in_dim(long_filter, z * groups, groups, 1)
    taps = jnp.concatenate(
        [jnp.zeros((1, groups), F32), taps[::-1], jnp.zeros((KL - 1, groups), F32)], axis=0
    ).T
    splits = (SPLIT, rows_dev - SPLIT)
    base = jnp.stack([q, f * n_tp]).astype(jnp.int32)
    gated = convolve(got_first, got_second, position, short, taps, n_seq, base, splits)

    halves = plane // n_seq
    cols = out_weight.shape[1] // halves

    def block_of(p):
        return lax.bitwise_xor(p // halves, z)

    def place_for(core):
        piece = [lax.bitwise_xor(f, e) * n_tp + core for e in range(n_fsdp)]
        blocks = [block_of(p) for p in piece]
        inverse = [lax.bitwise_xor(lax.bitwise_xor(t, z) * halves // n_tp, f) for t in range(n_fsdp)]
        return jnp.stack([piece[0] % halves] + blocks + inverse).astype(jnp.int32)

    place_away, place_keep = place_for(1 - c), place_for(c)

    def flat(s, p):
        return (p // n_tp * n_seq + s) * n_tp + p % n_tp

    pairs = [
        (flat(s, p), flat((p // halves) ^ s, s * halves + p % halves))
        for s in range(n_seq)
        for p in range(plane)
    ]
    placed, sends = [], None
    gathers = [lax.all_gather(part, "seq", axis=0) for part in gated]
    for gathered, count in zip(gathers, splits):
        if sends is not None:
            gathered, sends = lax.optimization_barrier((gathered, sends))
            placed[-1] = sends
        gathered = gathered.reshape(n_seq, n_seq * count, chan)
        away = out_proj(gathered, out_weight, place_away, n_fsdp, count, cols)
        near = swap_core(away)
        keep = out_proj(gathered, out_weight, place_keep, n_fsdp, count, cols)
        total = keep[0].astype(F32) + near[0].astype(F32)
        sends = [(keep[e].astype(F32) + near[e].astype(F32)).astype(BF) for e in range(1, n_fsdp)]
        for e in range(1, n_fsdp):
            total = total + swap_chip(sends[e - 1], e).astype(F32)
        sends = total.astype(BF)
        placed.append(sends)
    placed = [lax.ppermute(p, ("fsdp", "seq", "tp"), pairs) for p in placed]
    residual = lax.dynamic_slice_in_dim(tokens, q * cols, cols, 1)
    return (residual.astype(F32) + jnp.concatenate(placed, axis=0).astype(F32)).astype(BF)


def solution(mesh):
    return jax.shard_map(
        shards,
        mesh=mesh,
        in_specs=(
            P("seq", None),
            P(),
            P(None, "seq", ("fsdp", "tp")),
            P(None, None, ("fsdp", "tp")),
            P(None, ("fsdp", "tp")),
            P(("fsdp", "tp"), "seq"),
            P(),
        ),
        out_specs=P("seq", ("fsdp", "tp")),
        check_vma=False,
    )
```

time: 333 us -> 285 us (0.86)
  the two profiles are of different devices: /device:TPU:2 before, /device:TPU:18 now
where the time goes in v2:
time: 285 us; the launch traced here: 284 us
  waiting for transfers between devices  172 us (60%)
  Pallas kernels  43.7 us (15%)
  blocking collectives  23 us (8%)
  starting transfers between devices  17.6 us (6%)
  between operations  13.7 us (5%)
  local copies, waits for them, and re-layouts  8.08 us (3%)
  other arithmetic  6.55 us (2%)
    reduce_scatter x1, waiting for transfers between devices, shards(): got_second = lax.psum_scatter(second, 'seq', scatter_dimension=0)  85.7 us
    ppermute x9, waiting for transfers between devices, swap_chip(): return lax.ppermute(v, 'fsdp', [(i, i ^ e) for i in range(n_fsdp)])  40.6 us
    all_gather x2, waiting for transfers between devices, shards(): gathers = [lax.all_gather(part, 'seq', axis=0) for part in gated]  32.1 us
    pallas_call x2, Pallas kernels, in_proj(): pl.pallas_call(in_proj_body, grid=(3, chan // tile), in_specs=[pl.BlockSp...  21.6 us
    all_to_all x1, blocking collectives, shards(): own = lax.all_to_all(split, 'seq', 0, 0).reshape(n_seq * rows, depth)  16.8 us
    ppermute x2, waiting for transfers between devices, shards(): placed = [lax.ppermute(p, ('fsdp', 'seq', 'tp'), pairs) for p in placed]  13.3 us
    pallas_call x4, Pallas kernels, out_proj(): pl.pallas_call(out_proj_body, grid_spec=pltpu.PrefetchScalarGridSpec(num_...  13.2 us
    ppermute x9, starting transfers between devices, swap_chip(): return lax.ppermute(v, 'fsdp', [(i, i ^ e) for i in range(n_fsdp)])  10.6 us
  transfers between devices with their start and end apart: 18, of which 12 were waited for; matrix products, arithmetic and copies ran while one was open for 1% of the time, Pallas kernels for 11%

profile of v2, /device:TPU:18, one launch (start us, length us, event | category | flops | bytes accessed | tf_op | source)
XLA Modules:
  0.0 284.4 jit_solution(7200211572161827927)
XLA Ops:
  6.5 1.3 fusion.1
  7.8 1.3 fusion.3
  9.1 0.4 reshape.60
  9.5 0.3 copy.22
  9.8 16.8 %all_to_all.10 = bf16[4,32,2048]{2,1,0:T(8,128)(2,1)S(1)} all-to-all(bf16[4,32,2048]{2,1,0:T(8,128)(2,1)S(1)} %copy.22), channel_id=1, replica_groups=mesh['fsdp'=4,'seq'=4,'tp'=2] {'seq'}, dimensions={0} | all-to-all | bytes 1048576 | tf_op jit(solution)/shard_map/all_to_all | solution.py:219
  26.6 0.5 collective-permute-start.1
  27.1 1.5 collective-permute-start.2
  28.6 1.4 collective-permute-start.3
  30.2 8.1 %shard_map.73 = bf16[4,2,3,128,256]{4,3,2,1,0:T(8,128)(2,1)} custom-call(bf16[256,2048]{1,0:T(8,128)(2,1)S(1)} %bitcast.65, bf16[3,2048,1024]{2,1,0:T(8,128)(2,1)} %w_ref.7), custom_call_target="tpu_custom_call" | custom-call | flops 3221225472 | bytes 15204352 | tf_op jit(solution)/shard_map/pallas_call | solution.py:35
  38.3 3.0 %collective-permute-done.1 = bf16[128,2048]{1,0:T(8,128)(2,1)S(1)} collective-permute-done((bf16[128,2048]{1,0:T(8,128)(2,1)S(1)}, bf16[128,2048]{1,0:T(8,128)(2,1)S(1)}, u32[]{:S(2)}, u32[]{:S(2)}) %collective-permute-start.1) | collective-permute-done | bytes 524320 | tf_op jit(solution)/shard_map/ppermute | solution.py:213
  41.3 10.2 %collective-permute-done.2 = bf16[128,2048]{1,0:T(8,128)(2,1)S(1)} collective-permute-done((bf16[128,2048]{1,0:T(8,128)(2,1)S(1)}, bf16[128,2048]{1,0:T(8,128)(2,1)S(1)}, u32[]{:S(2)}, u32[]{:S(2)}) %collective-permute-start.2) | collective-permute-done | bytes 524320 | tf_op jit(solution)/shard_map/ppermute | solution.py:213
  51.5 1.6 collective-permute-done.3
  53.3 0.4 broadcast_in_dim.6
  53.7 6.3 %all_to_all.11 = bf16[2,3,128,2048]{3,2,1,0:T(8,128)(2,1)S(1)} all-to-all(bf16[2,3,128,2048]{3,2,1,0:T(8,128)(2,1)S(1)} %broadcast_in_dim.6), channel_id=1, replica_groups=mesh['fsdp'=4,'seq'=4,'tp'=2] {'tp'}, dimensions={0} | all-to-all | bytes 6291456 | tf_op jit(solution)/shard_map/all_to_all | solution.py:226
  59.9 0.4 copy.23
  60.3 13.5 %shard_map.74 = bf16[4,6,3,128,256]{4,3,2,1,0:T(8,128)(2,1)} custom-call(bf16[768,2048]{1,0:T(8,128)(2,1)S(1)} %bitcast.66, bf16[3,2048,1024]{2,1,0:T(8,128)(2,1)} %w_ref.7), custom_call_target="tpu_custom_call" | custom-call | flops 96636764160 | bytes 20447232 | tf_op jit(solution)/shard_map/pallas_call | solution.py:35
  73.9 0.6 copy-done.5
  74.5 0.5 convert_reduce_fusion
  75.0 0.2 copy.25.pos_ref
  75.3 0.7 constant_dynamic-slice_fusion
  76.3 85.7 %reduce-scatter.5.cloned.1.call-done = bf16[1,6,3,128,256]{4,3,2,1,0:T(8,128)(2,1)} async-done(((bf16[4,6,3,128,256]{4,3,2,1,0:T(8,128)(2,1)}), bf16[1,6,3,128,256]{4,3,2,1,0:T(8,128)(2,1)}) %reduce-scatter.5.cloned.1.call-update) | async-done | bytes 1179664 | tf_op jit(solution)/shard_map/reduce_scatter | solution.py:229
  162.1 1.3 copy-done.1
  163.3 1.0 copy-done.4
  164.3 8.9 %shard_map.75 = (bf16[4,128,256]{2,1,0:T(8,128)(2,1)}, bf16[4,128,256]{2,1,0:T(8,128)(2,1)}) custom-call(s32[2]{0:T(128)S(1)} %pad_add_fusion.base_ref, bf16[2,3,128,256]{3,2,1,0:T(8,128)(2,1)S(1)} %bitcast.72, bf16[6,3,128,256]{3,2,1,0:T(8,128)(2,1)S(1)} %bitcast.67, s32[1024,1]{1,0:T(8,128)S(1)} %copy.25.pos_ref, f32[7,3,256]{2,1,0:T(4,128)S(1)} %copy.26.short_ref, ...), custom_call_target="tpu_custom_call" | custom-call | flops 1073741824 | bytes 2097152 | tf_op jit(solution)/shard_map/pallas_call | solution.py:126
  173.9 27.0 %all-gather.7.cloned.1.call-done = bf16[16,128,256]{2,1,0:T(8,128)(2,1)} async-done(((bf16[4,128,256]{2,1,0:T(8,128)(2,1)}), bf16[16,128,256]{2,1,0:T(8,128)(2,1)}) %all-gather.7.cloned.1.call-update) | async-done | bytes 1048592 | tf_op jit(solution)/shard_map/all_gather | solution.py:268
  200.9 1.2 copy-done.2
  202.1 3.3 %shard_map.77 = bf16[4,128,1024]{2,1,0:T(8,128)(2,1)S(1)} custom-call(s32[9]{0:T(128)S(1)} %stack.103.place_ref, bf16[4,512,256]{2,1,0:T(8,128)(2,1)S(1)} %bitcast.68, bf16[1024,2048]{1,0:T(8,128)(2,1)} %w_ref.11), custom_call_target="tpu_custom_call" | custom-call | flops 17179869184 | bytes 4194304 | tf_op jit(solution)/shard_map/pallas_call | solution.py:177
  205.5 3.3 %shard_map.76 = bf16[4,128,1024]{2,1,0:T(8,128)(2,1)S(1)} custom-call(s32[9]{0:T(128)S(1)} %stack.97.place_ref, bf16[4,512,256]{2,1,0:T(8,128)(2,1)S(1)} %bitcast.69, bf16[1024,2048]{1,0:T(8,128)(2,1)} %w_ref.11), custom_call_target="tpu_custom_call" | custom-call | flops 17179869184 | bytes 4194304 | tf_op jit(solution)/shard_map/pallas_call | solution.py:177
  208.8 0.3 fusion.10
  209.1 1.5 collective-permute-start.7
  210.7 0.6 collective-permute-start.6
  211.2 1.5 collective-permute-start.5
  212.7 6.6 %collective-permute-done.7 = bf16[128,1024]{1,0:T(8,128)(2,1)S(1)} collective-permute-done((bf16[128,1024]{1,0:T(8,128)(2,1)S(1)}, bf16[128,1024]{1,0:T(8,128)(2,1)S(1)}, u32[]{:S(2)}, u32[]{:S(2)}) %collective-permute-start.7) | collective-permute-done | bytes 262176 | tf_op jit(solution)/shard_map/ppermute | solution.py:213
  219.2 5.2 %collective-permute-done.6 = bf16[128,1024]{1,0:T(8,128)(2,1)S(1)} collective-permute-done((bf16[128,1024]{1,0:T(8,128)(2,1)S(1)}, bf16[128,1024]{1,0:T(8,128)(2,1)S(1)}, u32[]{:S(2)}, u32[]{:S(2)}) %collective-permute-start.6) | collective-permute-done | bytes 262176 | tf_op jit(solution)/shard_map/ppermute | solution.py:213
  224.7 5.1 %all-gather.5.cloned.1.call-done = bf16[16,128,256]{2,1,0:T(8,128)(2,1)} async-done(((bf16[4,128,256]{2,1,0:T(8,128)(2,1)}), bf16[16,128,256]{2,1,0:T(8,128)(2,1)}) %all-gather.5.cloned.1.call-update) | async-done | bytes 1048592 | tf_op jit(solution)/shard_map/all_gather | solution.py:268
  229.8 1.2 copy-done.3
  231.0 3.3 %shard_map.79 = bf16[4,128,1024]{2,1,0:T(8,128)(2,1)S(1)} custom-call(s32[9]{0:T(128)S(1)} %stack.103.place_ref, bf16[4,512,256]{2,1,0:T(8,128)(2,1)S(1)} %bitcast.70, bf16[1024,2048]{1,0:T(8,128)(2,1)} %w_ref.11), custom_call_target="tpu_custom_call" | custom-call | flops 17179869184 | bytes 4194304 | tf_op jit(solution)/shard_map/pallas_call | solution.py:177
  234.4 3.3 %shard_map.78 = bf16[4,128,1024]{2,1,0:T(8,128)(2,1)S(1)} custom-call(s32[9]{0:T(128)S(1)} %stack.97.place_ref, bf16[4,512,256]{2,1,0:T(8,128)(2,1)S(1)} %bitcast.71, bf16[1024,2048]{1,0:T(8,128)(2,1)} %w_ref.11), custom_call_target="tpu_custom_call" | custom-call | flops 17179869184 | bytes 4194304 | tf_op jit(solution)/shard_map/pallas_call | solution.py:177
  237.7 0.3 fusion.13
  238.0 1.5 collective-permute-start.12
  239.5 0.6 collective-permute-start.11
  240.1 1.5 collective-permute-start.10
  241.6 3.3 %collective-permute-start.8 = (bf16[128,1024]{1,0:T(8,128)(2,1)S(1)}, bf16[128,1024]{1,0:T(8,128)(2,1)S(1)}, u32[]{:S(2)}, u32[]{:S(2)}) collective-permute-start(bf16[128,1024]{1,0:T(8,128)(2,1)S(1)} %fusion.9), channel_id=1, source_target_pairs={{0,0},{1,1},{8,2},{9,3},{16,4},{17,5},{24,6},{25,7},{2,10},{3,11},... | collective-permute-start | bytes 786440 | tf_op jit(solution)/shard_map/ppermute | solution.py:283
  244.9 3.9 %collective-permute-done.12 = bf16[128,1024]{1,0:T(8,128)(2,1)S(1)} collective-permute-done((bf16[128,1024]{1,0:T(8,128)(2,1)S(1)}, bf16[128,1024]{1,0:T(8,128)(2,1)S(1)}, u32[]{:S(2)}, u32[]{:S(2)}) %collective-permute-start.12) | collective-permute-done | bytes 262176 | tf_op jit(solution)/shard_map/ppermute | solution.py:213
  248.8 10.1 %collective-permute-done.11 = bf16[128,1024]{1,0:T(8,128)(2,1)S(1)} collective-permute-done((bf16[128,1024]{1,0:T(8,128)(2,1)S(1)}, bf16[128,1024]{1,0:T(8,128)(2,1)S(1)}, u32[]{:S(2)}, u32[]{:S(2)}) %collective-permute-start.11) | collective-permute-done | bytes 262176 | tf_op jit(solution)/shard_map/ppermute | solution.py:213
  259.1 3.4 %collective-permute-start.13 = (bf16[128,1024]{1,0:T(8,128)(2,1)S(1)}, bf16[128,1024]{1,0:T(8,128)(2,1)S(1)}, u32[]{:S(2)}, u32[]{:S(2)}) collective-permute-start(bf16[128,1024]{1,0:T(8,128)(2,1)S(1)} %fusion.6), channel_id=1, source_target_pairs={{0,0},{1,1},{8,2},{9,3},{16,4},{17,5},{24,6},{25,7},{2,10},{3,11},... | collective-permute-start | bytes 786440 | tf_op jit(solution)/shard_map/ppermute | solution.py:283
  262.5 13.3 %collective-permute-done.13 = bf16[128,1024]{1,0:T(8,128)(2,1)S(1)} collective-permute-done((bf16[128,1024]{1,0:T(8,128)(2,1)S(1)}, bf16[128,1024]{1,0:T(8,128)(2,1)S(1)}, u32[]{:S(2)}, u32[]{:S(2)}) %collective-permute-start.13) | collective-permute-done | bytes 262176 | tf_op jit(solution)/shard_map/ppermute | solution.py:283
  275.8 2.0 add_convert_fusion
  (40 shorter events, 1.6 us)
Async XLA Ops:
  6.5 68.7 %copy-start = (f32[7,3,1024]{2,0,1:T(8,128)S(1)}, f32[7,3,1024]{2,0,1:T(8,128)}, u32[]{:S(2)}) copy-start(f32[7,3,1024]{2,0,1:T(8,128)} %param.10) | copy-start | bytes 258052
  6.5 69.8 %reduce-scatter.3.cloned.1.call-start = ((), (), s32[]{:S(2)}) async-start(), calls=%async_computation.4 | async-start | bytes 1966080 | tf_op jit(solution)/shard_map/reduce_scatter | solution.py:223
  26.6 3.5 %collective-permute-start = (bf16[128,2048]{1,0:T(8,128)(2,1)S(1)}, bf16[128,2048]{1,0:T(8,128)(2,1)S(1)}, u32[]{:S(2)}, u32[]{:S(2)}) collective-permute-start(bf16[128,2048]{1,0:T(8,128)(2,1)S(1)} %bitcast.75), channel_id=1, source_target_pairs={{0,1},{1,0},{2,3},{3,2},{4,5},{5,4},{6,7},{7,6},{8,9},{9,8},{10,11... | collective-permute-start | bytes 1572872 | tf_op jit(solution)/shard_map/ppermute | solution.py:210
  26.6 14.7 %collective-permute-start.1 = (bf16[128,2048]{1,0:T(8,128)(2,1)S(1)}, bf16[128,2048]{1,0:T(8,128)(2,1)S(1)}, u32[]{:S(2)}, u32[]{:S(2)}) collective-permute-start(bf16[128,2048]{1,0:T(8,128)(2,1)S(1)} %bitcast.76), channel_id=1, source_target_pairs={{0,8},{8,0},{16,24},{24,16},{1,9},{9,1},{17,25},{25,17},{2,10},{10... | collective-permute-start | bytes 1572872 | tf_op jit(solution)/shard_map/ppermute | solution.py:213
  27.1 24.4 %collective-permute-start.2 = (bf16[128,2048]{1,0:T(8,128)(2,1)S(1)}, bf16[128,2048]{1,0:T(8,128)(2,1)S(1)}, u32[]{:S(2)}, u32[]{:S(2)}) collective-permute-start(bf16[128,2048]{1,0:T(8,128)(2,1)S(1)} %bitcast.77), channel_id=1, source_target_pairs={{0,16},{8,24},{16,0},{24,8},{1,17},{9,25},{17,1},{25,9},{2,18},{10... | collective-permute-start | bytes 1572872 | tf_op jit(solution)/shard_map/ppermute | solution.py:213
  28.6 24.5 %collective-permute-start.3 = (bf16[128,2048]{1,0:T(8,128)(2,1)S(1)}, bf16[128,2048]{1,0:T(8,128)(2,1)S(1)}, u32[]{:S(2)}, u32[]{:S(2)}) collective-permute-start(bf16[128,2048]{1,0:T(8,128)(2,1)S(1)} %bitcast.78), channel_id=1, source_target_pairs={{0,24},{8,16},{16,8},{24,0},{1,25},{9,17},{17,9},{25,1},{2,26},{10... | collective-permute-start | bytes 1572872 | tf_op jit(solution)/shard_map/ppermute | solution.py:213
  38.3 123.8 %reduce-scatter.5.cloned.1.call-start = ((), (), s32[]{:S(2)}) async-start(), calls=%async_computation.5 | async-start | bytes 5898240 | tf_op jit(solution)/shard_map/reduce_scatter | solution.py:229
  73.8 0.7 copy-start.5
  73.9 127.0 %all-gather.7.cloned.1.call-start = ((), (), s32[]{:S(2)}) async-start(), calls=%async_computation.7 | async-start | bytes 1310720 | tf_op jit(solution)/shard_map/all_gather | solution.py:268
  162.1 1.3 copy-start.1
  163.3 1.0 copy-start.4
  173.3 56.5 %all-gather.5.cloned.1.call-start = ((), (), s32[]{:S(2)}) async-start(), calls=%async_computation.6 | async-start | bytes 1310720 | tf_op jit(solution)/shard_map/all_gather | solution.py:268
  200.9 1.2 copy-start.2
  205.4 3.4 %collective-permute-start.4 = (bf16[4,128,1024]{2,1,0:T(8,128)(2,1)S(1)}, bf16[4,128,1024]{2,1,0:T(8,128)(2,1)S(1)}, u32[]{:S(2)}, u32[]{:S(2)}) collective-permute-start(bf16[4,128,1024]{2,1,0:T(8,128)(2,1)S(1)} %shard_map.77), channel_id=1, source_target_pairs={{0,1},{1,0},{2,3},{3,2},{4,5},{5,4},{6,7},{7,6},{8,9},{9,8},{10,11... | collective-permute-start | bytes 3145736 | tf_op jit(solution)/shard_map/ppermute | solution.py:210
  209.1 10.1 %collective-permute-start.7 = (bf16[128,1024]{1,0:T(8,128)(2,1)S(1)}, bf16[128,1024]{1,0:T(8,128)(2,1)S(1)}, u32[]{:S(2)}, u32[]{:S(2)}) collective-permute-start(bf16[128,1024]{1,0:T(8,128)(2,1)S(1)} %get-tuple-element.23), channel_id=1, source_target_pairs={{0,24},{8,16},{16,8},{24,0},{1,25},{9,17},{17,9},{25,1},{2,26},{10... | collective-permute-start | bytes 786440 | tf_op jit(solution)/shard_map/ppermute | solution.py:213
  210.7 13.8 %collective-permute-start.6 = (bf16[128,1024]{1,0:T(8,128)(2,1)S(1)}, bf16[128,1024]{1,0:T(8,128)(2,1)S(1)}, u32[]{:S(2)}, u32[]{:S(2)}) collective-permute-start(bf16[128,1024]{1,0:T(8,128)(2,1)S(1)} %get-tuple-element.24), channel_id=1, source_target_pairs={{0,16},{8,24},{16,0},{24,8},{1,17},{9,25},{17,1},{25,9},{2,18},{10... | collective-permute-start | bytes 786440 | tf_op jit(solution)/shard_map/ppermute | solution.py:213
  211.2 13.3 %collective-permute-start.5 = (bf16[128,1024]{1,0:T(8,128)(2,1)S(1)}, bf16[128,1024]{1,0:T(8,128)(2,1)S(1)}, u32[]{:S(2)}, u32[]{:S(2)}) collective-permute-start(bf16[128,1024]{1,0:T(8,128)(2,1)S(1)} %get-tuple-element.22), channel_id=1, source_target_pairs={{0,8},{8,0},{16,24},{24,16},{1,9},{9,1},{17,25},{25,17},{2,10},{10... | collective-permute-start | bytes 786440 | tf_op jit(solution)/shard_map/ppermute | solution.py:213
  229.8 1.2 copy-start.3
  234.3 3.4 %collective-permute-start.9 = (bf16[4,128,1024]{2,1,0:T(8,128)(2,1)S(1)}, bf16[4,128,1024]{2,1,0:T(8,128)(2,1)S(1)}, u32[]{:S(2)}, u32[]{:S(2)}) collective-permute-start(bf16[4,128,1024]{2,1,0:T(8,128)(2,1)S(1)} %shard_map.79), channel_id=1, source_target_pairs={{0,1},{1,0},{2,3},{3,2},{4,5},{5,4},{6,7},{7,6},{8,9},{9,8},{10,11... | collective-permute-start | bytes 3145736 | tf_op jit(solution)/shard_map/ppermute | solution.py:210
  238.0 10.8 %collective-permute-start.12 = (bf16[128,1024]{1,0:T(8,128)(2,1)S(1)}, bf16[128,1024]{1,0:T(8,128)(2,1)S(1)}, u32[]{:S(2)}, u32[]{:S(2)}) collective-permute-start(bf16[128,1024]{1,0:T(8,128)(2,1)S(1)} %get-tuple-element.20), channel_id=1, source_target_pairs={{0,24},{8,16},{16,8},{24,0},{1,25},{9,17},{17,9},{25,1},{2,26},{10... | collective-permute-start | bytes 786440 | tf_op jit(solution)/shard_map/ppermute | solution.py:213
  239.5 19.4 %collective-permute-start.11 = (bf16[128,1024]{1,0:T(8,128)(2,1)S(1)}, bf16[128,1024]{1,0:T(8,128)(2,1)S(1)}, u32[]{:S(2)}, u32[]{:S(2)}) collective-permute-start(bf16[128,1024]{1,0:T(8,128)(2,1)S(1)} %get-tuple-element.21), channel_id=1, source_target_pairs={{0,16},{8,24},{16,0},{24,8},{1,17},{9,25},{17,1},{25,9},{2,18},{10... | collective-permute-start | bytes 786440 | tf_op jit(solution)/shard_map/ppermute | solution.py:213
  240.1 18.8 %collective-permute-start.10 = (bf16[128,1024]{1,0:T(8,128)(2,1)S(1)}, bf16[128,1024]{1,0:T(8,128)(2,1)S(1)}, u32[]{:S(2)}, u32[]{:S(2)}) collective-permute-start(bf16[128,1024]{1,0:T(8,128)(2,1)S(1)} %get-tuple-element.19), channel_id=1, source_target_pairs={{0,8},{8,0},{16,24},{24,16},{1,9},{9,1},{17,25},{25,17},{2,10},{10... | collective-permute-start | bytes 786440 | tf_op jit(solution)/shard_map/ppermute | solution.py:213
  241.6 20.9 %collective-permute-start.8 = (bf16[128,1024]{1,0:T(8,128)(2,1)S(1)}, bf16[128,1024]{1,0:T(8,128)(2,1)S(1)}, u32[]{:S(2)}, u32[]{:S(2)}) collective-permute-start(bf16[128,1024]{1,0:T(8,128)(2,1)S(1)} %fusion.9), channel_id=1, source_target_pairs={{0,0},{1,1},{8,2},{9,3},{16,4},{17,5},{24,6},{25,7},{2,10},{3,11},... | collective-permute-start | bytes 786440 | tf_op jit(solution)/shard_map/ppermute | solution.py:283
  259.1 16.7 %collective-permute-start.13 = (bf16[128,1024]{1,0:T(8,128)(2,1)S(1)}, bf16[128,1024]{1,0:T(8,128)(2,1)S(1)}, u32[]{:S(2)}, u32[]{:S(2)}) collective-permute-start(bf16[128,1024]{1,0:T(8,128)(2,1)S(1)} %fusion.6), channel_id=1, source_target_pairs={{0,0},{1,1},{8,2},{9,3},{16,4},{17,5},{24,6},{25,7},{2,10},{3,11},... | collective-permute-start | bytes 786440 | tf_op jit(solution)/shard_map/ppermute | solution.py:283
Sparse Core Ops, SparseCore 0:
  38.4 35.5 reduce-scatter.2
  76.3 85.7 reduce-scatter.4
  173.4 27.4 all-gather.6
  202.3 27.4 all-gather.4

commit v3 on v2

--- a/solution.py
+++ b/solution.py
@@ -7,12 +7,39 @@
 from jax.sharding import PartitionSpec as P
 
 GROUP = 16
-SPLIT = 128
+SPLIT = 160
 KS = 7
 KL = 128
 BF = jnp.bfloat16
 F32 = jnp.float32
 MIB = 1024 * 1024
+
+
+def norm_body(at_ref, t_ref, gain_ref, o_ref):
+    wide = t_ref[...].astype(F32)
+    squares = jnp.mean(wide * wide, axis=1, keepdims=True)
+    normed = (wide * lax.rsqrt(squares + 1e-06) * gain_ref[...]).astype(BF)
+    parts, _, depth = o_ref.shape
+    for p in range(parts):
+        o_ref[p] = normed[:, p * depth : (p + 1) * depth]
+
+
+def norm(tokens, gain, at, rows, parts):
+    width = tokens.shape[1]
+    return pl.pallas_call(
+        norm_body,
+        grid_spec=pltpu.PrefetchScalarGridSpec(
+            num_scalar_prefetch=1,
+            grid=(1,),
+            in_specs=[
+                pl.BlockSpec((rows, width), lambda i, s: (s[0], 0)),
+                pl.BlockSpec((1, width), lambda i, s: (0, 0)),
+            ],
+            out_specs=pl.BlockSpec((parts, rows, width // parts), lambda i, s: (0, 0, 0)),
+        ),
+        out_shape=jax.ShapeDtypeStruct((parts, rows, width // parts), BF),
+        compiler_params=pltpu.CompilerParams(vmem_limit_bytes=62 * MIB),
+    )(at, tokens, gain.reshape(1, width))
 
 
 def in_proj_body(x_ref, w_ref, o_ref):
@@ -50,8 +77,27 @@
     )(x.reshape(pieces * rows, depth), w)
 
 
-def conv_body(groups, base_ref, a_ref, b_ref, pos_ref, short_ref, taps_ref, *refs):
-    outs, (proj, prod, toep) = refs[:-3], refs[-3:]
+def toeplitz_body(taps_ref, o_ref):
+    groups = taps_ref.shape[1]
+    for g in range(groups):
+        row = jnp.broadcast_to(taps_ref[0, pl.ds(g, 1), :], (KL, 2 * KL))
+        o_ref[0, pl.ds(g * KL, KL), :] = pltpu.roll(row, 0, 1, stride=1, stride_axis=0).astype(BF)
+
+
+def toeplitz(taps):
+    tiles, groups, _ = taps.shape
+    return pl.pallas_call(
+        toeplitz_body,
+        grid=(tiles,),
+        in_specs=[pl.BlockSpec((1, groups, 2 * KL), lambda c: (c, 0, 0))],
+        out_specs=pl.BlockSpec((1, groups * KL, 2 * KL), lambda c: (c, 0, 0)),
+        out_shape=jax.ShapeDtypeStruct((tiles, groups * KL, 2 * KL), BF),
+        cost_estimate=pl.CostEstimate(flops=0, bytes_accessed=0, transcendentals=0),
+    )(taps)
+
+
+def conv_body(groups, base_ref, a_ref, b_ref, pos_ref, short_ref, toep_ref, *refs):
+    outs, (proj, prod) = refs[:-2], refs[-2:]
     shards = outs[0].shape[0]
     rows, lanes = a_ref.shape[2], a_ref.shape[3]
     part = rows // shards
@@ -60,16 +106,15 @@
     for k in range(3):
         proj[k, pl.ds(0, 8), :] = jnp.zeros((8, lanes), F32)
     for i in range(near + b_ref.shape[0]):
-        y_ref, at, base = (a_ref, i, base_ref[0]) if i < near else (b_ref, i - near, base_ref[1])
-        offset = lax.bitwise_xor(jnp.int32(i), base) * part + 8
+        y_ref, at = (a_ref, i) if i < near else (b_ref, i - near)
+        others = b_ref.shape[0] // near
+        apart = i if i < near else (1 + at % others) * near + at // others
+        offset = lax.bitwise_xor(jnp.int32(apart), base_ref[0]) * part + 8
         for t in range(shards):
             place = pl.ds(pl.multiple_of(offset + t * shard_len, 8), part)
             for k in range(3):
                 proj[k, place, :] = y_ref[at, k, pl.ds(t * part, part), :].astype(F32)
     prod[pl.ds(0, KL), :] = jnp.zeros((KL, lanes), BF)
-    for g in range(groups):
-        row = jnp.broadcast_to(taps_ref[0, pl.ds(g, 1), :], (KL, 2 * KL))
-        toep[pl.ds(g * KL, KL), :] = pltpu.roll(row, 0, 1, stride=1, stride_axis=0)
     lag = (
         KL
         + lax.broadcasted_iota(jnp.int32, (KL, 2 * KL), 0)
@@ -81,11 +126,10 @@
         pos = pos_ref[pl.ds(start, KL), :]
         pos_lanes = jnp.broadcast_to(pos, (KL, lanes))
         sums = [None, None, None]
-        window = [proj[k, pl.ds(start, KL + 8), :] for k in range(3)]
         for j in range(KS):
             keep = pos_lanes >= j
             for k in range(3):
-                source = window[k][8 - j : 8 - j + KL]
+                source = proj[k, pl.ds(start + (8 - j), KL), :]
                 term = short_ref[j, k : k + 1, :] * source
                 if j == 0:
                     sums[k] = term
@@ -94,9 +138,10 @@
         prod[pl.ds(start + KL, KL), :] = (sums[1] * sums[2]).astype(BF)
         source = prod[pl.ds(start, 2 * KL), :]
         linked = (lag <= jnp.broadcast_to(pos, (KL, 2 * KL))) & (lag >= 0)
+        linked = linked.astype(F32).astype(BF)
         total = jnp.zeros((KL, lanes), F32)
         for g in range(groups):
-            masked = jnp.where(linked, toep[pl.ds(g * KL, KL), :], 0.0).astype(BF)
+            masked = toep_ref[0, pl.ds(g * KL, KL), :] * linked
             made = jnp.dot(masked, source, preferred_element_type=F32)
             total = jnp.where(group_of == g, made, total)
         return (sums[0] * total).astype(BF)
@@ -116,12 +161,12 @@
     lax.fori_loop(0, shards, shard, 0)
 
 
-def convolve(first, second, position, short, taps, shards, base, splits):
+def convolve(first, second, position, short, matrices, shards, base, splits):
     pieces, _, rows, chan = second.shape
     near = first.shape[0]
     pieces += near
     seq_len = pieces * rows
-    tile = 128 if chan % 128 == 0 else chan
+    tile = chan // matrices.shape[0]
     groups = tile // GROUP
     return pl.pallas_call(
         functools.partial(conv_body, groups),
@@ -133,23 +178,22 @@
                 pl.BlockSpec((pieces - near, 3, rows, tile), lambda c, s: (0, 0, 0, c)),
                 pl.BlockSpec((seq_len, 1), lambda c, s: (0, 0)),
                 pl.BlockSpec((KS, 3, tile), lambda c, s: (0, 0, c)),
-                pl.BlockSpec((1, groups, 2 * KL), lambda c, s: (c, 0, 0)),
+                pl.BlockSpec((1, groups * KL, 2 * KL), lambda c, s: (c, 0, 0)),
             ],
             out_specs=[pl.BlockSpec((shards, n, tile), lambda c, s: (0, 0, c)) for n in splits],
             scratch_shapes=[
                 pltpu.VMEM((3, seq_len + 8, tile), F32),
                 pltpu.VMEM((seq_len + KL, tile), BF),
-                pltpu.VMEM((groups * KL, 2 * KL), F32),
             ],
         ),
         out_shape=[jax.ShapeDtypeStruct((shards, n, chan), BF) for n in splits],
-        compiler_params=pltpu.CompilerParams(vmem_limit_bytes=48 * MIB),
+        compiler_params=pltpu.CompilerParams(vmem_limit_bytes=62 * MIB),
         cost_estimate=pl.CostEstimate(
             flops=2 * seq_len * chan * 2 * KL * groups,
             bytes_accessed=seq_len * chan * 8,
             transcendentals=0,
         ),
-    )(base, first, second, position, short, taps.reshape(chan // tile, groups, 2 * KL))
+    )(base, first, second, position, short, matrices)
 
 
 def out_proj_body(place_ref, g_ref, w_ref, o_ref):
@@ -212,35 +256,34 @@
     def swap_chip(v, e):
         return lax.ppermute(v, "fsdp", [(i, i ^ e) for i in range(n_fsdp)])
 
-    mine = lax.dynamic_slice_in_dim(tokens, q * rows, rows, 0).astype(F32)
-    squares = jnp.mean(mine * mine, axis=1, keepdims=True)
-    normed = (mine * lax.rsqrt(squares + 1e-06) * norm_gain).astype(BF)
-    split = normed.reshape(rows, n_seq, depth).transpose(1, 0, 2)
+    chan = chan_dev // n_seq
+    groups = chan // GROUP
+    taps = lax.dynamic_slice_in_dim(long_filter, z * groups, groups, 1)
+    taps = jnp.concatenate(
+        [jnp.zeros((1, groups), F32), taps[::-1], jnp.zeros((KL - 1, groups), F32)], axis=0
+    ).T
+    tiles = chan // 128 if chan % 128 == 0 else 1
+    matrices = toeplitz(taps.reshape(tiles, groups // tiles, 2 * KL))
+    split = norm(tokens, norm_gain, q.astype(jnp.int32).reshape(1), rows, n_seq)
     own = lax.all_to_all(split, "seq", 0, 0).reshape(n_seq * rows, depth)
     near = swap_core(own)
     far = [swap_chip(own, e) for e in range(1, n_fsdp)]
     first = in_proj(jnp.stack([own, near]), in_weight, n_seq)
     got_first = lax.psum_scatter(first, "seq", scatter_dimension=0)
     far, first = lax.optimization_barrier((far, first))
-    both = jnp.broadcast_to(jnp.stack(far)[None], (n_tp, n_fsdp - 1, n_seq * rows, depth))
-    both = lax.all_to_all(both, "tp", 0, 0)
-    both = both.transpose(1, 0, 2, 3).reshape(n_tp * (n_fsdp - 1), n_seq * rows, depth)
-    second = in_proj(both, in_weight, n_seq, 10)
+    far = jnp.stack(far)
+    both = jnp.concatenate([far, swap_core(far)])
+    both, matrices = lax.optimization_barrier((both, matrices))
+    second = in_proj(both, in_weight, n_seq, 1)
     got_second = lax.psum_scatter(second, "seq", scatter_dimension=0)
 
-    chan = chan_dev // n_seq
-    groups = chan // GROUP
     at = jnp.arange(seq_len, dtype=jnp.int32)
     earlier = (segment_ids[None, :] == segment_ids[:, None]) & (at[None, :] < at[:, None])
     position = jnp.sum(earlier.astype(jnp.int32), axis=1, keepdims=True)
     short = lax.dynamic_slice_in_dim(short_filter, z * chan, chan, 2)
-    taps = lax.dynamic_slice_in_dim(long_filter, z * groups, groups, 1)
-    taps = jnp.concatenate(
-        [jnp.zeros((1, groups), F32), taps[::-1], jnp.zeros((KL - 1, groups), F32)], axis=0
-    ).T
     splits = (SPLIT, rows_dev - SPLIT)
-    base = jnp.stack([q, f * n_tp]).astype(jnp.int32)
-    gated = convolve(got_first, got_second, position, short, taps, n_seq, base, splits)
+    base = q.astype(jnp.int32).reshape(1)
+    gated = convolve(got_first, got_second, position, short, matrices, n_seq, base, splits)
 
     halves = plane // n_seq
     cols = out_weight.shape[1] // halves
@@ -281,7 +324,7 @@
         sends = total.astype(BF)
         placed.append(sends)
     placed = [lax.ppermute(p, ("fsdp", "seq", "tp"), pairs) for p in placed]
-    residual = lax.dynamic_slice_in_dim(tokens, q * cols, cols, 1)
+    residual = lax.optimization_barrier(lax.dynamic_slice_in_dim(tokens, q * cols, cols, 1))
     return (residual.astype(F32) + jnp.concatenate(placed, axis=0).astype(F32)).astype(BF)
 
 

time: 285 us -> 277 us (0.972); the launches traced: 284 us -> 272 us
  waiting for transfers between devices: 172 us -> 147 us
  blocking collectives: 23 us -> 34.4 us
  starting transfers between devices: 17.6 us -> 21.3 us
    all_gather x0 -> x1, blocking collectives: none -> 17.4 us  [shards(): gathers = [lax.all_gather(part, 'seq', axis=0) for part in gated]]
    ppermute x9, waiting for transfers between devices: 40.6 us -> 24.4 us  [swap_chip(): return lax.ppermute(v, 'fsdp', [(i, i ^ e) for i in range(n_fsdp)])]
    ppermute x2, waiting for transfers between devices: 13.3 us -> 3.22 us  [shards(): placed = [lax.ppermute(p, ('fsdp', 'seq', 'tp'), pairs) for p in placed]]
    all_to_all x1 -> x0, blocking collectives: 6.26 us -> none  [shards(): both = lax.all_to_all(both, 'tp', 0, 0)]
    pallas_call x0 -> x2, Pallas kernels: none -> 4.17 us  [the longest x1 2.19 us: norm(): pl.pallas_call(norm_body, grid_spec=pltpu.PrefetchScalarGridSpec(num_scal...]
    ppermute x2, starting transfers between devices: 6.71 us -> 10.4 us  [shards(): placed = [lax.ppermute(p, ('fsdp', 'seq', 'tp'), pairs) for p in placed]]
    all_gather x2 -> x1, waiting for transfers between devices: 32.1 us -> 31.4 us  [shards(): gathers = [lax.all_gather(part, 'seq', axis=0) for part in gated]]
  transfers between devices with their start and end apart: 18 -> 18, of which waited for: 12 -> 9; matrix products, arithmetic and copies ran while one was open for 1% -> 3% of each run, Pallas kernels for 11% -> 11%
where the time goes in v3:
time: 277 us; the launch traced here: 272 us
  waiting for transfers between devices  147 us (53%)
  Pallas kernels  45.1 us (16%)
  blocking collectives  34.4 us (12%)
  starting transfers between devices  21.3 us (8%)
  between operations  13.6 us (5%)
  local copies, waits for them, and re-layouts  5.71 us (2%)
  other arithmetic  5.05 us (2%)
    reduce_scatter x1, waiting for transfers between devices, shards(): got_second = lax.psum_scatter(second, 'seq', scatter_dimension=0)  87.3 us
    all_gather x1, waiting for transfers between devices, shards(): gathers = [lax.all_gather(part, 'seq', axis=0) for part in gated]  31.4 us
    ppermute x9, waiting for transfers between devices, swap_chip(): return lax.ppermute(v, 'fsdp', [(i, i ^ e) for i in range(n_fsdp)])  24.4 us
    pallas_call x2, Pallas kernels, in_proj(): pl.pallas_call(in_proj_body, grid=(3, chan // tile), in_specs=[pl.BlockSp...  21.6 us
    all_gather x1, blocking collectives, shards(): gathers = [lax.all_gather(part, 'seq', axis=0) for part in gated]  17.4 us
    all_to_all x1, blocking collectives, shards(): own = lax.all_to_all(split, 'seq', 0, 0).reshape(n_seq * rows, depth)  17 us
    pallas_call x4, Pallas kernels, out_proj(): pl.pallas_call(out_proj_body, grid_spec=pltpu.PrefetchScalarGridSpec(num_...  11.1 us
    ppermute x9, starting transfers between devices, swap_chip(): return lax.ppermute(v, 'fsdp', [(i, i ^ e) for i in range(n_fsdp)])  10.6 us
  transfers between devices with their start and end apart: 18, of which 9 were waited for; matrix products, arithmetic and copies ran while one was open for 3% of the time, Pallas kernels for 11%

profile of v3, /device:TPU:18, one launch (start us, length us, event | category | flops | bytes accessed | tf_op | source)
XLA Modules:
  0.0 271.8 jit_solution(14873342824123566603)
XLA Ops:
  6.5 2.2 shard_map.73
  8.7 17.0 %all_to_all.5 = bf16[4,32,2048]{2,1,0:T(8,128)(2,1)S(1)} all-to-all(bf16[4,32,2048]{2,1,0:T(8,128)(2,1)} %shard_map.73), channel_id=1, replica_groups=mesh['fsdp'=4,'seq'=4,'tp'=2] {'seq'}, dimensions={0} | all-to-all | bytes 1048576 | tf_op jit(solution)/shard_map/all_to_all | solution.py:268
  25.7 0.5 collective-permute-start.1
  26.3 1.5 collective-permute-start.2
  27.8 1.4 collective-permute-start.3
  29.2 0.1 pad_maximum_fusion.2
  29.3 8.1 %shard_map.74 = bf16[4,2,3,128,256]{4,3,2,1,0:T(8,128)(2,1)} custom-call(bf16[256,2048]{1,0:T(8,128)(2,1)S(1)} %bitcast.63, bf16[3,2048,1024]{2,1,0:T(8,128)(2,1)} %w_ref.7), custom_call_target="tpu_custom_call" | custom-call | flops 3221225472 | bytes 15204352 | tf_op jit(solution)/shard_map/pallas_call | solution.py:62
  37.5 3.0 %collective-permute-done.1 = bf16[128,2048]{1,0:T(8,128)(2,1)S(1)} collective-permute-done((bf16[128,2048]{1,0:T(8,128)(2,1)S(1)}, bf16[128,2048]{1,0:T(8,128)(2,1)S(1)}, u32[]{:S(2)}, u32[]{:S(2)}) %collective-permute-start.1) | collective-permute-done | bytes 524320 | tf_op jit(solution)/shard_map/ppermute | solution.py:257
  40.4 10.2 %collective-permute-done.2 = bf16[128,2048]{1,0:T(8,128)(2,1)S(1)} collective-permute-done((bf16[128,2048]{1,0:T(8,128)(2,1)S(1)}, bf16[128,2048]{1,0:T(8,128)(2,1)S(1)}, u32[]{:S(2)}, u32[]{:S(2)}) %collective-permute-start.2) | collective-permute-done | bytes 524320 | tf_op jit(solution)/shard_map/ppermute | solution.py:257
  50.6 1.6 collective-permute-done.3
  52.2 0.2 pad_maximum_fusion.1
  52.5 0.7 constant_dynamic-slice_fusion.1
  53.4 0.7 maximum_bitcast_fusion.taps_ref
  54.1 2.0 shard_map.75.toep_ref
  56.0 1.6 pad_maximum_fusion
  57.6 13.5 %shard_map.76 = bf16[4,6,3,128,256]{4,3,2,1,0:T(8,128)(2,1)} custom-call(bf16[768,2048]{1,0:T(8,128)(2,1)S(1)} %bitcast.64, bf16[3,2048,1024]{2,1,0:T(8,128)(2,1)} %w_ref.7), custom_call_target="tpu_custom_call" | custom-call | flops 9663676416 | bytes 20447232 | tf_op jit(solution)/shard_map/pallas_call | solution.py:62
  71.2 0.6 copy-done.4
  71.8 0.5 convert_reduce_fusion
  72.3 1.0 copy.14.pos_ref
  73.4 0.6 copy.15.short_ref
  74.0 87.3 %reduce-scatter.5.cloned.1.call-done = bf16[1,6,3,128,256]{4,3,2,1,0:T(8,128)(2,1)} async-done(((bf16[4,6,3,128,256]{4,3,2,1,0:T(8,128)(2,1)}), bf16[1,6,3,128,256]{4,3,2,1,0:T(8,128)(2,1)}) %reduce-scatter.5.cloned.1.call-update) | async-done | bytes 1179664 | tf_op jit(solution)/shard_map/reduce_scatter | solution.py:278
  161.2 8.3 %shard_map.77 = (bf16[4,160,256]{2,1,0:T(8,128)(2,1)}, bf16[4,96,256]{2,1,0:T(8,128)(2,1)}) custom-call(s32[1]{0:T(128)} %bitcast.at_ref.base_ref, bf16[2,3,128,256]{3,2,1,0:T(8,128)(2,1)} %bitcast.84, bf16[6,3,128,256]{3,2,1,0:T(8,128)(2,1)} %bitcast.83, s32[1024,1]{1,0:T(8,128)} %copy.14.pos_ref, f32[7,3,256]{2,1,0:T(4,128)} %copy.15.short_ref, ...), custom_call_target="tpu_custom_call" | custom-call | flops 1073741824 | bytes 2097152 | tf_op jit(solution)/shard_map/pallas_call | solution.py:171
  169.8 0.1 stack.91.place_ref
  170.0 31.4 %all-gather.4.cloned.1.call-done = bf16[16,160,256]{2,1,0:T(8,128)(2,1)} async-done(((bf16[4,160,256]{2,1,0:T(8,128)(2,1)}), bf16[16,160,256]{2,1,0:T(8,128)(2,1)}) %all-gather.4.cloned.1.call-update) | async-done | bytes 1310736 | tf_op jit(solution)/shard_map/all_gather | solution.py:311
  201.4 1.3 copy-done.2
  202.7 3.6 %shard_map.79 = bf16[4,160,1024]{2,1,0:T(8,128)(2,1)S(1)} custom-call(s32[9]{0:T(128)S(1)} %stack.91.place_ref, bf16[4,640,256]{2,1,0:T(8,128)(2,1)S(1)} %bitcast.67, bf16[1024,2048]{1,0:T(8,128)(2,1)} %w_ref.11), custom_call_target="tpu_custom_call" | custom-call | flops 21474836480 | bytes 4718592 | tf_op jit(solution)/shard_map/pallas_call | solution.py:221
  206.4 3.6 %shard_map.78 = bf16[4,160,1024]{2,1,0:T(8,128)(2,1)S(1)} custom-call(s32[9]{0:T(128)S(1)} %stack.85.place_ref, bf16[4,640,256]{2,1,0:T(8,128)(2,1)S(1)} %bitcast.68, bf16[1024,2048]{1,0:T(8,128)(2,1)} %w_ref.11), custom_call_target="tpu_custom_call" | custom-call | flops 21474836480 | bytes 4718592 | tf_op jit(solution)/shard_map/pallas_call | solution.py:221
  210.0 0.4 fusion.7
  210.4 1.5 collective-permute-start.8
  211.9 0.6 collective-permute-start.7
  212.5 1.5 collective-permute-start.6
  213.9 17.4 %all-gather = bf16[16,96,256]{2,1,0:T(8,128)(2,1)S(1)} all-gather(bf16[4,96,256]{2,1,0:T(8,128)(2,1)S(1)} %copy-done.3), channel_id=2, replica_groups=mesh['fsdp'=4,'seq'=4,'tp'=2] {'seq'}, dimensions={0}, use_global_device_ids=true | all-gather | bytes 983040 | tf_op jit(solution)/shard_map/all_gather | solution.py:311
  231.4 0.3 fusion.3
  231.7 2.0 shard_map.81
  233.7 2.0 shard_map.80
  235.7 0.3 collective-permute-done.10
  236.0 0.2 fusion.10
  236.2 1.5 collective-permute-start.13
  237.8 0.5 collective-permute-start.12
  238.3 1.5 collective-permute-start.11
  239.8 4.4 %collective-permute-start.9 = (bf16[160,1024]{1,0:T(8,128)(2,1)S(1)}, bf16[160,1024]{1,0:T(8,128)(2,1)S(1)}, u32[]{:S(2)}, u32[]{:S(2)}) collective-permute-start(bf16[160,1024]{1,0:T(8,128)(2,1)S(1)} %fusion.3), channel_id=1, source_target_pairs={{0,0},{1,1},{8,2},{9,3},{16,4},{17,5},{24,6},{25,7},{2,10},{3,11},... | collective-permute-start | bytes 983048 | tf_op jit(solution)/shard_map/ppermute | solution.py:326
  244.2 1.0 collective-permute-done.13
  245.2 8.6 %collective-permute-done.12 = bf16[96,1024]{1,0:T(8,128)(2,1)S(1)} collective-permute-done((bf16[96,1024]{1,0:T(8,128)(2,1)S(1)}, bf16[96,1024]{1,0:T(8,128)(2,1)S(1)}, u32[]{:S(2)}, u32[]{:S(2)}) %collective-permute-start.12) | collective-permute-done | bytes 196640 | tf_op jit(solution)/shard_map/ppermute | solution.py:257
  253.8 0.2 fusion.6
  254.0 6.0 %collective-permute-start.14 = (bf16[96,1024]{1,0:T(8,128)(2,1)S(1)}, bf16[96,1024]{1,0:T(8,128)(2,1)S(1)}, u32[]{:S(2)}, u32[]{:S(2)}) collective-permute-start(bf16[96,1024]{1,0:T(8,128)(2,1)S(1)} %fusion.6), channel_id=1, source_target_pairs={{0,0},{1,1},{8,2},{9,3},{16,4},{17,5},{24,6},{25,7},{2,10},{3,11},... | collective-permute-start | bytes 589832 | tf_op jit(solution)/shard_map/ppermute | solution.py:326
  260.0 1.1 constant_dynamic-slice_fusion.2
  261.1 3.2 %collective-permute-done.14 = bf16[96,1024]{1,0:T(8,128)(2,1)S(1)} collective-permute-done((bf16[96,1024]{1,0:T(8,128)(2,1)S(1)}, bf16[96,1024]{1,0:T(8,128)(2,1)S(1)}, u32[]{:S(2)}, u32[]{:S(2)}) %collective-permute-start.14) | collective-permute-done | bytes 196640 | tf_op jit(solution)/shard_map/ppermute | solution.py:326
  264.3 1.0 add_convert_fusion
  (33 shorter events, 0.6 us)
Async XLA Ops:
  6.5 66.8 %copy-start = (f32[7,3,1024]{2,0,1:T(8,128)S(1)}, f32[7,3,1024]{2,0,1:T(8,128)}, u32[]{:S(2)}) copy-start(f32[7,3,1024]{2,0,1:T(8,128)} %param.10) | copy-start | bytes 258052
  6.5 67.4 %reduce-scatter.3.cloned.1.call-start = ((), (), s32[]{:S(2)}) async-start(), calls=%async_computation.3 | async-start | bytes 1966080 | tf_op jit(solution)/shard_map/reduce_scatter | solution.py:272
  25.7 3.5 %collective-permute-start = (bf16[128,2048]{1,0:T(8,128)(2,1)S(1)}, bf16[128,2048]{1,0:T(8,128)(2,1)S(1)}, u32[]{:S(2)}, u32[]{:S(2)}) collective-permute-start(bf16[128,2048]{1,0:T(8,128)(2,1)S(1)} %bitcast.75), channel_id=1, source_target_pairs={{0,1},{1,0},{2,3},{3,2},{4,5},{5,4},{6,7},{7,6},{8,9},{9,8},{10,11... | collective-permute-start | bytes 1572872 | tf_op jit(solution)/shard_map/ppermute | solution.py:254
  25.7 14.7 %collective-permute-start.1 = (bf16[128,2048]{1,0:T(8,128)(2,1)S(1)}, bf16[128,2048]{1,0:T(8,128)(2,1)S(1)}, u32[]{:S(2)}, u32[]{:S(2)}) collective-permute-start(bf16[128,2048]{1,0:T(8,128)(2,1)S(1)} %bitcast.76), channel_id=1, source_target_pairs={{0,8},{8,0},{16,24},{24,16},{1,9},{9,1},{17,25},{25,17},{2,10},{10... | collective-permute-start | bytes 1572872 | tf_op jit(solution)/shard_map/ppermute | solution.py:257
  26.3 24.4 %collective-permute-start.2 = (bf16[128,2048]{1,0:T(8,128)(2,1)S(1)}, bf16[128,2048]{1,0:T(8,128)(2,1)S(1)}, u32[]{:S(2)}, u32[]{:S(2)}) collective-permute-start(bf16[128,2048]{1,0:T(8,128)(2,1)S(1)} %bitcast.77), channel_id=1, source_target_pairs={{0,16},{8,24},{16,0},{24,8},{1,17},{9,25},{17,1},{25,9},{2,18},{10... | collective-permute-start | bytes 1572872 | tf_op jit(solution)/shard_map/ppermute | solution.py:257
  27.8 24.5 %collective-permute-start.3 = (bf16[128,2048]{1,0:T(8,128)(2,1)S(1)}, bf16[128,2048]{1,0:T(8,128)(2,1)S(1)}, u32[]{:S(2)}, u32[]{:S(2)}) collective-permute-start(bf16[128,2048]{1,0:T(8,128)(2,1)S(1)} %bitcast.78), channel_id=1, source_target_pairs={{0,24},{8,16},{16,8},{24,0},{1,25},{9,17},{17,9},{25,1},{2,26},{10... | collective-permute-start | bytes 1572872 | tf_op jit(solution)/shard_map/ppermute | solution.py:257
  37.4 123.8 %reduce-scatter.5.cloned.1.call-start = ((), (), s32[]{:S(2)}) async-start(), calls=%async_computation.4 | async-start | bytes 5898240 | tf_op jit(solution)/shard_map/reduce_scatter | solution.py:278
  52.4 3.6 %collective-permute-start.4 = (bf16[3,128,2048]{2,1,0:T(8,128)(2,1)S(1)}, bf16[3,128,2048]{2,1,0:T(8,128)(2,1)}, u32[]{:S(2)}, u32[]{:S(2)}) collective-permute-start(bf16[3,128,2048]{2,1,0:T(8,128)(2,1)S(1)} %pad_maximum_fusion.1), channel_id=1, source_target_pairs={{0,1},{1,0},{2,3},{3,2},{4,5},{5,4},{6,7},{7,6},{8,9},{9,8},{10,11... | collective-permute-start | bytes 4718600 | tf_op jit(solution)/shard_map/ppermute | solution.py:254
  71.1 0.7 copy-start.4
  71.1 130.2 %all-gather.4.cloned.1.call-start = ((), (), s32[]{:S(2)}) async-start(), calls=%async_computation.5 | async-start | bytes 1638400 | tf_op jit(solution)/shard_map/all_gather | solution.py:311
  201.4 1.3 copy-start.2
  206.3 7.7 %copy-start.3 = (bf16[4,96,256]{2,1,0:T(8,128)(2,1)S(1)}, bf16[4,96,256]{2,1,0:T(8,128)(2,1)}, u32[]{:S(2)}) copy-start(bf16[4,96,256]{2,1,0:T(8,128)(2,1)} %get-tuple-element.19) | copy-start | bytes 589828
  206.3 3.7 %collective-permute-start.5 = (bf16[4,160,1024]{2,1,0:T(8,128)(2,1)S(1)}, bf16[4,160,1024]{2,1,0:T(8,128)(2,1)S(1)}, u32[]{:S(2)}, u32[]{:S(2)}) collective-permute-start(bf16[4,160,1024]{2,1,0:T(8,128)(2,1)S(1)} %shard_map.79), channel_id=1, source_target_pairs={{0,1},{1,0},{2,3},{3,2},{4,5},{5,4},{6,7},{7,6},{8,9},{9,8},{10,11... | collective-permute-start | bytes 3932168 | tf_op jit(solution)/shard_map/ppermute | solution.py:254
  210.0 21.7 %copy-start.1 = (bf16[1024,2048]{1,0:T(8,128)(2,1)S(1)}, bf16[1024,2048]{1,0:T(8,128)(2,1)}, u32[]{:S(2)}) copy-start(bf16[1024,2048]{1,0:T(8,128)(2,1)} %w_ref.11) | copy-start | bytes 12582916
  210.4 21.0 %collective-permute-start.8 = (bf16[160,1024]{1,0:T(8,128)(2,1)S(1)}, bf16[160,1024]{1,0:T(8,128)(2,1)S(1)}, u32[]{:S(2)}, u32[]{:S(2)}) collective-permute-start(bf16[160,1024]{1,0:T(8,128)(2,1)S(1)} %get-tuple-element.24), channel_id=1, source_target_pairs={{0,24},{8,16},{16,8},{24,0},{1,25},{9,17},{17,9},{25,1},{2,26},{10... | collective-permute-start | bytes 983048 | tf_op jit(solution)/shard_map/ppermute | solution.py:257
  211.9 19.5 %collective-permute-start.7 = (bf16[160,1024]{1,0:T(8,128)(2,1)S(1)}, bf16[160,1024]{1,0:T(8,128)(2,1)S(1)}, u32[]{:S(2)}, u32[]{:S(2)}) collective-permute-start(bf16[160,1024]{1,0:T(8,128)(2,1)S(1)} %get-tuple-element.25), channel_id=1, source_target_pairs={{0,16},{8,24},{16,0},{24,8},{1,17},{9,25},{17,1},{25,9},{2,18},{10... | collective-permute-start | bytes 983048 | tf_op jit(solution)/shard_map/ppermute | solution.py:257
  212.5 18.9 %collective-permute-start.6 = (bf16[160,1024]{1,0:T(8,128)(2,1)S(1)}, bf16[160,1024]{1,0:T(8,128)(2,1)S(1)}, u32[]{:S(2)}, u32[]{:S(2)}) collective-permute-start(bf16[160,1024]{1,0:T(8,128)(2,1)S(1)} %get-tuple-element.23), channel_id=1, source_target_pairs={{0,8},{8,0},{16,24},{24,16},{1,9},{9,1},{17,25},{25,17},{2,10},{10... | collective-permute-start | bytes 983048 | tf_op jit(solution)/shard_map/ppermute | solution.py:257
  233.7 2.4 collective-permute-start.10
  236.2 9.0 %collective-permute-start.13 = (bf16[96,1024]{1,0:T(8,128)(2,1)S(1)}, bf16[96,1024]{1,0:T(8,128)(2,1)S(1)}, u32[]{:S(2)}, u32[]{:S(2)}) collective-permute-start(bf16[96,1024]{1,0:T(8,128)(2,1)S(1)} %get-tuple-element.27), channel_id=1, source_target_pairs={{0,24},{8,16},{16,8},{24,0},{1,25},{9,17},{17,9},{25,1},{2,26},{10... | collective-permute-start | bytes 589832 | tf_op jit(solution)/shard_map/ppermute | solution.py:257
  237.8 16.0 %collective-permute-start.12 = (bf16[96,1024]{1,0:T(8,128)(2,1)S(1)}, bf16[96,1024]{1,0:T(8,128)(2,1)S(1)}, u32[]{:S(2)}, u32[]{:S(2)}) collective-permute-start(bf16[96,1024]{1,0:T(8,128)(2,1)S(1)} %get-tuple-element.28), channel_id=1, source_target_pairs={{0,16},{8,24},{16,0},{24,8},{1,17},{9,25},{17,1},{25,9},{2,18},{10... | collective-permute-start | bytes 589832 | tf_op jit(solution)/shard_map/ppermute | solution.py:257
  238.3 15.5 %collective-permute-start.11 = (bf16[96,1024]{1,0:T(8,128)(2,1)S(1)}, bf16[96,1024]{1,0:T(8,128)(2,1)S(1)}, u32[]{:S(2)}, u32[]{:S(2)}) collective-permute-start(bf16[96,1024]{1,0:T(8,128)(2,1)S(1)} %get-tuple-element.26), channel_id=1, source_target_pairs={{0,8},{8,0},{16,24},{24,16},{1,9},{9,1},{17,25},{25,17},{2,10},{10... | collective-permute-start | bytes 589832 | tf_op jit(solution)/shard_map/ppermute | solution.py:257
  239.8 21.3 %collective-permute-start.9 = (bf16[160,1024]{1,0:T(8,128)(2,1)S(1)}, bf16[160,1024]{1,0:T(8,128)(2,1)S(1)}, u32[]{:S(2)}, u32[]{:S(2)}) collective-permute-start(bf16[160,1024]{1,0:T(8,128)(2,1)S(1)} %fusion.3), channel_id=1, source_target_pairs={{0,0},{1,1},{8,2},{9,3},{16,4},{17,5},{24,6},{25,7},{2,10},{3,11},... | collective-permute-start | bytes 983048 | tf_op jit(solution)/shard_map/ppermute | solution.py:326
  254.0 10.3 %collective-permute-start.14 = (bf16[96,1024]{1,0:T(8,128)(2,1)S(1)}, bf16[96,1024]{1,0:T(8,128)(2,1)S(1)}, u32[]{:S(2)}, u32[]{:S(2)}) collective-permute-start(bf16[96,1024]{1,0:T(8,128)(2,1)S(1)} %fusion.6), channel_id=1, source_target_pairs={{0,0},{1,1},{8,2},{9,3},{16,4},{17,5},{24,6},{25,7},{2,10},{3,11},... | collective-permute-start | bytes 589832 | tf_op jit(solution)/shard_map/ppermute | solution.py:326
Sparse Core Ops, SparseCore 0:
  37.5 35.5 reduce-scatter.2
  75.4 85.7 reduce-scatter.4
  169.6 31.6 all-gather.3

commit v4 on v3

--- a/solution.py
+++ b/solution.py
@@ -7,7 +7,7 @@
 from jax.sharding import PartitionSpec as P
 
 GROUP = 16
-SPLIT = 160
+SPLIT = 80
 KS = 7
 KL = 128
 BF = jnp.bfloat16
@@ -15,17 +15,21 @@
 MIB = 1024 * 1024
 
 
-def norm_body(at_ref, t_ref, gain_ref, o_ref):
+def norm_body(at_ref, t_ref, gain_ref, *refs):
+    outs, held = refs[:-1], refs[-1]
     wide = t_ref[...].astype(F32)
     squares = jnp.mean(wide * wide, axis=1, keepdims=True)
     normed = (wide * lax.rsqrt(squares + 1e-06) * gain_ref[...]).astype(BF)
-    parts, _, depth = o_ref.shape
-    for p in range(parts):
-        o_ref[p] = normed[:, p * depth : (p + 1) * depth]
+    depth = held.shape[2]
+    for p in range(held.shape[0]):
+        held[p] = normed[:, p * depth : (p + 1) * depth]
+    for e, o in enumerate(outs):
+        o[...] = held[lax.bitwise_xor(at_ref[1], e)]
 
 
 def norm(tokens, gain, at, rows, parts):
     width = tokens.shape[1]
+    depth = width // parts
     return pl.pallas_call(
         norm_body,
         grid_spec=pltpu.PrefetchScalarGridSpec(
@@ -35,46 +39,56 @@
                 pl.BlockSpec((rows, width), lambda i, s: (s[0], 0)),
                 pl.BlockSpec((1, width), lambda i, s: (0, 0)),
             ],
-            out_specs=pl.BlockSpec((parts, rows, width // parts), lambda i, s: (0, 0, 0)),
-        ),
-        out_shape=jax.ShapeDtypeStruct((parts, rows, width // parts), BF),
+            out_specs=[pl.BlockSpec((rows, depth), lambda i, s: (0, 0))] * parts,
+            scratch_shapes=[pltpu.VMEM((parts, rows, depth), BF)],
+        ),
+        out_shape=[jax.ShapeDtypeStruct((rows, depth), BF)] * parts,
         compiler_params=pltpu.CompilerParams(vmem_limit_bytes=62 * MIB),
     )(at, tokens, gain.reshape(1, width))
 
 
-def in_proj_body(x_ref, w_ref, o_ref):
-    parts, pieces, rows, width = o_ref.shape[0], o_ref.shape[1], o_ref.shape[3], o_ref.shape[4]
+def in_proj_body(at_ref, x_ref, w_ref, o_ref, *, parts):
+    each, pieces, rows, width = o_ref.shape[0], o_ref.shape[1], o_ref.shape[3], o_ref.shape[4]
     made = jnp.dot(x_ref[...], w_ref[0], preferred_element_type=F32).astype(BF)
-    for p in range(parts):
+    part = rows // parts
+    for e in range(parts):
+        place = pl.ds(pl.multiple_of(lax.bitwise_xor(at_ref[0], e) * part, part), part)
         for i in range(pieces):
-            o_ref[p, i, 0] = made[i * rows : (i + 1) * rows, p * width : (p + 1) * width]
-
-
-def in_proj(x, w, parts, weight=1):
+            begin = i * rows + e * part
+            for p in range(each):
+                o_ref[p, i, 0, place, :] = made[begin : begin + part, p * width : (p + 1) * width]
+
+
+def in_proj(x, w, parts, at):
     pieces, rows, depth = x.shape
     chan = w.shape[2]
     width = chan // parts
     if width % 128:
         y = jnp.einsum("ird,kdpc->pikrc", x, w.reshape(3, depth, parts, width), preferred_element_type=F32)
-        return y.astype(BF)
+        y = y.astype(BF).reshape(parts, pieces, 3, parts, rows // parts, width)
+        order = lax.bitwise_xor(jnp.arange(parts, dtype=jnp.int32), at)
+        return jnp.take(y, order, axis=3).reshape(parts, pieces, 3, rows, width)
     tile = chan if pieces * rows <= 256 else max(width, chan // 2)
     each = tile // width
     return pl.pallas_call(
-        in_proj_body,
-        grid=(3, chan // tile),
-        in_specs=[
-            pl.BlockSpec((pieces * rows, depth), lambda k, p: (0, 0)),
-            pl.BlockSpec((1, depth, tile), lambda k, p: (k, 0, p)),
-        ],
-        out_specs=pl.BlockSpec((each, pieces, 1, rows, width), lambda k, p: (p, 0, k, 0, 0)),
+        functools.partial(in_proj_body, parts=parts),
+        grid_spec=pltpu.PrefetchScalarGridSpec(
+            num_scalar_prefetch=1,
+            grid=(3, chan // tile),
+            in_specs=[
+                pl.BlockSpec((pieces * rows, depth), lambda k, p, s: (0, 0)),
+                pl.BlockSpec((1, depth, tile), lambda k, p, s: (k, 0, p)),
+            ],
+            out_specs=pl.BlockSpec((each, pieces, 1, rows, width), lambda k, p, s: (p, 0, k, 0, 0)),
+        ),
         out_shape=jax.ShapeDtypeStruct((parts, pieces, 3, rows, width), BF),
         compiler_params=pltpu.CompilerParams(vmem_limit_bytes=48 * MIB),
         cost_estimate=pl.CostEstimate(
-            flops=2 * pieces * rows * depth * 3 * chan * weight,
+            flops=2 * pieces * rows * depth * 3 * chan,
             bytes_accessed=2 * (3 * depth * chan + pieces * rows * (depth + 3 * chan)),
             transcendentals=0,
         ),
-    )(x.reshape(pieces * rows, depth), w)
+    )(at.reshape(1), x.reshape(pieces * rows, depth), w)
 
 
 def toeplitz_body(taps_ref, o_ref):
@@ -264,17 +278,20 @@
     ).T
     tiles = chan // 128 if chan % 128 == 0 else 1
     matrices = toeplitz(taps.reshape(tiles, groups // tiles, 2 * KL))
-    split = norm(tokens, norm_gain, q.astype(jnp.int32).reshape(1), rows, n_seq)
-    own = lax.all_to_all(split, "seq", 0, 0).reshape(n_seq * rows, depth)
+    def swap_shard(v, e):
+        return lax.ppermute(v, "seq", [(i, i ^ e) for i in range(n_seq)])
+
+    split = norm(tokens, norm_gain, jnp.stack([q, z]).astype(jnp.int32), rows, n_seq)
+    own = jnp.concatenate([split[0]] + [swap_shard(split[e], e) for e in range(1, n_seq)])
     near = swap_core(own)
     far = [swap_chip(own, e) for e in range(1, n_fsdp)]
-    first = in_proj(jnp.stack([own, near]), in_weight, n_seq)
+    first = in_proj(jnp.stack([own, near]), in_weight, n_seq, z)
     got_first = lax.psum_scatter(first, "seq", scatter_dimension=0)
     far, first = lax.optimization_barrier((far, first))
     far = jnp.stack(far)
     both = jnp.concatenate([far, swap_core(far)])
     both, matrices = lax.optimization_barrier((both, matrices))
-    second = in_proj(both, in_weight, n_seq, 1)
+    second = in_proj(both, in_weight, n_seq, z)
     got_second = lax.psum_scatter(second, "seq", scatter_dimension=0)
 
     at = jnp.arange(seq_len, dtype=jnp.int32)

time: 277 us -> 272 us (0.982); the launches traced: 272 us -> 271 us
  blocking collectives: 34.4 us -> 20.2 us
  waiting for transfers between devices: 147 us -> 155 us
  local copies, waits for them, and re-layouts: 5.71 us -> 8.65 us
    all_gather x1, waiting for transfers between devices: 31.4 us -> 0.6 us  [shards(): gathers = [lax.all_gather(part, 'seq', axis=0) for part in gated]]
    all_to_all x1 -> x0, blocking collectives: 17 us -> none  [shards(): own = lax.all_to_all(split, 'seq', 0, 0).reshape(n_seq * rows, depth)]
    ppermute x2, waiting for transfers between devices: 3.22 us -> 19.9 us  [shards(): placed = [lax.ppermute(p, ('fsdp', 'seq', 'tp'), pairs) for p in placed]]
    ppermute x9, waiting for transfers between devices: 24.4 us -> 38 us  [swap_chip(): return lax.ppermute(v, 'fsdp', [(i, i ^ e) for i in range(n_fsdp)])]
    ppermute x0 -> x3, waiting for transfers between devices: none -> 10.7 us  [swap_shard(): return lax.ppermute(v, 'seq', [(i, i ^ e) for i in range(n_seq)])]
    ppermute x2, starting transfers between devices: 10.4 us -> 6.88 us  [shards(): placed = [lax.ppermute(p, ('fsdp', 'seq', 'tp'), pairs) for p in placed]]
    ppermute x0 -> x3, starting transfers between devices: none -> 3.49 us  [swap_shard(): return lax.ppermute(v, 'seq', [(i, i ^ e) for i in range(n_seq)])]
    unnamed x11 -> x12, local copies, waits for them, and re-layouts: 2.56 us -> 5.5 us
  transfers between devices with their start and end apart: 18 -> 21, of which waited for: 9 -> 15; matrix products, arithmetic and copies ran while one was open for 3% -> 3% of each run, Pallas kernels for 11% -> 11%
where the time goes in v4:
time: 272 us; the launch traced here: 271 us
  waiting for transfers between devices  155 us (57%)
  Pallas kernels  45.9 us (17%)
  starting transfers between devices  21.4 us (8%)
  blocking collectives  20.2 us (7%)
  between operations  13.5 us (5%)
  local copies, waits for them, and re-layouts  8.65 us (3%)
  other arithmetic  5.68 us (2%)
    reduce_scatter x1, waiting for transfers between devices, shards(): got_second = lax.psum_scatter(second, 'seq', scatter_dimension=0)  85.8 us
    ppermute x9, waiting for transfers between devices, swap_chip(): return lax.ppermute(v, 'fsdp', [(i, i ^ e) for i in range(n_fsdp)])  38 us
    pallas_call x2, Pallas kernels, in_proj(): pl.pallas_call(functools.partial(in_proj_body, parts=parts), grid_spec=pl...  21.7 us
    all_gather x1, blocking collectives, shards(): gathers = [lax.all_gather(part, 'seq', axis=0) for part in gated]  20.2 us
    ppermute x2, waiting for transfers between devices, shards(): placed = [lax.ppermute(p, ('fsdp', 'seq', 'tp'), pairs) for p in placed]  19.9 us
    pallas_call x4, Pallas kernels, out_proj(): pl.pallas_call(out_proj_body, grid_spec=pltpu.PrefetchScalarGridSpec(num_...  11.1 us
    ppermute x3, waiting for transfers between devices, swap_shard(): return lax.ppermute(v, 'seq', [(i, i ^ e) for i in range(n_seq)])  10.7 us
    ppermute x9, starting transfers between devices, swap_chip(): return lax.ppermute(v, 'fsdp', [(i, i ^ e) for i in range(n_fsdp)])  10.7 us
  transfers between devices with their start and end apart: 21, of which 15 were waited for; matrix products, arithmetic and copies ran while one was open for 3% of the time, Pallas kernels for 11%

profile of v4, /device:TPU:18, one launch (start us, length us, event | category | flops | bytes accessed | tf_op | source)
XLA Modules:
  0.0 270.7 jit_solution(11418583827245155084)
XLA Ops:
  6.5 0.6 pad_add_fusion.at_ref
  7.2 2.8 %shard_map.73 = (bf16[32,2048]{1,0:T(8,128)(2,1)}, bf16[32,2048]{1,0:T(8,128)(2,1)}, bf16[32,2048]{1,0:T(8,128)(2,1)}, bf16[32,2048]{1,0:T(8,128)(2,1)}) custom-call(s32[2]{0:T(128)} %pad_add_fusion.at_ref, bf16[256,8192]{1,0:T(8,128)(2,1)} %t_ref.1, f32[1,8192]{1,0:T(1,128)} %bitcast.77), custom_call_target="tpu_custom_call" | custom-call | tf_op jit(solution)/shard_map/pallas_call | solution.py:33
  10.0 1.6 collective-permute-start
  11.9 1.6 collective-permute-start.2
  13.5 0.9 constant_dynamic-update-slice_fusion.3
  14.4 2.2 collective-permute-done
  16.6 5.2 %collective-permute-done.1 = bf16[32,2048]{1,0:T(8,128)(2,1)S(1)} collective-permute-done((bf16[32,2048]{1,0:T(8,128)(2,1)}, bf16[32,2048]{1,0:T(8,128)(2,1)S(1)}, u32[]{:S(2)}, u32[]{:S(2)}) %collective-permute-start.1) | collective-permute-done | bytes 131104 | tf_op jit(solution)/shard_map/ppermute | solution.py:282
  21.8 3.3 %collective-permute-done.2 = bf16[32,2048]{1,0:T(8,128)(2,1)S(1)} collective-permute-done((bf16[32,2048]{1,0:T(8,128)(2,1)}, bf16[32,2048]{1,0:T(8,128)(2,1)S(1)}, u32[]{:S(2)}, u32[]{:S(2)}) %collective-permute-start.2) | collective-permute-done | bytes 131104 | tf_op jit(solution)/shard_map/ppermute | solution.py:282
  25.2 0.6 collective-permute-start.4
  25.8 1.5 collective-permute-start.5
  27.3 1.4 collective-permute-start.6
  28.9 8.1 %shard_map.74 = bf16[4,2,3,128,256]{4,3,2,1,0:T(8,128)(2,1)} custom-call(s32[1]{0:T(128)} %bitcast.1.at_ref, bf16[256,2048]{1,0:T(8,128)(2,1)S(1)} %bitcast.63, bf16[3,2048,1024]{2,1,0:T(8,128)(2,1)} %w_ref.7), custom_call_target="tpu_custom_call" | custom-call | flops 3221225472 | bytes 15204352 | tf_op jit(solution)/shard_map/pallas_call | solution.py:73
  37.1 2.9 %collective-permute-done.4 = bf16[128,2048]{1,0:T(8,128)(2,1)S(1)} collective-permute-done((bf16[128,2048]{1,0:T(8,128)(2,1)S(1)}, bf16[128,2048]{1,0:T(8,128)(2,1)S(1)}, u32[]{:S(2)}, u32[]{:S(2)}) %collective-permute-start.4) | collective-permute-done | bytes 524320 | tf_op jit(solution)/shard_map/ppermute | solution.py:271
  40.0 10.1 %collective-permute-done.5 = bf16[128,2048]{1,0:T(8,128)(2,1)S(1)} collective-permute-done((bf16[128,2048]{1,0:T(8,128)(2,1)S(1)}, bf16[128,2048]{1,0:T(8,128)(2,1)S(1)}, u32[]{:S(2)}, u32[]{:S(2)}) %collective-permute-start.5) | collective-permute-done | bytes 524320 | tf_op jit(solution)/shard_map/ppermute | solution.py:271
  50.1 1.6 collective-permute-done.6
  52.0 0.7 constant_dynamic-slice_fusion.1
  52.9 0.7 maximum_bitcast_fusion.taps_ref
  53.5 2.0 shard_map.75.toep_ref
  55.5 1.6 pad_maximum_fusion
  57.1 13.6 %shard_map.76 = bf16[4,6,3,128,256]{4,3,2,1,0:T(8,128)(2,1)} custom-call(s32[1]{0:T(128)} %bitcast.1.at_ref, bf16[768,2048]{1,0:T(8,128)(2,1)S(1)} %bitcast.64, bf16[3,2048,1024]{2,1,0:T(8,128)(2,1)} %w_ref.7), custom_call_target="tpu_custom_call" | custom-call | flops 9663676416 | bytes 20447232 | tf_op jit(solution)/shard_map/pallas_call | solution.py:73
  71.4 0.5 convert_reduce_fusion
  71.9 1.0 copy.14.pos_ref
  73.0 0.6 copy.15.short_ref
  73.7 85.8 %reduce-scatter.5.cloned.1.call-done = bf16[1,6,3,128,256]{4,3,2,1,0:T(8,128)(2,1)} async-done(((bf16[4,6,3,128,256]{4,3,2,1,0:T(8,128)(2,1)}), bf16[1,6,3,128,256]{4,3,2,1,0:T(8,128)(2,1)}) %reduce-scatter.5.cloned.1.call-update) | async-done | bytes 1179664 | tf_op jit(solution)/shard_map/reduce_scatter | solution.py:295
  159.6 8.3 %shard_map.77 = (bf16[4,80,256]{2,1,0:T(8,128)(2,1)}, bf16[4,176,256]{2,1,0:T(8,128)(2,1)}) custom-call(s32[1]{0:T(128)} %bitcast.base_ref, bf16[2,3,128,256]{3,2,1,0:T(8,128)(2,1)} %bitcast.80, bf16[6,3,128,256]{3,2,1,0:T(8,128)(2,1)} %bitcast.79, s32[1024,1]{1,0:T(8,128)} %copy.14.pos_ref, f32[7,3,256]{2,1,0:T(4,128)} %copy.15.short_ref, ...), custom_call_target="tpu_custom_call" | custom-call | flops 1073741824 | bytes 2097152 | tf_op jit(solution)/shard_map/pallas_call | solution.py:185
  167.8 20.2 %all-gather.1 = bf16[16,80,256]{2,1,0:T(8,128)(2,1)S(1)} all-gather(bf16[4,80,256]{2,1,0:T(8,128)(2,1)} %get-tuple-element.28), channel_id=3, replica_groups=mesh['fsdp'=4,'seq'=4,'tp'=2] {'seq'}, dimensions={0}, use_global_device_ids=true | all-gather | bytes 819200 | tf_op jit(solution)/shard_map/all_gather | solution.py:328
  188.0 2.2 copy-done.1
  190.2 1.8 shard_map.79
  192.2 1.8 shard_map.78
  194.4 1.5 collective-permute-start.11
  196.1 1.8 collective-permute-start.9
  198.0 4.5 %collective-permute-done.11 = bf16[80,1024]{1,0:T(8,128)(2,1)S(1)} collective-permute-done((bf16[80,1024]{1,0:T(8,128)(2,1)S(1)}, bf16[80,1024]{1,0:T(8,128)(2,1)S(1)}, u32[]{:S(2)}, u32[]{:S(2)}) %collective-permute-start.11) | collective-permute-done | bytes 163872 | tf_op jit(solution)/shard_map/ppermute | solution.py:271
  202.5 2.8 %collective-permute-done.10 = bf16[80,1024]{1,0:T(8,128)(2,1)S(1)} collective-permute-done((bf16[80,1024]{1,0:T(8,128)(2,1)S(1)}, bf16[80,1024]{1,0:T(8,128)(2,1)S(1)}, u32[]{:S(2)}, u32[]{:S(2)}) %collective-permute-start.10) | collective-permute-done | bytes 163872 | tf_op jit(solution)/shard_map/ppermute | solution.py:271
  205.5 0.6 all-gather.4.cloned.1.call-done
  206.1 1.4 copy-done.2
  207.5 3.7 %shard_map.81 = bf16[4,176,1024]{2,1,0:T(8,128)(2,1)S(1)} custom-call(s32[9]{0:T(128)S(1)} %stack.101.place_ref, bf16[4,704,256]{2,1,0:T(8,128)(2,1)S(1)} %bitcast.67, bf16[1024,2048]{1,0:T(8,128)(2,1)} %w_ref.11), custom_call_target="tpu_custom_call" | custom-call | flops 23622320128 | bytes 4980736 | tf_op jit(solution)/shard_map/pallas_call | solution.py:235
  211.3 3.7 %shard_map.80 = bf16[4,176,1024]{2,1,0:T(8,128)(2,1)S(1)} custom-call(s32[9]{0:T(128)S(1)} %stack.95.place_ref, bf16[4,704,256]{2,1,0:T(8,128)(2,1)S(1)} %bitcast.68, bf16[1024,2048]{1,0:T(8,128)(2,1)} %w_ref.11), custom_call_target="tpu_custom_call" | custom-call | flops 23622320128 | bytes 4980736 | tf_op jit(solution)/shard_map/pallas_call | solution.py:235
  215.1 0.4 fusion.4
  215.5 1.5 collective-permute-start.16
  217.1 0.4 collective-permute-start.15
  217.5 1.6 collective-permute-start.14
  219.1 8.7 %collective-permute-done.16 = bf16[176,1024]{1,0:T(8,128)(2,1)S(1)} collective-permute-done((bf16[176,1024]{1,0:T(8,128)(2,1)S(1)}, bf16[176,1024]{1,0:T(8,128)(2,1)S(1)}, u32[]{:S(2)}, u32[]{:S(2)}) %collective-permute-start.16) | collective-permute-done | bytes 360480 | tf_op jit(solution)/shard_map/ppermute | solution.py:271
  227.8 7.2 %collective-permute-done.15 = bf16[176,1024]{1,0:T(8,128)(2,1)S(1)} collective-permute-done((bf16[176,1024]{1,0:T(8,128)(2,1)S(1)}, bf16[176,1024]{1,0:T(8,128)(2,1)S(1)}, u32[]{:S(2)}, u32[]{:S(2)}) %collective-permute-start.15) | collective-permute-done | bytes 360480 | tf_op jit(solution)/shard_map/ppermute | solution.py:271
  235.3 4.4 %collective-permute-start.17 = (bf16[176,1024]{1,0:T(8,128)(2,1)S(1)}, bf16[176,1024]{1,0:T(8,128)(2,1)S(1)}, u32[]{:S(2)}, u32[]{:S(2)}) collective-permute-start(bf16[176,1024]{1,0:T(8,128)(2,1)S(1)} %fusion.3), channel_id=1, source_target_pairs={{0,0},{1,1},{8,2},{9,3},{16,4},{17,5},{24,6},{25,7},{2,10},{3,11},... | collective-permute-start | bytes 1081352 | tf_op jit(solution)/shard_map/ppermute | solution.py:343
  239.8 2.4 collective-permute-start.12
  242.2 1.1 constant_dynamic-slice_fusion.2
  243.3 19.9 %collective-permute-done.12 = bf16[80,1024]{1,0:T(8,128)(2,1)S(1)} collective-permute-done((bf16[80,1024]{1,0:T(8,128)(2,1)S(1)}, bf16[80,1024]{1,0:T(8,128)(2,1)S(1)}, u32[]{:S(2)}, u32[]{:S(2)}) %collective-permute-start.12) | collective-permute-done | bytes 163872 | tf_op jit(solution)/shard_map/ppermute | solution.py:343
  263.2 1.0 add_convert_fusion
  (41 shorter events, 3.0 us)
Async XLA Ops:
  6.5 66.4 %copy-start = (f32[7,3,1024]{2,0,1:T(8,128)S(1)}, f32[7,3,1024]{2,0,1:T(8,128)}, u32[]{:S(2)}) copy-start(f32[7,3,1024]{2,0,1:T(8,128)} %param.10) | copy-start | bytes 258052
  6.5 67.2 %reduce-scatter.3.cloned.1.call-start = ((), (), s32[]{:S(2)}) async-start(), calls=%async_computation.2 | async-start | bytes 1966080 | tf_op jit(solution)/shard_map/reduce_scatter | solution.py:289
  10.0 6.6 %collective-permute-start = (bf16[32,2048]{1,0:T(8,128)(2,1)}, bf16[32,2048]{1,0:T(8,128)(2,1)S(1)}, u32[]{:S(2)}, u32[]{:S(2)}) collective-permute-start(bf16[32,2048]{1,0:T(8,128)(2,1)} %get-tuple-element.19), channel_id=1, source_target_pairs={{0,2},{2,0},{4,6},{6,4},{1,3},{3,1},{5,7},{7,5},{8,10},{10,8},{12,... | collective-permute-start | bytes 393224 | tf_op jit(solution)/shard_map/ppermute | solution.py:282
  11.6 10.2 %collective-permute-start.1 = (bf16[32,2048]{1,0:T(8,128)(2,1)}, bf16[32,2048]{1,0:T(8,128)(2,1)S(1)}, u32[]{:S(2)}, u32[]{:S(2)}) collective-permute-start(bf16[32,2048]{1,0:T(8,128)(2,1)} %get-tuple-element.20), channel_id=1, source_target_pairs={{0,4},{2,6},{4,0},{6,2},{1,5},{3,7},{5,1},{7,3},{8,12},{10,14},{12... | collective-permute-start | bytes 393224 | tf_op jit(solution)/shard_map/ppermute | solution.py:282
  11.9 13.2 %collective-permute-start.2 = (bf16[32,2048]{1,0:T(8,128)(2,1)}, bf16[32,2048]{1,0:T(8,128)(2,1)S(1)}, u32[]{:S(2)}, u32[]{:S(2)}) collective-permute-start(bf16[32,2048]{1,0:T(8,128)(2,1)} %get-tuple-element.21), channel_id=1, source_target_pairs={{0,6},{2,4},{4,2},{6,0},{1,7},{3,5},{5,3},{7,1},{8,14},{10,12},{12... | collective-permute-start | bytes 393224 | tf_op jit(solution)/shard_map/ppermute | solution.py:282
  25.1 3.6 %collective-permute-start.3 = (bf16[128,2048]{1,0:T(8,128)(2,1)S(1)}, bf16[128,2048]{1,0:T(8,128)(2,1)S(1)}, u32[]{:S(2)}, u32[]{:S(2)}) collective-permute-start(bf16[128,2048]{1,0:T(8,128)(2,1)S(1)} %constant_dynamic-update-slice_fusion), channel_id=1, source_target_pairs={{0,1},{1,0},{2,3},{3,2},{4,5},{5,4},{6,7},{7,6},{8,9},{9,8},{10,11... | collective-permute-start | bytes 1572872 | tf_op jit(solution)/shard_map/ppermute | solution.py:268
  25.2 14.8 %collective-permute-start.4 = (bf16[128,2048]{1,0:T(8,128)(2,1)S(1)}, bf16[128,2048]{1,0:T(8,128)(2,1)S(1)}, u32[]{:S(2)}, u32[]{:S(2)}) collective-permute-start(bf16[128,2048]{1,0:T(8,128)(2,1)S(1)} %constant_dynamic-update-slice_fusion), channel_id=1, source_target_pairs={{0,8},{8,0},{16,24},{24,16},{1,9},{9,1},{17,25},{25,17},{2,10},{10... | collective-permute-start | bytes 1572872 | tf_op jit(solution)/shard_map/ppermute | solution.py:271
  25.8 24.3 %collective-permute-start.5 = (bf16[128,2048]{1,0:T(8,128)(2,1)S(1)}, bf16[128,2048]{1,0:T(8,128)(2,1)S(1)}, u32[]{:S(2)}, u32[]{:S(2)}) collective-permute-start(bf16[128,2048]{1,0:T(8,128)(2,1)S(1)} %constant_dynamic-update-slice_fusion), channel_id=1, source_target_pairs={{0,16},{8,24},{16,0},{24,8},{1,17},{9,25},{17,1},{25,9},{2,18},{10... | collective-permute-start | bytes 1572872 | tf_op jit(solution)/shard_map/ppermute | solution.py:271
  27.3 24.4 %collective-permute-start.6 = (bf16[128,2048]{1,0:T(8,128)(2,1)S(1)}, bf16[128,2048]{1,0:T(8,128)(2,1)S(1)}, u32[]{:S(2)}, u32[]{:S(2)}) collective-permute-start(bf16[128,2048]{1,0:T(8,128)(2,1)S(1)} %constant_dynamic-update-slice_fusion), channel_id=1, source_target_pairs={{0,24},{8,16},{16,8},{24,0},{1,25},{9,17},{17,9},{25,1},{2,26},{10... | collective-permute-start | bytes 1572872 | tf_op jit(solution)/shard_map/ppermute | solution.py:271
  37.0 122.5 %reduce-scatter.5.cloned.1.call-start = ((), (), s32[]{:S(2)}) async-start(), calls=%async_computation.3 | async-start | bytes 5898240 | tf_op jit(solution)/shard_map/reduce_scatter | solution.py:295
  51.9 3.6 %collective-permute-start.7 = (bf16[3,128,2048]{2,1,0:T(8,128)(2,1)S(1)}, bf16[3,128,2048]{2,1,0:T(8,128)(2,1)}, u32[]{:S(2)}, u32[]{:S(2)}) collective-permute-start(bf16[3,128,2048]{2,1,0:T(8,128)(2,1)S(1)} %pad_maximum_fusion.1), channel_id=1, source_target_pairs={{0,1},{1,0},{2,3},{3,2},{4,5},{5,4},{6,7},{7,6},{8,9},{9,8},{10,11... | collective-permute-start | bytes 4718600 | tf_op jit(solution)/shard_map/ppermute | solution.py:268
  70.7 0.7 copy-start.3
  70.7 135.4 %all-gather.4.cloned.1.call-start = ((), (), s32[]{:S(2)}) async-start(), calls=%async_computation.4 | async-start | bytes 1802240 | tf_op jit(solution)/shard_map/all_gather | solution.py:328
  188.0 2.2 copy-start.1
  192.1 2.2 collective-permute-start.8
  194.4 8.0 %collective-permute-start.11 = (bf16[80,1024]{1,0:T(8,128)(2,1)S(1)}, bf16[80,1024]{1,0:T(8,128)(2,1)S(1)}, u32[]{:S(2)}, u32[]{:S(2)}) collective-permute-start(bf16[80,1024]{1,0:T(8,128)(2,1)S(1)} %get-tuple-element.35), channel_id=1, source_target_pairs={{0,24},{8,16},{16,8},{24,0},{1,25},{9,17},{17,9},{25,1},{2,26},{10... | collective-permute-start | bytes 491528 | tf_op jit(solution)/shard_map/ppermute | solution.py:271
  195.9 9.3 %collective-permute-start.10 = (bf16[80,1024]{1,0:T(8,128)(2,1)S(1)}, bf16[80,1024]{1,0:T(8,128)(2,1)S(1)}, u32[]{:S(2)}, u32[]{:S(2)}) collective-permute-start(bf16[80,1024]{1,0:T(8,128)(2,1)S(1)} %get-tuple-element.36), channel_id=1, source_target_pairs={{0,16},{8,24},{16,0},{24,8},{1,17},{9,25},{17,1},{25,9},{2,18},{10... | collective-permute-start | bytes 491528 | tf_op jit(solution)/shard_map/ppermute | solution.py:271
  196.1 9.2 %collective-permute-start.9 = (bf16[80,1024]{1,0:T(8,128)(2,1)S(1)}, bf16[80,1024]{1,0:T(8,128)(2,1)S(1)}, u32[]{:S(2)}, u32[]{:S(2)}) collective-permute-start(bf16[80,1024]{1,0:T(8,128)(2,1)S(1)} %get-tuple-element.34), channel_id=1, source_target_pairs={{0,8},{8,0},{16,24},{24,16},{1,9},{9,1},{17,25},{25,17},{2,10},{10... | collective-permute-start | bytes 491528 | tf_op jit(solution)/shard_map/ppermute | solution.py:271
  206.1 1.4 copy-start.2
  211.2 3.9 %collective-permute-start.13 = (bf16[4,176,1024]{2,1,0:T(8,128)(2,1)S(1)}, bf16[4,176,1024]{2,1,0:T(8,128)(2,1)S(1)}, u32[]{:S(2)}, u32[]{:S(2)}) collective-permute-start(bf16[4,176,1024]{2,1,0:T(8,128)(2,1)S(1)} %shard_map.81), channel_id=1, source_target_pairs={{0,1},{1,0},{2,3},{3,2},{4,5},{5,4},{6,7},{7,6},{8,9},{9,8},{10,11... | collective-permute-start | bytes 4325384 | tf_op jit(solution)/shard_map/ppermute | solution.py:268
  215.5 12.2 %collective-permute-start.16 = (bf16[176,1024]{1,0:T(8,128)(2,1)S(1)}, bf16[176,1024]{1,0:T(8,128)(2,1)S(1)}, u32[]{:S(2)}, u32[]{:S(2)}) collective-permute-start(bf16[176,1024]{1,0:T(8,128)(2,1)S(1)} %get-tuple-element.32), channel_id=1, source_target_pairs={{0,24},{8,16},{16,8},{24,0},{1,25},{9,17},{17,9},{25,1},{2,26},{10... | collective-permute-start | bytes 1081352 | tf_op jit(solution)/shard_map/ppermute | solution.py:271
  217.1 17.9 %collective-permute-start.15 = (bf16[176,1024]{1,0:T(8,128)(2,1)S(1)}, bf16[176,1024]{1,0:T(8,128)(2,1)S(1)}, u32[]{:S(2)}, u32[]{:S(2)}) collective-permute-start(bf16[176,1024]{1,0:T(8,128)(2,1)S(1)} %get-tuple-element.33), channel_id=1, source_target_pairs={{0,16},{8,24},{16,0},{24,8},{1,17},{9,25},{17,1},{25,9},{2,18},{10... | collective-permute-start | bytes 1081352 | tf_op jit(solution)/shard_map/ppermute | solution.py:271
  217.5 17.5 %collective-permute-start.14 = (bf16[176,1024]{1,0:T(8,128)(2,1)S(1)}, bf16[176,1024]{1,0:T(8,128)(2,1)S(1)}, u32[]{:S(2)}, u32[]{:S(2)}) collective-permute-start(bf16[176,1024]{1,0:T(8,128)(2,1)S(1)} %get-tuple-element.31), channel_id=1, source_target_pairs={{0,8},{8,0},{16,24},{24,16},{1,9},{9,1},{17,25},{25,17},{2,10},{10... | collective-permute-start | bytes 1081352 | tf_op jit(solution)/shard_map/ppermute | solution.py:271
  235.3 27.9 %collective-permute-start.17 = (bf16[176,1024]{1,0:T(8,128)(2,1)S(1)}, bf16[176,1024]{1,0:T(8,128)(2,1)S(1)}, u32[]{:S(2)}, u32[]{:S(2)}) collective-permute-start(bf16[176,1024]{1,0:T(8,128)(2,1)S(1)} %fusion.3), channel_id=1, source_target_pairs={{0,0},{1,1},{8,2},{9,3},{16,4},{17,5},{24,6},{25,7},{2,10},{3,11},... | collective-permute-start | bytes 1081352 | tf_op jit(solution)/shard_map/ppermute | solution.py:343
  239.8 23.4 %collective-permute-start.12 = (bf16[80,1024]{1,0:T(8,128)(2,1)S(1)}, bf16[80,1024]{1,0:T(8,128)(2,1)S(1)}, u32[]{:S(2)}, u32[]{:S(2)}) collective-permute-start(bf16[80,1024]{1,0:T(8,128)(2,1)S(1)} %fusion.9), channel_id=1, source_target_pairs={{0,0},{1,1},{8,2},{9,3},{16,4},{17,5},{24,6},{25,7},{2,10},{3,11},... | collective-permute-start | bytes 491528 | tf_op jit(solution)/shard_map/ppermute | solution.py:343
Sparse Core Ops, SparseCore 0:
  37.1 34.2 reduce-scatter.2
  73.8 85.7 reduce-scatter.4
  168.0 38.0 all-gather.3

commit v5 on v4

--- a/solution.py
+++ b/solution.py
@@ -15,7 +15,7 @@
 MIB = 1024 * 1024
 
 
-def norm_body(at_ref, t_ref, gain_ref, *refs):
+def norm_body(row_ref, shard_ref, t_ref, gain_ref, *refs):
     outs, held = refs[:-1], refs[-1]
     wide = t_ref[...].astype(F32)
     squares = jnp.mean(wide * wide, axis=1, keepdims=True)
@@ -24,27 +24,27 @@
     for p in range(held.shape[0]):
         held[p] = normed[:, p * depth : (p + 1) * depth]
     for e, o in enumerate(outs):
-        o[...] = held[lax.bitwise_xor(at_ref[1], e)]
-
-
-def norm(tokens, gain, at, rows, parts):
+        o[...] = held[lax.bitwise_xor(shard_ref[0], e)]
+
+
+def norm(tokens, gain, at, shard, rows, parts):
     width = tokens.shape[1]
     depth = width // parts
     return pl.pallas_call(
         norm_body,
         grid_spec=pltpu.PrefetchScalarGridSpec(
-            num_scalar_prefetch=1,
+            num_scalar_prefetch=2,
             grid=(1,),
             in_specs=[
-                pl.BlockSpec((rows, width), lambda i, s: (s[0], 0)),
-                pl.BlockSpec((1, width), lambda i, s: (0, 0)),
-            ],
-            out_specs=[pl.BlockSpec((rows, depth), lambda i, s: (0, 0))] * parts,
+                pl.BlockSpec((rows, width), lambda i, a, s: (a[0], 0)),
+                pl.BlockSpec((1, width), lambda i, a, s: (0, 0)),
+            ],
+            out_specs=[pl.BlockSpec((rows, depth), lambda i, a, s: (0, 0))] * parts,
             scratch_shapes=[pltpu.VMEM((parts, rows, depth), BF)],
         ),
         out_shape=[jax.ShapeDtypeStruct((rows, depth), BF)] * parts,
         compiler_params=pltpu.CompilerParams(vmem_limit_bytes=62 * MIB),
-    )(at, tokens, gain.reshape(1, width))
+    )(at.reshape(1), shard.reshape(1), tokens, gain.reshape(1, width))
 
 
 def in_proj_body(at_ref, x_ref, w_ref, o_ref, *, parts):
@@ -230,7 +230,7 @@
 
 def out_proj(g, w, place, pieces, rows, cols):
     parts, seq_len, width = g.shape
-    tile = min(512, cols)
+    tile = min(1024, cols)
     per = cols // tile
     return pl.pallas_call(
         out_proj_body,
@@ -281,7 +281,7 @@
     def swap_shard(v, e):
         return lax.ppermute(v, "seq", [(i, i ^ e) for i in range(n_seq)])
 
-    split = norm(tokens, norm_gain, jnp.stack([q, z]).astype(jnp.int32), rows, n_seq)
+    split = norm(tokens, norm_gain, q.astype(jnp.int32), z.astype(jnp.int32), rows, n_seq)
     own = jnp.concatenate([split[0]] + [swap_shard(split[e], e) for e in range(1, n_seq)])
     near = swap_core(own)
     far = [swap_chip(own, e) for e in range(1, n_fsdp)]
@@ -305,13 +305,16 @@
     halves = plane // n_seq
     cols = out_weight.shape[1] // halves
 
+    def spread(s):
+        return (((s ^ (s >> 1)) & 1) << 1) | (s >> 1) if n_seq == 4 else s
+
     def block_of(p):
-        return lax.bitwise_xor(p // halves, z)
+        return (p // halves) ^ spread(z)
 
     def place_for(core):
         piece = [lax.bitwise_xor(f, e) * n_tp + core for e in range(n_fsdp)]
         blocks = [block_of(p) for p in piece]
-        inverse = [lax.bitwise_xor(lax.bitwise_xor(t, z) * halves // n_tp, f) for t in range(n_fsdp)]
+        inverse = [((t ^ spread(z)) * halves // n_tp) ^ f for t in range(n_fsdp)]
         return jnp.stack([piece[0] % halves] + blocks + inverse).astype(jnp.int32)
 
     place_away, place_keep = place_for(1 - c), place_for(c)
@@ -320,7 +323,7 @@
         return (p // n_tp * n_seq + s) * n_tp + p % n_tp
 
     pairs = [
-        (flat(s, p), flat((p // halves) ^ s, s * halves + p % halves))
+        (flat(s, p), flat((p // halves) ^ spread(s), s * halves + p % halves))
         for s in range(n_seq)
         for p in range(plane)
     ]

time: 272 us -> 261 us (0.960)
  waiting for transfers between devices: 155 us -> 146 us
    ppermute x2, waiting for transfers between devices: 19.9 us -> 9.75 us  [shards(): placed = [lax.ppermute(p, ('fsdp', 'seq', 'tp'), pairs) for p in placed]]
  transfers between devices with their start and end apart: 21 -> 21, of which waited for: 15 -> 14; matrix products, arithmetic and copies ran while one was open for 3% -> 3% of each run, Pallas kernels for 11% -> 12%
where the time goes in v5:
time: 261 us; the launch traced here: 258 us
  waiting for transfers between devices  146 us (56%)
  Pallas kernels  44.5 us (17%)
  starting transfers between devices  20.3 us (8%)
  blocking collectives  20.2 us (8%)
  between operations  13.5 us (5%)
  local copies, waits for them, and re-layouts  8.64 us (3%)
  other arithmetic  5.03 us (2%)
    reduce_scatter x1, waiting for transfers between devices, shards(): got_second = lax.psum_scatter(second, 'seq', scatter_dimension=0)  85.8 us
    ppermute x9, waiting for transfers between devices, swap_chip(): return lax.ppermute(v, 'fsdp', [(i, i ^ e) for i in range(n_fsdp)])  37.8 us
    pallas_call x2, Pallas kernels, in_proj(): pl.pallas_call(functools.partial(in_proj_body, parts=parts), grid_spec=pl...  21.7 us
    all_gather x1, blocking collectives, shards(): gathers = [lax.all_gather(part, 'seq', axis=0) for part in gated]  20.2 us
    ppermute x3, waiting for transfers between devices, swap_shard(): return lax.ppermute(v, 'seq', [(i, i ^ e) for i in range(n_seq)])  10.7 us
    ppermute x9, starting transfers between devices, swap_chip(): return lax.ppermute(v, 'fsdp', [(i, i ^ e) for i in range(n_fsdp)])  10.7 us
    pallas_call x4, Pallas kernels, out_proj(): pl.pallas_call(out_proj_body, grid_spec=pltpu.PrefetchScalarGridSpec(num_...  10.3 us
    ppermute x2, waiting for transfers between devices, shards(): placed = [lax.ppermute(p, ('fsdp', 'seq', 'tp'), pairs) for p in placed]  9.75 us
  transfers between devices with their start and end apart: 21, of which 14 were waited for; matrix products, arithmetic and copies ran while one was open for 3% of the time, Pallas kernels for 12%

profile of v5, /device:TPU:18, one launch (start us, length us, event | category | flops | bytes accessed | tf_op | source)
XLA Modules:
  0.0 258.3 jit_solution(1644383454413860343)
XLA Ops:
  6.5 2.2 shard_map.73
  8.7 1.6 collective-permute-start
  10.6 1.6 collective-permute-start.2
  12.2 0.9 constant_dynamic-update-slice_fusion.3
  13.1 2.2 collective-permute-done
  15.3 5.2 %collective-permute-done.1 = bf16[32,2048]{1,0:T(8,128)(2,1)S(1)} collective-permute-done((bf16[32,2048]{1,0:T(8,128)(2,1)}, bf16[32,2048]{1,0:T(8,128)(2,1)S(1)}, u32[]{:S(2)}, u32[]{:S(2)}) %collective-permute-start.1) | collective-permute-done | bytes 131104 | tf_op jit(solution)/shard_map/ppermute | solution.py:282
  20.5 3.3 %collective-permute-done.2 = bf16[32,2048]{1,0:T(8,128)(2,1)S(1)} collective-permute-done((bf16[32,2048]{1,0:T(8,128)(2,1)}, bf16[32,2048]{1,0:T(8,128)(2,1)S(1)}, u32[]{:S(2)}, u32[]{:S(2)}) %collective-permute-start.2) | collective-permute-done | bytes 131104 | tf_op jit(solution)/shard_map/ppermute | solution.py:282
  23.9 0.6 collective-permute-start.4
  24.5 1.5 collective-permute-start.5
  26.0 1.4 collective-permute-start.6
  27.6 8.1 %shard_map.74 = bf16[4,2,3,128,256]{4,3,2,1,0:T(8,128)(2,1)} custom-call(s32[1]{0:T(128)} %bitcast.1.shard_ref.at_ref, bf16[256,2048]{1,0:T(8,128)(2,1)S(1)} %bitcast.63, bf16[3,2048,1024]{2,1,0:T(8,128)(2,1)} %w_ref.7), custom_call_target="tpu_custom_call" | custom-call | flops 3221225472 | bytes 15204352 | tf_op jit(solution)/shard_map/pallas_call | solution.py:73
  35.8 2.9 %collective-permute-done.4 = bf16[128,2048]{1,0:T(8,128)(2,1)S(1)} collective-permute-done((bf16[128,2048]{1,0:T(8,128)(2,1)S(1)}, bf16[128,2048]{1,0:T(8,128)(2,1)S(1)}, u32[]{:S(2)}, u32[]{:S(2)}) %collective-permute-start.4) | collective-permute-done | bytes 524320 | tf_op jit(solution)/shard_map/ppermute | solution.py:271
  38.7 10.1 %collective-permute-done.5 = bf16[128,2048]{1,0:T(8,128)(2,1)S(1)} collective-permute-done((bf16[128,2048]{1,0:T(8,128)(2,1)S(1)}, bf16[128,2048]{1,0:T(8,128)(2,1)S(1)}, u32[]{:S(2)}, u32[]{:S(2)}) %collective-permute-start.5) | collective-permute-done | bytes 524320 | tf_op jit(solution)/shard_map/ppermute | solution.py:271
  48.8 1.6 collective-permute-done.6
  50.7 0.7 constant_dynamic-slice_fusion.1
  51.6 0.7 maximum_bitcast_fusion.taps_ref
  52.3 2.0 shard_map.75.toep_ref
  54.2 1.6 pad_maximum_fusion
  55.8 13.6 %shard_map.76 = bf16[4,6,3,128,256]{4,3,2,1,0:T(8,128)(2,1)} custom-call(s32[1]{0:T(128)} %bitcast.1.shard_ref.at_ref, bf16[768,2048]{1,0:T(8,128)(2,1)S(1)} %bitcast.64, bf16[3,2048,1024]{2,1,0:T(8,128)(2,1)} %w_ref.7), custom_call_target="tpu_custom_call" | custom-call | flops 9663676416 | bytes 20447232 | tf_op jit(solution)/shard_map/pallas_call | solution.py:73
  70.1 0.5 convert_reduce_fusion
  70.6 1.0 copy.14.pos_ref
  71.7 0.6 copy.15.short_ref
  72.4 85.8 %reduce-scatter.5.cloned.1.call-done = bf16[1,6,3,128,256]{4,3,2,1,0:T(8,128)(2,1)} async-done(((bf16[4,6,3,128,256]{4,3,2,1,0:T(8,128)(2,1)}), bf16[1,6,3,128,256]{4,3,2,1,0:T(8,128)(2,1)}) %reduce-scatter.5.cloned.1.call-update) | async-done | bytes 1179664 | tf_op jit(solution)/shard_map/reduce_scatter | solution.py:295
  158.3 8.3 %shard_map.77 = (bf16[4,80,256]{2,1,0:T(8,128)(2,1)}, bf16[4,176,256]{2,1,0:T(8,128)(2,1)}) custom-call(s32[1]{0:T(128)} %bitcast.row_ref.base_ref, bf16[2,3,128,256]{3,2,1,0:T(8,128)(2,1)} %bitcast.80, bf16[6,3,128,256]{3,2,1,0:T(8,128)(2,1)} %bitcast.79, s32[1024,1]{1,0:T(8,128)} %copy.14.pos_ref, f32[7,3,256]{2,1,0:T(4,128)} %copy.15.short_ref, ...), custom_call_target="tpu_custom_call" | custom-call | flops 1073741824 | bytes 2097152 | tf_op jit(solution)/shard_map/pallas_call | solution.py:185
  166.5 20.2 %all-gather.1 = bf16[16,80,256]{2,1,0:T(8,128)(2,1)S(1)} all-gather(bf16[4,80,256]{2,1,0:T(8,128)(2,1)} %get-tuple-element.28), channel_id=3, replica_groups=mesh['fsdp'=4,'seq'=4,'tp'=2] {'seq'}, dimensions={0}, use_global_device_ids=true | all-gather | bytes 819200 | tf_op jit(solution)/shard_map/all_gather | solution.py:331
  186.8 2.2 copy-done.1
  189.0 1.4 shard_map.79
  190.4 1.4 shard_map.78
  191.8 0.7 collective-permute-done.8
  192.7 1.5 collective-permute-start.11
  194.5 1.8 collective-permute-start.9
  196.3 4.5 %collective-permute-done.11 = bf16[80,1024]{1,0:T(8,128)(2,1)S(1)} collective-permute-done((bf16[80,1024]{1,0:T(8,128)(2,1)S(1)}, bf16[80,1024]{1,0:T(8,128)(2,1)S(1)}, u32[]{:S(2)}, u32[]{:S(2)}) %collective-permute-start.11) | collective-permute-done | bytes 163872 | tf_op jit(solution)/shard_map/ppermute | solution.py:271
  200.8 2.7 %collective-permute-done.10 = bf16[80,1024]{1,0:T(8,128)(2,1)S(1)} collective-permute-done((bf16[80,1024]{1,0:T(8,128)(2,1)S(1)}, bf16[80,1024]{1,0:T(8,128)(2,1)S(1)}, u32[]{:S(2)}, u32[]{:S(2)}) %collective-permute-start.10) | collective-permute-done | bytes 163872 | tf_op jit(solution)/shard_map/ppermute | solution.py:271
  203.6 1.3 all-gather.4.cloned.1.call-done
  204.8 1.4 copy-done.2
  206.2 3.8 %shard_map.81 = bf16[4,176,1024]{2,1,0:T(8,128)(2,1)S(1)} custom-call(s32[9]{0:T(128)S(1)} %stack.95.place_ref, bf16[4,704,256]{2,1,0:T(8,128)(2,1)S(1)} %bitcast.67, bf16[1024,2048]{1,0:T(8,128)(2,1)} %w_ref.11), custom_call_target="tpu_custom_call" | custom-call | flops 23622320128 | bytes 4980736 | tf_op jit(solution)/shard_map/pallas_call | solution.py:235
  210.1 3.8 %shard_map.80 = bf16[4,176,1024]{2,1,0:T(8,128)(2,1)S(1)} custom-call(s32[9]{0:T(128)S(1)} %stack.89.place_ref, bf16[4,704,256]{2,1,0:T(8,128)(2,1)S(1)} %bitcast.68, bf16[1024,2048]{1,0:T(8,128)(2,1)} %w_ref.11), custom_call_target="tpu_custom_call" | custom-call | flops 23622320128 | bytes 4980736 | tf_op jit(solution)/shard_map/pallas_call | solution.py:235
  213.9 0.4 fusion.4
  214.3 1.5 collective-permute-start.16
  215.8 0.4 collective-permute-start.15
  216.3 1.6 collective-permute-start.14
  217.9 8.7 %collective-permute-done.16 = bf16[176,1024]{1,0:T(8,128)(2,1)S(1)} collective-permute-done((bf16[176,1024]{1,0:T(8,128)(2,1)S(1)}, bf16[176,1024]{1,0:T(8,128)(2,1)S(1)}, u32[]{:S(2)}, u32[]{:S(2)}) %collective-permute-start.16) | collective-permute-done | bytes 360480 | tf_op jit(solution)/shard_map/ppermute | solution.py:271
  226.5 7.2 %collective-permute-done.15 = bf16[176,1024]{1,0:T(8,128)(2,1)S(1)} collective-permute-done((bf16[176,1024]{1,0:T(8,128)(2,1)S(1)}, bf16[176,1024]{1,0:T(8,128)(2,1)S(1)}, u32[]{:S(2)}, u32[]{:S(2)}) %collective-permute-start.15) | collective-permute-done | bytes 360480 | tf_op jit(solution)/shard_map/ppermute | solution.py:271
  234.1 3.3 %collective-permute-start.17 = (bf16[176,1024]{1,0:T(8,128)(2,1)S(1)}, bf16[176,1024]{1,0:T(8,128)(2,1)S(1)}, u32[]{:S(2)}, u32[]{:S(2)}) collective-permute-start(bf16[176,1024]{1,0:T(8,128)(2,1)S(1)} %fusion.3), channel_id=1, source_target_pairs={{0,0},{1,1},{8,2},{9,3},{16,4},{17,5},{24,6},{25,7},{2,12},{3,13},... | collective-permute-start | bytes 1081352 | tf_op jit(solution)/shard_map/ppermute | solution.py:346
  237.5 2.4 collective-permute-start.12
  239.9 1.1 constant_dynamic-slice_fusion.2
  241.0 9.7 %collective-permute-done.12 = bf16[80,1024]{1,0:T(8,128)(2,1)S(1)} collective-permute-done((bf16[80,1024]{1,0:T(8,128)(2,1)S(1)}, bf16[80,1024]{1,0:T(8,128)(2,1)S(1)}, u32[]{:S(2)}, u32[]{:S(2)}) %collective-permute-start.12) | collective-permute-done | bytes 163872 | tf_op jit(solution)/shard_map/ppermute | solution.py:346
  250.8 1.0 add_convert_fusion
  (40 shorter events, 2.7 us)
Async XLA Ops:
  6.5 65.1 %copy-start = (f32[7,3,1024]{2,0,1:T(8,128)S(1)}, f32[7,3,1024]{2,0,1:T(8,128)}, u32[]{:S(2)}) copy-start(f32[7,3,1024]{2,0,1:T(8,128)} %param.10) | copy-start | bytes 258052
  6.5 65.9 %reduce-scatter.3.cloned.1.call-start = ((), (), s32[]{:S(2)}) async-start(), calls=%async_computation.2 | async-start | bytes 1966080 | tf_op jit(solution)/shard_map/reduce_scatter | solution.py:289
  8.7 6.6 %collective-permute-start = (bf16[32,2048]{1,0:T(8,128)(2,1)}, bf16[32,2048]{1,0:T(8,128)(2,1)S(1)}, u32[]{:S(2)}, u32[]{:S(2)}) collective-permute-start(bf16[32,2048]{1,0:T(8,128)(2,1)} %get-tuple-element.19), channel_id=1, source_target_pairs={{0,2},{2,0},{4,6},{6,4},{1,3},{3,1},{5,7},{7,5},{8,10},{10,8},{12,... | collective-permute-start | bytes 393224 | tf_op jit(solution)/shard_map/ppermute | solution.py:282
  10.3 10.2 %collective-permute-start.1 = (bf16[32,2048]{1,0:T(8,128)(2,1)}, bf16[32,2048]{1,0:T(8,128)(2,1)S(1)}, u32[]{:S(2)}, u32[]{:S(2)}) collective-permute-start(bf16[32,2048]{1,0:T(8,128)(2,1)} %get-tuple-element.20), channel_id=1, source_target_pairs={{0,4},{2,6},{4,0},{6,2},{1,5},{3,7},{5,1},{7,3},{8,12},{10,14},{12... | collective-permute-start | bytes 393224 | tf_op jit(solution)/shard_map/ppermute | solution.py:282
  10.6 13.2 %collective-permute-start.2 = (bf16[32,2048]{1,0:T(8,128)(2,1)}, bf16[32,2048]{1,0:T(8,128)(2,1)S(1)}, u32[]{:S(2)}, u32[]{:S(2)}) collective-permute-start(bf16[32,2048]{1,0:T(8,128)(2,1)} %get-tuple-element.21), channel_id=1, source_target_pairs={{0,6},{2,4},{4,2},{6,0},{1,7},{3,5},{5,3},{7,1},{8,14},{10,12},{12... | collective-permute-start | bytes 393224 | tf_op jit(solution)/shard_map/ppermute | solution.py:282
  23.8 3.6 %collective-permute-start.3 = (bf16[128,2048]{1,0:T(8,128)(2,1)S(1)}, bf16[128,2048]{1,0:T(8,128)(2,1)S(1)}, u32[]{:S(2)}, u32[]{:S(2)}) collective-permute-start(bf16[128,2048]{1,0:T(8,128)(2,1)S(1)} %constant_dynamic-update-slice_fusion), channel_id=1, source_target_pairs={{0,1},{1,0},{2,3},{3,2},{4,5},{5,4},{6,7},{7,6},{8,9},{9,8},{10,11... | collective-permute-start | bytes 1572872 | tf_op jit(solution)/shard_map/ppermute | solution.py:268
  23.9 14.8 %collective-permute-start.4 = (bf16[128,2048]{1,0:T(8,128)(2,1)S(1)}, bf16[128,2048]{1,0:T(8,128)(2,1)S(1)}, u32[]{:S(2)}, u32[]{:S(2)}) collective-permute-start(bf16[128,2048]{1,0:T(8,128)(2,1)S(1)} %constant_dynamic-update-slice_fusion), channel_id=1, source_target_pairs={{0,8},{8,0},{16,24},{24,16},{1,9},{9,1},{17,25},{25,17},{2,10},{10... | collective-permute-start | bytes 1572872 | tf_op jit(solution)/shard_map/ppermute | solution.py:271
  24.5 24.3 %collective-permute-start.5 = (bf16[128,2048]{1,0:T(8,128)(2,1)S(1)}, bf16[128,2048]{1,0:T(8,128)(2,1)S(1)}, u32[]{:S(2)}, u32[]{:S(2)}) collective-permute-start(bf16[128,2048]{1,0:T(8,128)(2,1)S(1)} %constant_dynamic-update-slice_fusion), channel_id=1, source_target_pairs={{0,16},{8,24},{16,0},{24,8},{1,17},{9,25},{17,1},{25,9},{2,18},{10... | collective-permute-start | bytes 1572872 | tf_op jit(solution)/shard_map/ppermute | solution.py:271
  26.0 24.4 %collective-permute-start.6 = (bf16[128,2048]{1,0:T(8,128)(2,1)S(1)}, bf16[128,2048]{1,0:T(8,128)(2,1)S(1)}, u32[]{:S(2)}, u32[]{:S(2)}) collective-permute-start(bf16[128,2048]{1,0:T(8,128)(2,1)S(1)} %constant_dynamic-update-slice_fusion), channel_id=1, source_target_pairs={{0,24},{8,16},{16,8},{24,0},{1,25},{9,17},{17,9},{25,1},{2,26},{10... | collective-permute-start | bytes 1572872 | tf_op jit(solution)/shard_map/ppermute | solution.py:271
  35.7 122.5 %reduce-scatter.5.cloned.1.call-start = ((), (), s32[]{:S(2)}) async-start(), calls=%async_computation.3 | async-start | bytes 5898240 | tf_op jit(solution)/shard_map/reduce_scatter | solution.py:295
  50.6 3.6 %collective-permute-start.7 = (bf16[3,128,2048]{2,1,0:T(8,128)(2,1)S(1)}, bf16[3,128,2048]{2,1,0:T(8,128)(2,1)}, u32[]{:S(2)}, u32[]{:S(2)}) collective-permute-start(bf16[3,128,2048]{2,1,0:T(8,128)(2,1)S(1)} %pad_maximum_fusion.1), channel_id=1, source_target_pairs={{0,1},{1,0},{2,3},{3,2},{4,5},{5,4},{6,7},{7,6},{8,9},{9,8},{10,11... | collective-permute-start | bytes 4718600 | tf_op jit(solution)/shard_map/ppermute | solution.py:268
  69.4 0.7 copy-start.3
  69.4 135.4 %all-gather.4.cloned.1.call-start = ((), (), s32[]{:S(2)}) async-start(), calls=%async_computation.4 | async-start | bytes 1802240 | tf_op jit(solution)/shard_map/all_gather | solution.py:331
  186.8 2.2 copy-start.1
  190.4 2.2 collective-permute-start.8
  192.7 8.1 %collective-permute-start.11 = (bf16[80,1024]{1,0:T(8,128)(2,1)S(1)}, bf16[80,1024]{1,0:T(8,128)(2,1)S(1)}, u32[]{:S(2)}, u32[]{:S(2)}) collective-permute-start(bf16[80,1024]{1,0:T(8,128)(2,1)S(1)} %get-tuple-element.35), channel_id=1, source_target_pairs={{0,24},{8,16},{16,8},{24,0},{1,25},{9,17},{17,9},{25,1},{2,26},{10... | collective-permute-start | bytes 491528 | tf_op jit(solution)/shard_map/ppermute | solution.py:271
  194.2 9.2 %collective-permute-start.10 = (bf16[80,1024]{1,0:T(8,128)(2,1)S(1)}, bf16[80,1024]{1,0:T(8,128)(2,1)S(1)}, u32[]{:S(2)}, u32[]{:S(2)}) collective-permute-start(bf16[80,1024]{1,0:T(8,128)(2,1)S(1)} %get-tuple-element.36), channel_id=1, source_target_pairs={{0,16},{8,24},{16,0},{24,8},{1,17},{9,25},{17,1},{25,9},{2,18},{10... | collective-permute-start | bytes 491528 | tf_op jit(solution)/shard_map/ppermute | solution.py:271
  194.5 8.9 %collective-permute-start.9 = (bf16[80,1024]{1,0:T(8,128)(2,1)S(1)}, bf16[80,1024]{1,0:T(8,128)(2,1)S(1)}, u32[]{:S(2)}, u32[]{:S(2)}) collective-permute-start(bf16[80,1024]{1,0:T(8,128)(2,1)S(1)} %get-tuple-element.34), channel_id=1, source_target_pairs={{0,8},{8,0},{16,24},{24,16},{1,9},{9,1},{17,25},{25,17},{2,10},{10... | collective-permute-start | bytes 491528 | tf_op jit(solution)/shard_map/ppermute | solution.py:271
  204.8 1.4 copy-start.2
  210.0 3.9 %collective-permute-start.13 = (bf16[4,176,1024]{2,1,0:T(8,128)(2,1)S(1)}, bf16[4,176,1024]{2,1,0:T(8,128)(2,1)S(1)}, u32[]{:S(2)}, u32[]{:S(2)}) collective-permute-start(bf16[4,176,1024]{2,1,0:T(8,128)(2,1)S(1)} %shard_map.81), channel_id=1, source_target_pairs={{0,1},{1,0},{2,3},{3,2},{4,5},{5,4},{6,7},{7,6},{8,9},{9,8},{10,11... | collective-permute-start | bytes 4325384 | tf_op jit(solution)/shard_map/ppermute | solution.py:268
  214.3 12.2 %collective-permute-start.16 = (bf16[176,1024]{1,0:T(8,128)(2,1)S(1)}, bf16[176,1024]{1,0:T(8,128)(2,1)S(1)}, u32[]{:S(2)}, u32[]{:S(2)}) collective-permute-start(bf16[176,1024]{1,0:T(8,128)(2,1)S(1)} %get-tuple-element.32), channel_id=1, source_target_pairs={{0,24},{8,16},{16,8},{24,0},{1,25},{9,17},{17,9},{25,1},{2,26},{10... | collective-permute-start | bytes 1081352 | tf_op jit(solution)/shard_map/ppermute | solution.py:271
  215.8 17.9 %collective-permute-start.15 = (bf16[176,1024]{1,0:T(8,128)(2,1)S(1)}, bf16[176,1024]{1,0:T(8,128)(2,1)S(1)}, u32[]{:S(2)}, u32[]{:S(2)}) collective-permute-start(bf16[176,1024]{1,0:T(8,128)(2,1)S(1)} %get-tuple-element.33), channel_id=1, source_target_pairs={{0,16},{8,24},{16,0},{24,8},{1,17},{9,25},{17,1},{25,9},{2,18},{10... | collective-permute-start | bytes 1081352 | tf_op jit(solution)/shard_map/ppermute | solution.py:271
  216.3 17.6 %collective-permute-start.14 = (bf16[176,1024]{1,0:T(8,128)(2,1)S(1)}, bf16[176,1024]{1,0:T(8,128)(2,1)S(1)}, u32[]{:S(2)}, u32[]{:S(2)}) collective-permute-start(bf16[176,1024]{1,0:T(8,128)(2,1)S(1)} %get-tuple-element.31), channel_id=1, source_target_pairs={{0,8},{8,0},{16,24},{24,16},{1,9},{9,1},{17,25},{25,17},{2,10},{10... | collective-permute-start | bytes 1081352 | tf_op jit(solution)/shard_map/ppermute | solution.py:271
  234.1 16.6 %collective-permute-start.17 = (bf16[176,1024]{1,0:T(8,128)(2,1)S(1)}, bf16[176,1024]{1,0:T(8,128)(2,1)S(1)}, u32[]{:S(2)}, u32[]{:S(2)}) collective-permute-start(bf16[176,1024]{1,0:T(8,128)(2,1)S(1)} %fusion.3), channel_id=1, source_target_pairs={{0,0},{1,1},{8,2},{9,3},{16,4},{17,5},{24,6},{25,7},{2,12},{3,13},... | collective-permute-start | bytes 1081352 | tf_op jit(solution)/shard_map/ppermute | solution.py:346
  237.5 13.3 %collective-permute-start.12 = (bf16[80,1024]{1,0:T(8,128)(2,1)S(1)}, bf16[80,1024]{1,0:T(8,128)(2,1)S(1)}, u32[]{:S(2)}, u32[]{:S(2)}) collective-permute-start(bf16[80,1024]{1,0:T(8,128)(2,1)S(1)} %fusion.9), channel_id=1, source_target_pairs={{0,0},{1,1},{8,2},{9,3},{16,4},{17,5},{24,6},{25,7},{2,12},{3,13},... | collective-permute-start | bytes 491528 | tf_op jit(solution)/shard_map/ppermute | solution.py:346
Sparse Core Ops, SparseCore 0:
  35.8 34.2 reduce-scatter.2
  72.5 85.7 reduce-scatter.4
  166.7 38.1 all-gather.3

commit v6 on v5

--- a/solution.py
+++ b/solution.py
@@ -172,7 +172,7 @@
                 begin = end
         return carry
 
-    lax.fori_loop(0, shards, shard, 0)
+    lax.fori_loop(0, shards, shard, 0, unroll=4)
 
 
 def convolve(first, second, position, short, matrices, shards, base, splits):

time: 261 us -> 260 us (level)
  transfers between devices with their start and end apart: 21 -> 21, of which waited for: 14 -> 16; matrix products, arithmetic and copies ran while one was open for 3% -> 3% of each run, Pallas kernels for 12% -> 12%
where the time goes in v6:
time: 260 us; the launch traced here: 257 us
  waiting for transfers between devices  146 us (56%)
  Pallas kernels  43.1 us (17%)
  starting transfers between devices  20.4 us (8%)
  blocking collectives  20 us (8%)
  between operations  13.5 us (5%)
  local copies, waits for them, and re-layouts  8.63 us (3%)
  other arithmetic  5.03 us (2%)
    reduce_scatter x1, waiting for transfers between devices, shards(): got_second = lax.psum_scatter(second, 'seq', scatter_dimension=0)  85.8 us
    ppermute x9, waiting for transfers between devices, swap_chip(): return lax.ppermute(v, 'fsdp', [(i, i ^ e) for i in range(n_fsdp)])  37.8 us
    pallas_call x2, Pallas kernels, in_proj(): pl.pallas_call(functools.partial(in_proj_body, parts=parts), grid_spec=pl...  21.7 us
    all_gather x1, blocking collectives, shards(): gathers = [lax.all_gather(part, 'seq', axis=0) for part in gated]  20 us
    ppermute x3, waiting for transfers between devices, swap_shard(): return lax.ppermute(v, 'seq', [(i, i ^ e) for i in range(n_seq)])  10.7 us
    ppermute x9, starting transfers between devices, swap_chip(): return lax.ppermute(v, 'fsdp', [(i, i ^ e) for i in range(n_fsdp)])  10.7 us
    pallas_call x4, Pallas kernels, out_proj(): pl.pallas_call(out_proj_body, grid_spec=pltpu.PrefetchScalarGridSpec(num_...  10.3 us
    ppermute x2, waiting for transfers between devices, shards(): placed = [lax.ppermute(p, ('fsdp', 'seq', 'tp'), pairs) for p in placed]  9.73 us
  transfers between devices with their start and end apart: 21, of which 16 were waited for; matrix products, arithmetic and copies ran while one was open for 3% of the time, Pallas kernels for 12%

profile of v6, /device:TPU:18, one launch (start us, length us, event | category | flops | bytes accessed | tf_op | source)
XLA Modules:
  0.0 256.8 jit_solution(16089076689689805208)
XLA Ops:
  6.5 2.2 shard_map.73
  8.7 1.6 collective-permute-start
  10.6 1.6 collective-permute-start.2
  12.2 0.9 constant_dynamic-update-slice_fusion.3
  13.1 2.2 collective-permute-done
  15.3 5.2 %collective-permute-done.1 = bf16[32,2048]{1,0:T(8,128)(2,1)S(1)} collective-permute-done((bf16[32,2048]{1,0:T(8,128)(2,1)}, bf16[32,2048]{1,0:T(8,128)(2,1)S(1)}, u32[]{:S(2)}, u32[]{:S(2)}) %collective-permute-start.1) | collective-permute-done | bytes 131104 | tf_op jit(solution)/shard_map/ppermute | solution.py:282
  20.5 3.3 %collective-permute-done.2 = bf16[32,2048]{1,0:T(8,128)(2,1)S(1)} collective-permute-done((bf16[32,2048]{1,0:T(8,128)(2,1)}, bf16[32,2048]{1,0:T(8,128)(2,1)S(1)}, u32[]{:S(2)}, u32[]{:S(2)}) %collective-permute-start.2) | collective-permute-done | bytes 131104 | tf_op jit(solution)/shard_map/ppermute | solution.py:282
  23.9 0.6 collective-permute-start.4
  24.5 1.5 collective-permute-start.5
  26.0 1.4 collective-permute-start.6
  27.6 8.1 %shard_map.74 = bf16[4,2,3,128,256]{4,3,2,1,0:T(8,128)(2,1)} custom-call(s32[1]{0:T(128)} %bitcast.1.shard_ref.at_ref, bf16[256,2048]{1,0:T(8,128)(2,1)S(1)} %bitcast.63, bf16[3,2048,1024]{2,1,0:T(8,128)(2,1)} %w_ref.7), custom_call_target="tpu_custom_call" | custom-call | flops 3221225472 | bytes 15204352 | tf_op jit(solution)/shard_map/pallas_call | solution.py:73
  35.8 2.9 %collective-permute-done.4 = bf16[128,2048]{1,0:T(8,128)(2,1)S(1)} collective-permute-done((bf16[128,2048]{1,0:T(8,128)(2,1)S(1)}, bf16[128,2048]{1,0:T(8,128)(2,1)S(1)}, u32[]{:S(2)}, u32[]{:S(2)}) %collective-permute-start.4) | collective-permute-done | bytes 524320 | tf_op jit(solution)/shard_map/ppermute | solution.py:271
  38.7 10.1 %collective-permute-done.5 = bf16[128,2048]{1,0:T(8,128)(2,1)S(1)} collective-permute-done((bf16[128,2048]{1,0:T(8,128)(2,1)S(1)}, bf16[128,2048]{1,0:T(8,128)(2,1)S(1)}, u32[]{:S(2)}, u32[]{:S(2)}) %collective-permute-start.5) | collective-permute-done | bytes 524320 | tf_op jit(solution)/shard_map/ppermute | solution.py:271
  48.8 1.6 collective-permute-done.6
  50.7 0.7 constant_dynamic-slice_fusion.1
  51.6 0.7 maximum_bitcast_fusion.taps_ref
  52.3 2.0 shard_map.75.toep_ref
  54.2 1.6 pad_maximum_fusion
  55.8 13.6 %shard_map.76 = bf16[4,6,3,128,256]{4,3,2,1,0:T(8,128)(2,1)} custom-call(s32[1]{0:T(128)} %bitcast.1.shard_ref.at_ref, bf16[768,2048]{1,0:T(8,128)(2,1)S(1)} %bitcast.64, bf16[3,2048,1024]{2,1,0:T(8,128)(2,1)} %w_ref.7), custom_call_target="tpu_custom_call" | custom-call | flops 9663676416 | bytes 20447232 | tf_op jit(solution)/shard_map/pallas_call | solution.py:73
  70.1 0.5 convert_reduce_fusion
  70.6 1.0 copy.14.pos_ref
  71.7 0.6 copy.15.short_ref
  72.4 85.8 %reduce-scatter.5.cloned.1.call-done = bf16[1,6,3,128,256]{4,3,2,1,0:T(8,128)(2,1)} async-done(((bf16[4,6,3,128,256]{4,3,2,1,0:T(8,128)(2,1)}), bf16[1,6,3,128,256]{4,3,2,1,0:T(8,128)(2,1)}) %reduce-scatter.5.cloned.1.call-update) | async-done | bytes 1179664 | tf_op jit(solution)/shard_map/reduce_scatter | solution.py:295
  158.3 6.8 %shard_map.77 = (bf16[4,80,256]{2,1,0:T(8,128)(2,1)}, bf16[4,176,256]{2,1,0:T(8,128)(2,1)}) custom-call(s32[1]{0:T(128)} %bitcast.row_ref.base_ref, bf16[2,3,128,256]{3,2,1,0:T(8,128)(2,1)} %bitcast.80, bf16[6,3,128,256]{3,2,1,0:T(8,128)(2,1)} %bitcast.79, s32[1024,1]{1,0:T(8,128)} %copy.14.pos_ref, f32[7,3,256]{2,1,0:T(4,128)} %copy.15.short_ref, ...), custom_call_target="tpu_custom_call" | custom-call | flops 1073741824 | bytes 2097152 | tf_op jit(solution)/shard_map/pallas_call | solution.py:185
  165.1 20.0 %all-gather.1 = bf16[16,80,256]{2,1,0:T(8,128)(2,1)S(1)} all-gather(bf16[4,80,256]{2,1,0:T(8,128)(2,1)} %get-tuple-element.28), channel_id=3, replica_groups=mesh['fsdp'=4,'seq'=4,'tp'=2] {'seq'}, dimensions={0}, use_global_device_ids=true | all-gather | bytes 819200 | tf_op jit(solution)/shard_map/all_gather | solution.py:331
  185.1 2.2 copy-done.1
  187.3 1.4 shard_map.79
  188.7 1.4 shard_map.78
  190.1 0.7 collective-permute-done.8
  191.0 1.8 collective-permute-start.11
  193.1 1.5 collective-permute-start.9
  194.5 4.5 %collective-permute-done.11 = bf16[80,1024]{1,0:T(8,128)(2,1)S(1)} collective-permute-done((bf16[80,1024]{1,0:T(8,128)(2,1)S(1)}, bf16[80,1024]{1,0:T(8,128)(2,1)S(1)}, u32[]{:S(2)}, u32[]{:S(2)}) %collective-permute-start.11) | collective-permute-done | bytes 163872 | tf_op jit(solution)/shard_map/ppermute | solution.py:271
  199.0 2.7 %collective-permute-done.10 = bf16[80,1024]{1,0:T(8,128)(2,1)S(1)} collective-permute-done((bf16[80,1024]{1,0:T(8,128)(2,1)S(1)}, bf16[80,1024]{1,0:T(8,128)(2,1)S(1)}, u32[]{:S(2)}, u32[]{:S(2)}) %collective-permute-start.10) | collective-permute-done | bytes 163872 | tf_op jit(solution)/shard_map/ppermute | solution.py:271
  201.9 1.5 all-gather.4.cloned.1.call-done
  203.3 1.4 copy-done.2
  204.7 3.8 %shard_map.81 = bf16[4,176,1024]{2,1,0:T(8,128)(2,1)S(1)} custom-call(s32[9]{0:T(128)S(1)} %stack.95.place_ref, bf16[4,704,256]{2,1,0:T(8,128)(2,1)S(1)} %bitcast.67, bf16[1024,2048]{1,0:T(8,128)(2,1)} %w_ref.11), custom_call_target="tpu_custom_call" | custom-call | flops 23622320128 | bytes 4980736 | tf_op jit(solution)/shard_map/pallas_call | solution.py:235
  208.6 3.8 %shard_map.80 = bf16[4,176,1024]{2,1,0:T(8,128)(2,1)S(1)} custom-call(s32[9]{0:T(128)S(1)} %stack.89.place_ref, bf16[4,704,256]{2,1,0:T(8,128)(2,1)S(1)} %bitcast.68, bf16[1024,2048]{1,0:T(8,128)(2,1)} %w_ref.11), custom_call_target="tpu_custom_call" | custom-call | flops 23622320128 | bytes 4980736 | tf_op jit(solution)/shard_map/pallas_call | solution.py:235
  212.4 0.4 fusion.4
  212.9 1.5 collective-permute-start.16
  214.4 0.4 collective-permute-start.15
  214.8 1.6 collective-permute-start.14
  216.4 8.7 %collective-permute-done.16 = bf16[176,1024]{1,0:T(8,128)(2,1)S(1)} collective-permute-done((bf16[176,1024]{1,0:T(8,128)(2,1)S(1)}, bf16[176,1024]{1,0:T(8,128)(2,1)S(1)}, u32[]{:S(2)}, u32[]{:S(2)}) %collective-permute-start.16) | collective-permute-done | bytes 360480 | tf_op jit(solution)/shard_map/ppermute | solution.py:271
  225.1 7.2 %collective-permute-done.15 = bf16[176,1024]{1,0:T(8,128)(2,1)S(1)} collective-permute-done((bf16[176,1024]{1,0:T(8,128)(2,1)S(1)}, bf16[176,1024]{1,0:T(8,128)(2,1)S(1)}, u32[]{:S(2)}, u32[]{:S(2)}) %collective-permute-start.15) | collective-permute-done | bytes 360480 | tf_op jit(solution)/shard_map/ppermute | solution.py:271
  232.7 3.3 %collective-permute-start.17 = (bf16[176,1024]{1,0:T(8,128)(2,1)S(1)}, bf16[176,1024]{1,0:T(8,128)(2,1)S(1)}, u32[]{:S(2)}, u32[]{:S(2)}) collective-permute-start(bf16[176,1024]{1,0:T(8,128)(2,1)S(1)} %fusion.3), channel_id=1, source_target_pairs={{0,0},{1,1},{8,2},{9,3},{16,4},{17,5},{24,6},{25,7},{2,12},{3,13},... | collective-permute-start | bytes 1081352 | tf_op jit(solution)/shard_map/ppermute | solution.py:346
  236.0 2.5 collective-permute-start.12
  238.5 1.1 constant_dynamic-slice_fusion.2
  239.6 9.7 %collective-permute-done.12 = bf16[80,1024]{1,0:T(8,128)(2,1)S(1)} collective-permute-done((bf16[80,1024]{1,0:T(8,128)(2,1)S(1)}, bf16[80,1024]{1,0:T(8,128)(2,1)S(1)}, u32[]{:S(2)}, u32[]{:S(2)}) %collective-permute-start.12) | collective-permute-done | bytes 163872 | tf_op jit(solution)/shard_map/ppermute | solution.py:346
  249.3 1.0 add_convert_fusion
  (40 shorter events, 2.8 us)
Async XLA Ops:
  6.5 65.1 %copy-start = (f32[7,3,1024]{2,0,1:T(8,128)S(1)}, f32[7,3,1024]{2,0,1:T(8,128)}, u32[]{:S(2)}) copy-start(f32[7,3,1024]{2,0,1:T(8,128)} %param.10) | copy-start | bytes 258052
  6.5 65.9 %reduce-scatter.3.cloned.1.call-start = ((), (), s32[]{:S(2)}) async-start(), calls=%async_computation.2 | async-start | bytes 1966080 | tf_op jit(solution)/shard_map/reduce_scatter | solution.py:289
  8.7 6.6 %collective-permute-start = (bf16[32,2048]{1,0:T(8,128)(2,1)}, bf16[32,2048]{1,0:T(8,128)(2,1)S(1)}, u32[]{:S(2)}, u32[]{:S(2)}) collective-permute-start(bf16[32,2048]{1,0:T(8,128)(2,1)} %get-tuple-element.19), channel_id=1, source_target_pairs={{0,2},{2,0},{4,6},{6,4},{1,3},{3,1},{5,7},{7,5},{8,10},{10,8},{12,... | collective-permute-start | bytes 393224 | tf_op jit(solution)/shard_map/ppermute | solution.py:282
  10.3 10.2 %collective-permute-start.1 = (bf16[32,2048]{1,0:T(8,128)(2,1)}, bf16[32,2048]{1,0:T(8,128)(2,1)S(1)}, u32[]{:S(2)}, u32[]{:S(2)}) collective-permute-start(bf16[32,2048]{1,0:T(8,128)(2,1)} %get-tuple-element.20), channel_id=1, source_target_pairs={{0,4},{2,6},{4,0},{6,2},{1,5},{3,7},{5,1},{7,3},{8,12},{10,14},{12... | collective-permute-start | bytes 393224 | tf_op jit(solution)/shard_map/ppermute | solution.py:282
  10.6 13.2 %collective-permute-start.2 = (bf16[32,2048]{1,0:T(8,128)(2,1)}, bf16[32,2048]{1,0:T(8,128)(2,1)S(1)}, u32[]{:S(2)}, u32[]{:S(2)}) collective-permute-start(bf16[32,2048]{1,0:T(8,128)(2,1)} %get-tuple-element.21), channel_id=1, source_target_pairs={{0,6},{2,4},{4,2},{6,0},{1,7},{3,5},{5,3},{7,1},{8,14},{10,12},{12... | collective-permute-start | bytes 393224 | tf_op jit(solution)/shard_map/ppermute | solution.py:282
  23.8 3.6 %collective-permute-start.3 = (bf16[128,2048]{1,0:T(8,128)(2,1)S(1)}, bf16[128,2048]{1,0:T(8,128)(2,1)S(1)}, u32[]{:S(2)}, u32[]{:S(2)}) collective-permute-start(bf16[128,2048]{1,0:T(8,128)(2,1)S(1)} %constant_dynamic-update-slice_fusion), channel_id=1, source_target_pairs={{0,1},{1,0},{2,3},{3,2},{4,5},{5,4},{6,7},{7,6},{8,9},{9,8},{10,11... | collective-permute-start | bytes 1572872 | tf_op jit(solution)/shard_map/ppermute | solution.py:268
  23.9 14.8 %collective-permute-start.4 = (bf16[128,2048]{1,0:T(8,128)(2,1)S(1)}, bf16[128,2048]{1,0:T(8,128)(2,1)S(1)}, u32[]{:S(2)}, u32[]{:S(2)}) collective-permute-start(bf16[128,2048]{1,0:T(8,128)(2,1)S(1)} %constant_dynamic-update-slice_fusion), channel_id=1, source_target_pairs={{0,8},{8,0},{16,24},{24,16},{1,9},{9,1},{17,25},{25,17},{2,10},{10... | collective-permute-start | bytes 1572872 | tf_op jit(solution)/shard_map/ppermute | solution.py:271
  24.5 24.3 %collective-permute-start.5 = (bf16[128,2048]{1,0:T(8,128)(2,1)S(1)}, bf16[128,2048]{1,0:T(8,128)(2,1)S(1)}, u32[]{:S(2)}, u32[]{:S(2)}) collective-permute-start(bf16[128,2048]{1,0:T(8,128)(2,1)S(1)} %constant_dynamic-update-slice_fusion), channel_id=1, source_target_pairs={{0,16},{8,24},{16,0},{24,8},{1,17},{9,25},{17,1},{25,9},{2,18},{10... | collective-permute-start | bytes 1572872 | tf_op jit(solution)/shard_map/ppermute | solution.py:271
  26.0 24.4 %collective-permute-start.6 = (bf16[128,2048]{1,0:T(8,128)(2,1)S(1)}, bf16[128,2048]{1,0:T(8,128)(2,1)S(1)}, u32[]{:S(2)}, u32[]{:S(2)}) collective-permute-start(bf16[128,2048]{1,0:T(8,128)(2,1)S(1)} %constant_dynamic-update-slice_fusion), channel_id=1, source_target_pairs={{0,24},{8,16},{16,8},{24,0},{1,25},{9,17},{17,9},{25,1},{2,26},{10... | collective-permute-start | bytes 1572872 | tf_op jit(solution)/shard_map/ppermute | solution.py:271
  35.7 122.5 %reduce-scatter.5.cloned.1.call-start = ((), (), s32[]{:S(2)}) async-start(), calls=%async_computation.3 | async-start | bytes 5898240 | tf_op jit(solution)/shard_map/reduce_scatter | solution.py:295
  50.6 3.6 %collective-permute-start.7 = (bf16[3,128,2048]{2,1,0:T(8,128)(2,1)S(1)}, bf16[3,128,2048]{2,1,0:T(8,128)(2,1)}, u32[]{:S(2)}, u32[]{:S(2)}) collective-permute-start(bf16[3,128,2048]{2,1,0:T(8,128)(2,1)S(1)} %pad_maximum_fusion.1), channel_id=1, source_target_pairs={{0,1},{1,0},{2,3},{3,2},{4,5},{5,4},{6,7},{7,6},{8,9},{9,8},{10,11... | collective-permute-start | bytes 4718600 | tf_op jit(solution)/shard_map/ppermute | solution.py:268
  69.4 0.7 copy-start.3
  69.4 133.9 %all-gather.4.cloned.1.call-start = ((), (), s32[]{:S(2)}) async-start(), calls=%async_computation.4 | async-start | bytes 1802240 | tf_op jit(solution)/shard_map/all_gather | solution.py:331
  185.1 2.2 copy-start.1
  188.6 2.2 collective-permute-start.8
  191.0 8.1 %collective-permute-start.11 = (bf16[80,1024]{1,0:T(8,128)(2,1)S(1)}, bf16[80,1024]{1,0:T(8,128)(2,1)S(1)}, u32[]{:S(2)}, u32[]{:S(2)}) collective-permute-start(bf16[80,1024]{1,0:T(8,128)(2,1)S(1)} %get-tuple-element.35), channel_id=1, source_target_pairs={{0,24},{8,16},{16,8},{24,0},{1,25},{9,17},{17,9},{25,1},{2,26},{10... | collective-permute-start | bytes 491528 | tf_op jit(solution)/shard_map/ppermute | solution.py:271
  192.7 9.0 %collective-permute-start.10 = (bf16[80,1024]{1,0:T(8,128)(2,1)S(1)}, bf16[80,1024]{1,0:T(8,128)(2,1)S(1)}, u32[]{:S(2)}, u32[]{:S(2)}) collective-permute-start(bf16[80,1024]{1,0:T(8,128)(2,1)S(1)} %get-tuple-element.36), channel_id=1, source_target_pairs={{0,16},{8,24},{16,0},{24,8},{1,17},{9,25},{17,1},{25,9},{2,18},{10... | collective-permute-start | bytes 491528 | tf_op jit(solution)/shard_map/ppermute | solution.py:271
  193.1 8.7 %collective-permute-start.9 = (bf16[80,1024]{1,0:T(8,128)(2,1)S(1)}, bf16[80,1024]{1,0:T(8,128)(2,1)S(1)}, u32[]{:S(2)}, u32[]{:S(2)}) collective-permute-start(bf16[80,1024]{1,0:T(8,128)(2,1)S(1)} %get-tuple-element.34), channel_id=1, source_target_pairs={{0,8},{8,0},{16,24},{24,16},{1,9},{9,1},{17,25},{25,17},{2,10},{10... | collective-permute-start | bytes 491528 | tf_op jit(solution)/shard_map/ppermute | solution.py:271
  203.3 1.4 copy-start.2
  208.5 3.9 %collective-permute-start.13 = (bf16[4,176,1024]{2,1,0:T(8,128)(2,1)S(1)}, bf16[4,176,1024]{2,1,0:T(8,128)(2,1)S(1)}, u32[]{:S(2)}, u32[]{:S(2)}) collective-permute-start(bf16[4,176,1024]{2,1,0:T(8,128)(2,1)S(1)} %shard_map.81), channel_id=1, source_target_pairs={{0,1},{1,0},{2,3},{3,2},{4,5},{5,4},{6,7},{7,6},{8,9},{9,8},{10,11... | collective-permute-start | bytes 4325384 | tf_op jit(solution)/shard_map/ppermute | solution.py:268
  212.9 12.2 %collective-permute-start.16 = (bf16[176,1024]{1,0:T(8,128)(2,1)S(1)}, bf16[176,1024]{1,0:T(8,128)(2,1)S(1)}, u32[]{:S(2)}, u32[]{:S(2)}) collective-permute-start(bf16[176,1024]{1,0:T(8,128)(2,1)S(1)} %get-tuple-element.32), channel_id=1, source_target_pairs={{0,24},{8,16},{16,8},{24,0},{1,25},{9,17},{17,9},{25,1},{2,26},{10... | collective-permute-start | bytes 1081352 | tf_op jit(solution)/shard_map/ppermute | solution.py:271
  214.4 17.9 %collective-permute-start.15 = (bf16[176,1024]{1,0:T(8,128)(2,1)S(1)}, bf16[176,1024]{1,0:T(8,128)(2,1)S(1)}, u32[]{:S(2)}, u32[]{:S(2)}) collective-permute-start(bf16[176,1024]{1,0:T(8,128)(2,1)S(1)} %get-tuple-element.33), channel_id=1, source_target_pairs={{0,16},{8,24},{16,0},{24,8},{1,17},{9,25},{17,1},{25,9},{2,18},{10... | collective-permute-start | bytes 1081352 | tf_op jit(solution)/shard_map/ppermute | solution.py:271
  214.8 17.6 %collective-permute-start.14 = (bf16[176,1024]{1,0:T(8,128)(2,1)S(1)}, bf16[176,1024]{1,0:T(8,128)(2,1)S(1)}, u32[]{:S(2)}, u32[]{:S(2)}) collective-permute-start(bf16[176,1024]{1,0:T(8,128)(2,1)S(1)} %get-tuple-element.31), channel_id=1, source_target_pairs={{0,8},{8,0},{16,24},{24,16},{1,9},{9,1},{17,25},{25,17},{2,10},{10... | collective-permute-start | bytes 1081352 | tf_op jit(solution)/shard_map/ppermute | solution.py:271
  232.7 16.6 %collective-permute-start.17 = (bf16[176,1024]{1,0:T(8,128)(2,1)S(1)}, bf16[176,1024]{1,0:T(8,128)(2,1)S(1)}, u32[]{:S(2)}, u32[]{:S(2)}) collective-permute-start(bf16[176,1024]{1,0:T(8,128)(2,1)S(1)} %fusion.3), channel_id=1, source_target_pairs={{0,0},{1,1},{8,2},{9,3},{16,4},{17,5},{24,6},{25,7},{2,12},{3,13},... | collective-permute-start | bytes 1081352 | tf_op jit(solution)/shard_map/ppermute | solution.py:346
  236.0 13.3 %collective-permute-start.12 = (bf16[80,1024]{1,0:T(8,128)(2,1)S(1)}, bf16[80,1024]{1,0:T(8,128)(2,1)S(1)}, u32[]{:S(2)}, u32[]{:S(2)}) collective-permute-start(bf16[80,1024]{1,0:T(8,128)(2,1)S(1)} %fusion.9), channel_id=1, source_target_pairs={{0,0},{1,1},{8,2},{9,3},{16,4},{17,5},{24,6},{25,7},{2,12},{3,13},... | collective-permute-start | bytes 491528 | tf_op jit(solution)/shard_map/ppermute | solution.py:346
Sparse Core Ops, SparseCore 0:
  35.8 34.2 reduce-scatter.2
  72.5 85.7 reduce-scatter.4
  165.2 38.0 all-gather.3
